TPU v7x, 32 devices: a whole 2x2x4 slice. The times are simulated.
32 devices in a mesh: tm: 16 (over z, y, x), space: 2 (over core).
Axes of the slice: x: 2, y: 2, z: 4, core: 2. Of those that a mesh axis runs over, the one named last changes fastest.
Arguments:
- queries: bfloat16 [16, 8, 64, 1536], P('tm', 'space'), may hold values from -16 to 16
- keys: bfloat16 [16, 8, 64, 1536], P('tm', 'space'), may hold values from -16 to 16
- values: bfloat16 [16, 8, 64, 1536], P('tm', 'space'), may hold values from -6 to 6
- key_lists: int32 [16, 4, 6, 2], P('tm', 'space'), may hold values from 0 to 1, each once within a row
- density: int32 [16, 3], P('tm'), may hold values from 1 to 2
Outputs:
- attended: bfloat16 [16, 8, 64, 1536], P('tm', 'space')
Inputs may be any that keep to these rules, and one draw needn't show every extreme that they name: `key_lists`: each list holds every block number of the partner band once.
All inputs are finite; a program needn't handle non-finite values.
Results may differ from a plain program's by a relative error of at most 0.0035.
Values may be sent and summed in bfloat16 or wider, within the bound.
No kernel may reach another device: no remote copies, remote signals or barrier semaphores. Data moves between devices by JAX's collectives and lax.ppermute only.
A program may use at most 64 MiB of HBM per device.

v0:
```python
import jax
import jax.numpy as jnp
from jax import lax
from jax.sharding import PartitionSpec as P

HEADS = 12
HEAD_DIM = 128
BROWS = 2
OFFSETS = 3


def extended(value, sides, width):
    for axis, dim in sides:
        size, length = (lax.axis_size(axis), value.shape[dim])
        up = [(i, (i + 1) % size) for i in range(size - 1)]
        down = [(j, i) for i, j in up]
        last = lax.slice_in_dim(value, length - width, length, axis=dim)
        leading = lax.slice_in_dim(value, 0, width, axis=dim)
        before = lax.ppermute(last, axis, up)
        after = lax.ppermute(leading, axis, down)
        value = jnp.concatenate([before, value, after], axis=dim)
    return value


def shifted(value, axis, steps):
    count = lax.axis_size(axis)
    leading, last = (max(0, -steps), min(count, count - steps))
    return lax.ppermute(value, axis, [(source, source + steps) for source in range(leading, last)])


def block_allowed(block_lists, live_counts):
    kb_count = block_lists.shape[2]
    positions = jnp.arange(kb_count, dtype=jnp.int32)
    live_cols = positions[None, :] < jnp.repeat(live_counts, 2)[:, None]
    matches = (block_lists[:, :, :, None] == positions[None, None, None, :]) & live_cols[
        None, :, :, None
    ]
    return jnp.any(matches, axis=2)


def expand_blocks(allowed, block_tokens):
    q_count, slot_count, k_count = allowed.shape
    widened = jnp.broadcast_to(
        allowed[:, None, :, :, None], (q_count, block_tokens, slot_count, k_count, block_tokens)
    )
    return widened.reshape(q_count * block_tokens, slot_count, k_count * block_tokens)


def attend(query_rows, key_rows, value_rows, mask):
    scale = 1.0 / float(HEAD_DIM) ** 0.5

    def one_head(head):
        query_head = lax.dynamic_slice_in_dim(query_rows, head * HEAD_DIM, HEAD_DIM, 1)
        key_head = lax.dynamic_slice_in_dim(key_rows, head * HEAD_DIM, HEAD_DIM, 1)
        value_head = lax.dynamic_slice_in_dim(value_rows, head * HEAD_DIM, HEAD_DIM, 1)
        scores = (
            lax.dot_general(
                query_head, key_head, (((1,), (1,)), ((), ())), preferred_element_type=jnp.float32
            )
            * scale
        )
        masked = jnp.where(mask, scores, -1e30)
        row_top = jnp.max(masked, axis=1, keepdims=True)
        weights = jnp.where(mask, jnp.exp(masked - row_top), 0.0)
        total = jnp.sum(weights, axis=1, keepdims=True)
        mixed = (
            jnp.dot(weights.astype(jnp.bfloat16), value_head, preferred_element_type=jnp.float32)
            / total
        )
        return mixed.astype(jnp.bfloat16)

    per_head = lax.map(one_head, jnp.arange(HEADS, dtype=jnp.int32))
    return jnp.transpose(per_head, (1, 0, 2)).reshape(query_rows.shape[0], HEADS * HEAD_DIM)


def body(queries, keys, values, key_lists, density):
    rows_dev = queries.shape[1]
    width = queries.shape[2]
    features = queries.shape[3]
    tok_rows = rows_dev * width
    block_tokens = BROWS * width
    stacked = jnp.concatenate([keys, values], axis=0)
    padded = extended(stacked, (("space", 1),), BROWS)
    near_pair = padded.reshape(2, -1, features)
    band_index = lax.axis_index("space")
    band_count = lax.axis_size("space")
    row_ids = jnp.arange(rows_dev + 2 * BROWS, dtype=jnp.int32)
    row_ok = ((row_ids >= BROWS) | (band_index > 0)) & (
        (row_ids < rows_dev + BROWS) | (band_index < band_count - 1)
    )
    near_ok = jnp.repeat(row_ok, width)
    frame_index = lax.axis_index("tm")
    frame_count = lax.axis_size("tm")
    partners = []
    slot_ok = []
    for degree in range(OFFSETS):
        for direction in (1, -1):
            partners.append(shifted(stacked, "tm", direction * 2**degree))
    for degree in range(OFFSETS):
        slot_ok.append(frame_index - 2**degree >= 0)
        slot_ok.append(frame_index + 2**degree < frame_count)
    key_rows = jnp.concatenate(
        [near_pair[0]] + [member[0].reshape(tok_rows, features) for member in partners], axis=0
    )
    value_rows = jnp.concatenate(
        [near_pair[1]] + [member[1].reshape(tok_rows, features) for member in partners], axis=0
    )
    allowed = expand_blocks(block_allowed(key_lists[0], density[0]), block_tokens)
    allowed = allowed & jnp.stack(slot_ok)[None, :, None]
    mask = jnp.concatenate(
        [
            jnp.broadcast_to(near_ok[None, :], (tok_rows, near_ok.shape[0])),
            allowed.reshape(tok_rows, -1),
        ],
        axis=1,
    )
    result = attend(queries.reshape(tok_rows, features), key_rows, value_rows, mask)
    return result.reshape(1, rows_dev, width, features)


def solution(mesh):
    in_specs = (
        P("tm", "space", None, None),
        P("tm", "space", None, None),
        P("tm", "space", None, None),
        P("tm", "space", None, None),
        P("tm", None),
    )
    out_specs = P("tm", "space", None, None)
    return jax.shard_map(body, mesh=mesh, in_specs=in_specs, out_specs=out_specs, check_vma=False)
```

profile of v0, /device:TPU:30, one launch (start us, length us, event | category | flops | bytes accessed | tf_op | source)
XLA Modules:
  0.0 212.6 jit_solution(14077513090796387950)
XLA Ops:
  3.7 5.7 %collective-permute-start.3 = (bf16[2,4,64,1536]{3,2,1,0:T(8,128)(2,1)S(1)}, bf16[2,4,64,1536]{3,2,1,0:T(8,128)(2,1)}, u32[]{:S(2)}, u32[]{:S(2)}) collective-permute-start(bf16[2,4,64,1536]{3,2,1,0:T(8,128)(2,1)S(1)} %constant_dynamic-update-slice_fusion), channel_id=1, source_target_pairs={{2,0},{4,2},{6,4},{8,6},{10,8},{12,10},{14,12},{16,14},{18,16},{20... | collective-permute-start | bytes 4718600 | tf_op jit(solution)/shard_map/ppermute | solution.py:28
  12.0 2.2 %collective-permute-start = (bf16[2,2,64,1536]{3,2,1,0:T(8,128)(2,1)}, bf16[2,2,64,1536]{3,2,1,0:T(8,128)(2,1)}, u32[]{:S(2)}, u32[]{:S(2)}) collective-permute-start(bf16[2,2,64,1536]{3,2,1,0:T(8,128)(2,1)} %get-tuple-element.73), channel_id=1, source_target_pairs={{0,1},{2,3},{4,5},{6,7},{8,9},{10,11},{12,13},{14,15},{16,17},{18,... | collective-permute-start | bytes 2359304 | tf_op jit(solution)/shard_map/ppermute | solution.py:19
  18.5 4.6 %collective-permute-start.5 = (bf16[2,4,64,1536]{3,2,1,0:T(8,128)(2,1)S(1)}, bf16[2,4,64,1536]{3,2,1,0:T(8,128)(2,1)S(1)}, u32[]{:S(2)}, u32[]{:S(2)}) collective-permute-start(bf16[2,4,64,1536]{3,2,1,0:T(8,128)(2,1)S(1)} %constant_dynamic-update-slice_fusion), channel_id=1, source_target_pairs={{4,0},{6,2},{8,4},{10,6},{12,8},{14,10},{16,12},{18,14},{20,16},{2... | collective-permute-start | bytes 4718600 | tf_op jit(solution)/shard_map/ppermute | solution.py:28
  26.6 15.1 %collective-permute-done.2 = bf16[2,4,64,1536]{3,2,1,0:T(8,128)(2,1)} collective-permute-done((bf16[2,4,64,1536]{3,2,1,0:T(8,128)(2,1)S(1)}, bf16[2,4,64,1536]{3,2,1,0:T(8,128)(2,1)}, u32[]{:S(2)}, u32[]{:S(2)}) %collective-permute-start.2) | collective-permute-done | bytes 1572896 | tf_op jit(solution)/shard_map/ppermute | solution.py:28
  41.7 21.4 %collective-permute-start.7 = (bf16[2,4,64,1536]{3,2,1,0:T(8,128)(2,1)S(1)}, bf16[2,4,64,1536]{3,2,1,0:T(8,128)(2,1)S(1)}, u32[]{:S(2)}, u32[]{:S(2)}) collective-permute-start(bf16[2,4,64,1536]{3,2,1,0:T(8,128)(2,1)S(1)} %constant_dynamic-update-slice_fusion), channel_id=1, source_target_pairs={{8,0},{10,2},{12,4},{14,6},{16,8},{18,10},{20,12},{22,14},{24,16},... | collective-permute-start | bytes 4718600 | tf_op jit(solution)/shard_map/ppermute | solution.py:28
  64.5 8.5 %collective-permute-done.3 = bf16[2,4,64,1536]{3,2,1,0:T(8,128)(2,1)} collective-permute-done((bf16[2,4,64,1536]{3,2,1,0:T(8,128)(2,1)S(1)}, bf16[2,4,64,1536]{3,2,1,0:T(8,128)(2,1)}, u32[]{:S(2)}, u32[]{:S(2)}) %collective-permute-start.3) | collective-permute-done | bytes 1572896 | tf_op jit(solution)/shard_map/ppermute | solution.py:28
  76.2 48.0 %collective-permute-done.5 = bf16[2,4,64,1536]{3,2,1,0:T(8,128)(2,1)S(1)} collective-permute-done((bf16[2,4,64,1536]{3,2,1,0:T(8,128)(2,1)S(1)}, bf16[2,4,64,1536]{3,2,1,0:T(8,128)(2,1)S(1)}, u32[]{:S(2)}, u32[]{:S(2)}) %collective-permute-start.5) | collective-permute-done | bytes 1572896 | tf_op jit(solution)/shard_map/ppermute | solution.py:28
  124.3 17.3 %collective-permute-done.6 = bf16[2,4,64,1536]{3,2,1,0:T(8,128)(2,1)S(1)} collective-permute-done((bf16[2,4,64,1536]{3,2,1,0:T(8,128)(2,1)S(1)}, bf16[2,4,64,1536]{3,2,1,0:T(8,128)(2,1)S(1)}, u32[]{:S(2)}, u32[]{:S(2)}) %collective-permute-start.6) | collective-permute-done | bytes 1572896 | tf_op jit(solution)/shard_map/ppermute | solution.py:28
  142.4 2.6 %copy-done = bf16[2048,1536]{1,0:T(8,128)(2,1)} copy-done((bf16[2048,1536]{1,0:T(8,128)(2,1)}, bf16[2048,1536]{1,0:T(8,128)(2,1)S(1)}, u32[]{:S(2)}) %copy-start) | copy-done | bytes 6291480
  145.0 1.9 copy-done.1
  146.9 63.7 %while.10 = (s32[]{:T(128)}, bf16[12,256,128]{2,1,0:T(8,128)(2,1)S(1)}, s32[12]{0:T(128)S(1)}, bf16[256,1536]{1,0:T(8,128)(2,1)}, bf16[2048,1536]{1,0:T(8,128)(2...) while((s32[]{:T(128)}, ...), condition=%wide.region_4.5_spmd, body=%wide.region_1.4_spmd.sunk | while | flops 273219072 | bytes 9050795 | solution.py:72
  148.1 1.7 fusion.31
  150.5 1.7 fusion.33
  153.5 1.7 fusion.31
  155.8 1.7 fusion.33
  158.8 1.7 fusion.31
  161.1 1.7 fusion.33
  164.1 1.7 fusion.31
  166.4 1.7 fusion.33
  171.7 1.7 fusion.33
  174.7 1.7 fusion.31
  177.0 1.7 fusion.33
  180.0 1.7 fusion.31
  182.3 1.7 fusion.33
  185.3 1.7 fusion.31
  187.6 1.7 fusion.33
  193.0 1.7 fusion.33
  195.9 1.7 fusion.31
  198.3 1.7 fusion.33
  203.6 1.7 fusion.33
  206.6 1.7 fusion.31
  208.9 1.7 fusion.33
  (85 shorter events, 41.0 us)
Async XLA Ops:
  0.0 15.7 %copy-start.3 = (s32[1,3]{1,0:T(1,128)S(1)}, s32[1,3]{1,0:T(1,128)}, u32[]{:S(2)}) copy-start(s32[1,3]{1,0:T(1,128)} %param.11) | copy-start | bytes 40
  0.0 15.8 %copy-start.2 = (s32[1,2,6,2]{2,3,1,0:T(2,128)S(1)}, s32[1,2,6,2]{2,3,1,0:T(2,128)}, u32[]{:S(2)}) copy-start(s32[1,2,6,2]{2,3,1,0:T(2,128)} %param.10) | copy-start | bytes 292
  2.4 39.3 %collective-permute-start.2 = (bf16[2,4,64,1536]{3,2,1,0:T(8,128)(2,1)S(1)}, bf16[2,4,64,1536]{3,2,1,0:T(8,128)(2,1)}, u32[]{:S(2)}, u32[]{:S(2)}) collective-permute-start(bf16[2,4,64,1536]{3,2,1,0:T(8,128)(2,1)S(1)} %constant_dynamic-update-slice_fusion), channel_id=1, source_target_pairs={{0,2},{2,4},{4,6},{6,8},{8,10},{10,12},{12,14},{14,16},{16,18},{18... | collective-permute-start | bytes 4718600 | tf_op jit(solution)/shard_map/ppermute | solution.py:28
  3.7 69.3 %collective-permute-start.3 = (bf16[2,4,64,1536]{3,2,1,0:T(8,128)(2,1)S(1)}, bf16[2,4,64,1536]{3,2,1,0:T(8,128)(2,1)}, u32[]{:S(2)}, u32[]{:S(2)}) collective-permute-start(bf16[2,4,64,1536]{3,2,1,0:T(8,128)(2,1)S(1)} %constant_dynamic-update-slice_fusion), channel_id=1, source_target_pairs={{2,0},{4,2},{6,4},{8,6},{10,8},{12,10},{14,12},{16,14},{18,16},{20... | collective-permute-start | bytes 4718600 | tf_op jit(solution)/shard_map/ppermute | solution.py:28
  9.4 65.2 %collective-permute-start.4 = (bf16[2,4,64,1536]{3,2,1,0:T(8,128)(2,1)S(1)}, bf16[2,4,64,1536]{3,2,1,0:T(8,128)(2,1)}, u32[]{:S(2)}, u32[]{:S(2)}) collective-permute-start(bf16[2,4,64,1536]{3,2,1,0:T(8,128)(2,1)S(1)} %constant_dynamic-update-slice_fusion), channel_id=1, source_target_pairs={{0,4},{2,6},{4,8},{6,10},{8,12},{10,14},{12,16},{14,18},{16,20},{1... | collective-permute-start | bytes 4718600 | tf_op jit(solution)/shard_map/ppermute | solution.py:28
  12.0 6.6 %collective-permute-start = (bf16[2,2,64,1536]{3,2,1,0:T(8,128)(2,1)}, bf16[2,2,64,1536]{3,2,1,0:T(8,128)(2,1)}, u32[]{:S(2)}, u32[]{:S(2)}) collective-permute-start(bf16[2,2,64,1536]{3,2,1,0:T(8,128)(2,1)} %get-tuple-element.73), channel_id=1, source_target_pairs={{0,1},{2,3},{4,5},{6,7},{8,9},{10,11},{12,13},{14,15},{16,17},{18,... | collective-permute-start | bytes 2359304 | tf_op jit(solution)/shard_map/ppermute | solution.py:19
  14.2 9.0 %collective-permute-start.1 = (bf16[2,2,64,1536]{3,2,1,0:T(8,128)(2,1)}, bf16[2,2,64,1536]{3,2,1,0:T(8,128)(2,1)}, u32[]{:S(2)}, u32[]{:S(2)}) collective-permute-start(bf16[2,2,64,1536]{3,2,1,0:T(8,128)(2,1)} %get-tuple-element.74), channel_id=1, source_target_pairs={{1,0},{3,2},{5,4},{7,6},{9,8},{11,10},{13,12},{15,14},{17,16},{19,... | collective-permute-start | bytes 2359304 | tf_op jit(solution)/shard_map/ppermute | solution.py:20
  18.5 105.7 %collective-permute-start.5 = (bf16[2,4,64,1536]{3,2,1,0:T(8,128)(2,1)S(1)}, bf16[2,4,64,1536]{3,2,1,0:T(8,128)(2,1)S(1)}, u32[]{:S(2)}, u32[]{:S(2)}) collective-permute-start(bf16[2,4,64,1536]{3,2,1,0:T(8,128)(2,1)S(1)} %constant_dynamic-update-slice_fusion), channel_id=1, source_target_pairs={{4,0},{6,2},{8,4},{10,6},{12,8},{14,10},{16,12},{18,14},{20,16},{2... | collective-permute-start | bytes 4718600 | tf_op jit(solution)/shard_map/ppermute | solution.py:28
  23.2 118.4 %collective-permute-start.6 = (bf16[2,4,64,1536]{3,2,1,0:T(8,128)(2,1)S(1)}, bf16[2,4,64,1536]{3,2,1,0:T(8,128)(2,1)S(1)}, u32[]{:S(2)}, u32[]{:S(2)}) collective-permute-start(bf16[2,4,64,1536]{3,2,1,0:T(8,128)(2,1)S(1)} %constant_dynamic-update-slice_fusion), channel_id=1, source_target_pairs={{0,8},{2,10},{4,12},{6,14},{8,16},{10,18},{12,20},{14,22},{16,24},... | collective-permute-start | bytes 4718600 | tf_op jit(solution)/shard_map/ppermute | solution.py:28
  41.7 100.5 %collective-permute-start.7 = (bf16[2,4,64,1536]{3,2,1,0:T(8,128)(2,1)S(1)}, bf16[2,4,64,1536]{3,2,1,0:T(8,128)(2,1)S(1)}, u32[]{:S(2)}, u32[]{:S(2)}) collective-permute-start(bf16[2,4,64,1536]{3,2,1,0:T(8,128)(2,1)S(1)} %constant_dynamic-update-slice_fusion), channel_id=1, source_target_pairs={{8,0},{10,2},{12,4},{14,6},{16,8},{18,10},{20,12},{22,14},{24,16},... | collective-permute-start | bytes 4718600 | tf_op jit(solution)/shard_map/ppermute | solution.py:28
  142.4 2.6 %copy-start = (bf16[2048,1536]{1,0:T(8,128)(2,1)}, bf16[2048,1536]{1,0:T(8,128)(2,1)S(1)}, u32[]{:S(2)}) copy-start(bf16[2048,1536]{1,0:T(8,128)(2,1)S(1)} %get-tuple-element.128) | copy-start | bytes 18874372
  142.4 4.5 %copy-start.1 = (bf16[2048,1536]{1,0:T(8,128)(2,1)}, bf16[2048,1536]{1,0:T(8,128)(2,1)S(1)}, u32[]{:S(2)}) copy-start(bf16[2048,1536]{1,0:T(8,128)(2,1)S(1)} %get-tuple-element.130) | copy-start | bytes 18874372
where the time goes:
time: 214 us; the launch traced here: 213 us
  waiting for transfers between devices  88.9 us (42%)
  matrix products  40.8 us (19%)
  starting transfers between devices  39.1 us (18%)
  local copies, waits for them, and re-layouts  25.5 us (12%)
  other arithmetic  9.78 us (5%)
  loops' own time  8.1 us (4%)
    ppermute x6, waiting for transfers between devices, shifted(): lax.ppermute(value, axis, [(source, source + steps) for source in range(l...  88.9 us
    ppermute x6, starting transfers between devices, shifted(): lax.ppermute(value, axis, [(source, source + steps) for source in range(l...  35.6 us
    dot_general x12, matrix products, one_head(): jnp.dot(weights.astype(jnp.bfloat16), value_head, preferred_element_type=...  20.7 us
    dot_general x12, matrix products, one_head(): lax.dot_general(query_head, key_head, (((1,), (1,)), ((), ())), preferred...  20.2 us
    another operation x1, loops' own time, attend(): per_head = lax.map(one_head, jnp.arange(HEADS, dtype=jnp.int32))  8.1 us
    reduce_sum x12, other arithmetic, one_head(): total = jnp.sum(weights, axis=1, keepdims=True)  7.74 us
    dynamic_slice x12, local copies, waits for them, and re-layouts, attend(): per_head = lax.map(one_head, jnp.arange(HEADS, dtype=jnp.int32))  7.03 us
    unnamed x21, local copies, waits for them, and re-layouts  6.46 us
  transfers between devices with their start and end apart: 8, of which 4 were waited for; matrix products, arithmetic and copies ran while one was open for 5% of the time, Pallas kernels for 0%

commit v1 on v0

v1 whole, which is shorter than its diff:
```python
import math

import jax
import jax.numpy as jnp
from jax import lax
from jax.experimental import pallas as pl
from jax.experimental.pallas import tpu as pltpu
from jax.sharding import PartitionSpec as P


HEADS = 12
HEAD_DIM = 128
BROWS = 2
OFFSETS = 3
GROUP = 2 ** (OFFSETS - 1)
HEADS_STEP = 3
NEG = -1e30
SCALE2 = math.log2(math.e) / math.sqrt(HEAD_DIM)


def routes(count):
    def pairs(target):
        out = []
        for t in range(count):
            to = target(t, t % GROUP)
            if to is not None and 0 <= to < count:
                out.append((t, to))
        return out

    up = GROUP // 2
    return {
        "x": pairs(lambda t, p: t ^ 1),
        "y": pairs(lambda t, p: t ^ 2),
        "o": pairs(lambda t, p: t - GROUP if p < up else t + GROUP),
        "b": pairs(lambda t, p: t + GROUP if p < up else t - GROUP),
        "g": pairs(lambda t, p: t ^ 1 if p in (0, GROUP - 1) else None),
        "e": pairs(lambda t, p: t ^ 1 if p not in (0, GROUP - 1) else None),
    }


def slot_of(name, p):
    low = (p < GROUP // 2).astype(jnp.int32)
    even = 1 - p % 2
    return {
        "X": even,
        "Y": 2 + low,
        "O": 4 + low,
        "B": 5 - low,
        "W": 3 - low,
        "GE": 1 - even,
    }[name]


def dot_nt(a, b):
    return lax.dot_general(a, b, (((1,), (1,)), ((), ())), preferred_element_type=jnp.float32)


def flash(q, blocks, state, halves):
    rows = q.shape[0] // halves
    scores = [dot_nt(q, k) for k, _, _ in blocks]
    tops = []
    for half in range(halves):
        top = None
        for s, (_, _, allow) in zip(scores, blocks):
            part = s[half * rows : (half + 1) * rows]
            width = part.shape[1] // len(allow[half])
            for kb, ok in enumerate(allow[half]):
                piece = part[:, kb * width : (kb + 1) * width]
                if ok is not None:
                    piece = jnp.where(ok, piece, NEG)
                for lane in range(0, width, 128):
                    lanes = piece[:, lane : lane + 128]
                    top = lanes if top is None else jnp.maximum(top, lanes)
        tops.append(jnp.max(top, axis=1, keepdims=True))
    top = jnp.concatenate(tops, axis=0)
    if state is not None:
        old_top, old_total, old_acc = state
        top = jnp.maximum(top, old_top)
    shift = top * SCALE2
    lane_sum = None
    acc = None
    for s, (_, v, allow) in zip(scores, blocks):
        rows_out = []
        for half in range(halves):
            part = s[half * rows : (half + 1) * rows]
            own = shift[half * rows : (half + 1) * rows]
            width = part.shape[1] // len(allow[half])
            cols = []
            for kb, ok in enumerate(allow[half]):
                off = own if ok is None else jnp.where(ok, own, -NEG)
                cols.append(jnp.exp2(part[:, kb * width : (kb + 1) * width] * SCALE2 - off))
            rows_out.append(cols[0] if len(cols) == 1 else jnp.concatenate(cols, axis=1))
        w = jnp.concatenate(rows_out, axis=0)
        for lane in range(0, w.shape[1], 128):
            lanes = w[:, lane : lane + 128]
            lane_sum = lanes if lane_sum is None else lane_sum + lanes
        mixed = jnp.dot(w.astype(jnp.bfloat16), v, preferred_element_type=jnp.float32)
        acc = mixed if acc is None else acc + mixed
    total = jnp.sum(lane_sum, axis=1, keepdims=True)
    if state is not None:
        decay = jnp.exp2((old_top - top) * SCALE2)
        total = total + old_total * decay
        acc = acc + old_acc * decay
    return top, total, acc


def stage_call(q, entries, state, lists, density, final):
    tokens, features = q.shape
    width = HEADS_STEP * HEAD_DIM
    steps = features // width
    kinds = [kind for kind, _, _ in entries]
    halves = lists.shape[1]
    positions = lists.shape[3]
    frames = lax.axis_size("tm")
    bands = lax.axis_size("space")
    n_in = 2 * len(entries)

    def kernel(lists_ref, density_ref, *refs):
        q_ref = refs[0]
        kv = refs[1 : 1 + n_in]
        rest = refs[1 + n_in :]
        if state is not None:
            stat_in, acc_in = rest[:2]
            rest = rest[2:]
        t = lax.axis_index("tm")
        band = lax.axis_index("space")
        p = t % GROUP

        def allow_of(kind):
            if kind == "own":
                return [[None]] * halves
            if kind == "before":
                return [[band > 0]] * halves
            if kind == "after":
                return [[band < bands - 1]] * halves
            slot = slot_of(kind, p)
            step = jnp.left_shift(1, slot // 2)
            there = t + jnp.where(slot % 2 == 0, -step, step)
            ok = (there >= 0) & (there < frames)
            live = density_ref[0, slot // 2]
            out = []
            for half in range(halves):
                row = []
                for kb in range(positions):
                    hit = (lists_ref[0, half, slot, 0] == kb) & (live > 0)
                    for i in range(1, positions):
                        hit = hit | ((lists_ref[0, half, slot, i] == kb) & (live > i))
                    row.append(ok & hit)
                out.append(row)
            return out

        allows = [allow_of(kind) for kind in kinds if kind != "E"]
        wrap = (p == 0) | (p == GROUP - 1)
        for h in range(HEADS_STEP):
            cols = slice(h * HEAD_DIM, (h + 1) * HEAD_DIM)
            blocks = []
            for i, kind in enumerate(kinds):
                if kind == "E":
                    continue
                k, v = kv[2 * i][:, cols], kv[2 * i + 1][:, cols]
                if kind == "GE":
                    j = kinds.index("E")
                    k = jnp.where(wrap, kv[2 * j][:, cols], k)
                    v = jnp.where(wrap, kv[2 * j + 1][:, cols], v)
                blocks.append((k, v, allows[len(blocks)]))
            old = None
            if state is not None:
                stat = stat_in[:, cols]
                old = (stat[:, 0:1], stat[:, HEAD_DIM // 2 : HEAD_DIM // 2 + 1], acc_in[:, cols])
            top, total, acc = flash(q_ref[:, cols], blocks, old, halves)
            if final:
                rest[0][:, cols] = (acc / total).astype(jnp.bfloat16)
            else:
                lane = lax.broadcasted_iota(jnp.int32, (tokens, HEAD_DIM), 1)
                rest[0][:, cols] = jnp.where(lane < HEAD_DIM // 2, top, total)
                rest[1][:, cols] = acc

    def spec(rows):
        return pl.BlockSpec((rows, width), lambda i: (0, i))

    smem = pl.BlockSpec(memory_space=pltpu.SMEM)
    operands = [lists, density, q]
    specs = [smem, smem, spec(tokens)]
    keys = 0
    for kind, k, v in entries:
        operands += [k, v]
        specs += [spec(k.shape[0]), spec(v.shape[0])]
        keys += k.shape[0] if kind != "E" else 0
    if state is not None:
        operands += list(state)
        specs += [spec(tokens), spec(tokens)]
    full = jax.ShapeDtypeStruct((tokens, features), jnp.float32)
    if final:
        outs, out_specs = jax.ShapeDtypeStruct((tokens, features), jnp.bfloat16), spec(tokens)
    else:
        outs, out_specs = (full, full), (spec(tokens), spec(tokens))
    return pl.pallas_call(
        kernel,
        grid=(steps,),
        in_specs=specs,
        out_specs=out_specs,
        out_shape=outs,
        cost_estimate=pl.CostEstimate(
            flops=4 * tokens * keys * features,
            transcendentals=tokens * keys * HEADS,
            bytes_accessed=2 * features * (2 * keys + 4 * tokens),
        ),
    )(*operands)


def body(queries, keys, values, key_lists, density):
    _, rows_dev, width, features = queries.shape
    frames = lax.axis_size("tm")
    bands = lax.axis_size("space")
    route = routes(frames)
    up = [(i, i + 1) for i in range(bands - 1)]
    down = [(j, i) for i, j in up]

    def send(value, pairs, axis="tm"):
        return lax.ppermute(value, axis, pairs)

    def flat(value):
        return value.reshape(-1, features)

    edge = BROWS
    y_k = send(keys, route["y"])
    x_k = send(keys, route["x"])
    o_k = send(keys, route["o"])
    b_k = send(keys, route["b"])
    last = jnp.concatenate([keys[:, rows_dev - edge :], values[:, rows_dev - edge :]], axis=0)
    first = jnp.concatenate([keys[:, :edge], values[:, :edge]], axis=0)
    before = send(last, up, "space")
    after = send(first, down, "space")
    y_v = send(values, route["y"])
    x_v = send(values, route["x"])
    o_v = send(values, route["o"])
    w_k = send(y_k, route["b"])
    g_k = send(y_k, route["g"])
    w_v = send(y_v, route["b"])
    e_k = send(w_k, route["e"])
    g_v = send(y_v, route["g"])
    b_v = send(values, route["b"])
    e_v = send(w_v, route["e"])

    q = flat(queries)
    state = stage_call(
        q,
        [
            ("own", flat(keys), flat(values)),
            ("before", flat(before[0]), flat(before[1])),
            ("after", flat(after[0]), flat(after[1])),
        ],
        None,
        key_lists,
        density,
        False,
    )
    state = stage_call(
        q,
        [("X", flat(x_k), flat(x_v)), ("Y", flat(y_k), flat(y_v)), ("O", flat(o_k), flat(o_v))],
        state,
        key_lists,
        density,
        False,
    )
    state = stage_call(q, [("W", flat(w_k), flat(w_v))], state, key_lists, density, False)
    result = stage_call(
        q,
        [("B", flat(b_k), flat(b_v)), ("GE", flat(g_k), flat(g_v)), ("E", flat(e_k), flat(e_v))],
        state,
        key_lists,
        density,
        True,
    )
    return result.reshape(1, rows_dev, width, features)


def solution(mesh):
    in_specs = (
        P("tm", "space", None, None),
        P("tm", "space", None, None),
        P("tm", "space", None, None),
        P("tm", "space", None, None),
        P("tm", None),
    )
    out_specs = P("tm", "space", None, None)
    return jax.shard_map(body, mesh=mesh, in_specs=in_specs, out_specs=out_specs, check_vma=False)
```

time: 214 us -> 149 us (0.70)
  the two profiles are of different devices: /device:TPU:30 before, /device:TPU:20 now
where the time goes in v1:
time: 149 us; the launch traced here: 148 us
  waiting for transfers between devices  65.5 us (44%)
  Pallas kernels  41.9 us (28%)
  starting transfers between devices  33.5 us (22%)
  local copies, waits for them, and re-layouts  6.88 us (5%)
    ppermute x16, waiting for transfers between devices, send(): return lax.ppermute(value, axis, pairs)  65.5 us
    pallas_call x4, Pallas kernels, stage_call(): pl.pallas_call(kernel, grid=(steps,), in_specs=specs, out_specs=out_specs...  41.9 us
    ppermute x16, starting transfers between devices, send(): return lax.ppermute(value, axis, pairs)  33.5 us
  transfers between devices with their start and end apart: 16, of which 5 were waited for; matrix products, arithmetic and copies ran while one was open for 3% of the time, Pallas kernels for 22%

profile of v1, /device:TPU:20, one launch (start us, length us, event | category | flops | bytes accessed | tf_op | source)
XLA Modules:
  0.0 148.2 jit_solution(1934831407364386158)
XLA Ops:
  0.0 1.2 fusion.1
  1.2 0.1 copy-done.1
  1.5 1.9 %collective-permute-start.14 = (bf16[2,2,64,1536]{3,2,1,0:T(8,128)(2,1)S(1)}, bf16[2,2,64,1536]{3,2,1,0:T(8,128)(2,1)S(1)}, u32[]{:S(2)}, u32[]{:S(2)}) collective-permute-start(bf16[2,2,64,1536]{3,2,1,0:T(8,128)(2,1)S(1)} %pad_maximum_fusion), channel_id=1, source_target_pairs={{0,1},{2,3},{4,5},{6,7},{8,9},{10,11},{12,13},{14,15},{16,17},{18,... | collective-permute-start | bytes 2359304 | tf_op jit(solution)/shard_map/ppermute | solution.py:220
  3.6 1.3 collective-permute-start.15
  4.9 0.6 collective-permute-start.2
  5.4 1.5 %collective-permute-start.4 = (bf16[1,4,64,1536]{3,2,1,0:T(8,128)(2,1)S(1)}, bf16[1,4,64,1536]{3,2,1,0:T(8,128)(2,1)S(1)}, u32[]{:S(2)}, u32[]{:S(2)}) collective-permute-start(bf16[1,4,64,1536]{3,2,1,0:T(8,128)(2,1)S(1)} %copy-done.1), channel_id=1, source_target_pairs={{0,4},{2,6},{4,0},{6,2},{8,12},{10,14},{12,8},{14,10},{16,20},{18,... | collective-permute-start | bytes 2359304 | tf_op jit(solution)/shard_map/ppermute | solution.py:220
  7.0 1.5 %collective-permute-start.11 = (bf16[1,4,64,1536]{3,2,1,0:T(8,128)(2,1)S(1)}, bf16[1,4,64,1536]{3,2,1,0:T(8,128)(2,1)S(1)}, u32[]{:S(2)}, u32[]{:S(2)}) collective-permute-start(bf16[1,4,64,1536]{3,2,1,0:T(8,128)(2,1)S(1)} %copy-done.1), channel_id=1, source_target_pairs={{0,2},{2,0},{4,6},{6,4},{8,10},{10,8},{12,14},{14,12},{16,18},{18,... | collective-permute-start | bytes 2359304 | tf_op jit(solution)/shard_map/ppermute | solution.py:220
  8.4 3.5 %collective-permute-start.12 = (bf16[1,4,64,1536]{3,2,1,0:T(8,128)(2,1)S(1)}, bf16[1,4,64,1536]{3,2,1,0:T(8,128)(2,1)S(1)}, u32[]{:S(2)}, u32[]{:S(2)}) collective-permute-start(bf16[1,4,64,1536]{3,2,1,0:T(8,128)(2,1)S(1)} %copy-done), channel_id=1, source_target_pairs={{4,12},{6,14},{8,0},{10,2},{12,20},{14,22},{16,8},{18,10},{20,28},... | collective-permute-start | bytes 2359304 | tf_op jit(solution)/shard_map/ppermute | solution.py:220
  12.0 1.9 %collective-permute-start.13 = (bf16[1,4,64,1536]{3,2,1,0:T(8,128)(2,1)S(1)}, bf16[1,4,64,1536]{3,2,1,0:T(8,128)(2,1)}, u32[]{:S(2)}, u32[]{:S(2)}) collective-permute-start(bf16[1,4,64,1536]{3,2,1,0:T(8,128)(2,1)S(1)} %copy-done.1), channel_id=1, source_target_pairs={{4,12},{6,14},{8,0},{10,2},{12,20},{14,22},{16,8},{18,10},{20,28},... | collective-permute-start | bytes 2359304 | tf_op jit(solution)/shard_map/ppermute | solution.py:220
  13.9 11.3 %collective-permute-done.2 = bf16[1,4,64,1536]{3,2,1,0:T(8,128)(2,1)S(1)} collective-permute-done((bf16[1,4,64,1536]{3,2,1,0:T(8,128)(2,1)S(1)}, bf16[1,4,64,1536]{3,2,1,0:T(8,128)(2,1)S(1)}, u32[]{:S(2)}, u32[]{:S(2)}) %collective-permute-start.2) | collective-permute-done | bytes 786464 | tf_op jit(solution)/shard_map/ppermute | solution.py:220
  25.1 1.5 %collective-permute-start.10 = (bf16[1,4,64,1536]{3,2,1,0:T(8,128)(2,1)S(1)}, bf16[1,4,64,1536]{3,2,1,0:T(8,128)(2,1)}, u32[]{:S(2)}, u32[]{:S(2)}) collective-permute-start(bf16[1,4,64,1536]{3,2,1,0:T(8,128)(2,1)S(1)} %copy-done), channel_id=1, source_target_pairs={{0,2},{2,0},{4,6},{6,4},{8,10},{10,8},{12,14},{14,12},{16,18},{18,... | collective-permute-start | bytes 2359304 | tf_op jit(solution)/shard_map/ppermute | solution.py:220
  26.6 15.4 %collective-permute-done.4 = bf16[1,4,64,1536]{3,2,1,0:T(8,128)(2,1)S(1)} collective-permute-done((bf16[1,4,64,1536]{3,2,1,0:T(8,128)(2,1)S(1)}, bf16[1,4,64,1536]{3,2,1,0:T(8,128)(2,1)S(1)}, u32[]{:S(2)}, u32[]{:S(2)}) %collective-permute-start.4) | collective-permute-done | bytes 786464 | tf_op jit(solution)/shard_map/ppermute | solution.py:220
  42.0 2.3 %collective-permute-start = (bf16[1,4,64,1536]{3,2,1,0:T(8,128)(2,1)S(1)}, bf16[1,4,64,1536]{3,2,1,0:T(8,128)(2,1)}, u32[]{:S(2)}, u32[]{:S(2)}) collective-permute-start(bf16[1,4,64,1536]{3,2,1,0:T(8,128)(2,1)S(1)} %copy-done), channel_id=1, source_target_pairs={{0,8},{2,10},{8,16},{10,18},{12,4},{14,6},{16,24},{18,26},{20,12},... | collective-permute-start | bytes 2359304 | tf_op jit(solution)/shard_map/ppermute | solution.py:220
  44.4 2.4 %collective-permute-start.6 = (bf16[1,4,64,1536]{3,2,1,0:T(8,128)(2,1)S(1)}, bf16[1,4,64,1536]{3,2,1,0:T(8,128)(2,1)}, u32[]{:S(2)}, u32[]{:S(2)}) collective-permute-start(bf16[1,4,64,1536]{3,2,1,0:T(8,128)(2,1)S(1)} %collective-permute-done.2), channel_id=1, source_target_pairs={{0,8},{2,10},{8,16},{10,18},{12,4},{14,6},{16,24},{18,26},{20,12},... | collective-permute-start | bytes 2359304 | tf_op jit(solution)/shard_map/ppermute | solution.py:220
  46.8 0.9 copy-done.5
  47.7 1.9 %collective-permute-start.8 = (bf16[1,4,64,1536]{3,2,1,0:T(8,128)(2,1)S(1)}, bf16[1,4,64,1536]{3,2,1,0:T(8,128)(2,1)}, u32[]{:S(2)}, u32[]{:S(2)}) collective-permute-start(bf16[1,4,64,1536]{3,2,1,0:T(8,128)(2,1)S(1)} %collective-permute-done.4), channel_id=1, source_target_pairs={{0,8},{2,10},{8,16},{10,18},{12,4},{14,6},{16,24},{18,26},{20,12},... | collective-permute-start | bytes 2359304 | tf_op jit(solution)/shard_map/ppermute | solution.py:220
  49.6 0.7 copy.9.lists_ref
  50.3 2.0 %collective-permute-start.1 = (bf16[1,4,64,1536]{3,2,1,0:T(8,128)(2,1)S(1)}, bf16[1,4,64,1536]{3,2,1,0:T(8,128)(2,1)}, u32[]{:S(2)}, u32[]{:S(2)}) collective-permute-start(bf16[1,4,64,1536]{3,2,1,0:T(8,128)(2,1)S(1)} %copy-done.1), channel_id=1, source_target_pairs={{0,8},{2,10},{8,16},{10,18},{12,4},{14,6},{16,24},{18,26},{20,12},... | collective-permute-start | bytes 2359304 | tf_op jit(solution)/shard_map/ppermute | solution.py:220
  52.4 1.3 collective-permute-start.3
  53.7 10.7 %collective-permute-done = bf16[1,4,64,1536]{3,2,1,0:T(8,128)(2,1)} collective-permute-done((bf16[1,4,64,1536]{3,2,1,0:T(8,128)(2,1)S(1)}, bf16[1,4,64,1536]{3,2,1,0:T(8,128)(2,1)}, u32[]{:S(2)}, u32[]{:S(2)}) %collective-permute-start) | collective-permute-done | bytes 786464 | tf_op jit(solution)/shard_map/ppermute | solution.py:220
  64.4 1.3 collective-permute-start.5
  65.7 15.6 %collective-permute-done.6 = bf16[1,4,64,1536]{3,2,1,0:T(8,128)(2,1)} collective-permute-done((bf16[1,4,64,1536]{3,2,1,0:T(8,128)(2,1)S(1)}, bf16[1,4,64,1536]{3,2,1,0:T(8,128)(2,1)}, u32[]{:S(2)}, u32[]{:S(2)}) %collective-permute-start.6) | collective-permute-done | bytes 786464 | tf_op jit(solution)/shard_map/ppermute | solution.py:220
  81.3 4.3 %collective-permute-start.7 = (bf16[1,4,64,1536]{3,2,1,0:T(8,128)(2,1)}, bf16[1,4,64,1536]{3,2,1,0:T(8,128)(2,1)}, u32[]{:S(2)}, u32[]{:S(2)}) collective-permute-start(bf16[1,4,64,1536]{3,2,1,0:T(8,128)(2,1)} %collective-permute-done.6), channel_id=1, source_target_pairs={{2,0},{4,6},{10,8},{12,14},{18,16},{20,22},{26,24},{28,30},{3,1},{... | collective-permute-start | bytes 2359304 | tf_op jit(solution)/shard_map/ppermute | solution.py:220
  85.5 12.6 %collective-permute-done.8 = bf16[1,4,64,1536]{3,2,1,0:T(8,128)(2,1)} collective-permute-done((bf16[1,4,64,1536]{3,2,1,0:T(8,128)(2,1)S(1)}, bf16[1,4,64,1536]{3,2,1,0:T(8,128)(2,1)}, u32[]{:S(2)}, u32[]{:S(2)}) %collective-permute-start.8) | collective-permute-done | bytes 786464 | tf_op jit(solution)/shard_map/ppermute | solution.py:220
  98.1 4.3 %collective-permute-start.9 = (bf16[1,4,64,1536]{3,2,1,0:T(8,128)(2,1)}, bf16[1,4,64,1536]{3,2,1,0:T(8,128)(2,1)}, u32[]{:S(2)}, u32[]{:S(2)}) collective-permute-start(bf16[1,4,64,1536]{3,2,1,0:T(8,128)(2,1)} %collective-permute-done.8), channel_id=1, source_target_pairs={{2,0},{4,6},{10,8},{12,14},{18,16},{20,22},{26,24},{28,30},{3,1},{... | collective-permute-start | bytes 2359304 | tf_op jit(solution)/shard_map/ppermute | solution.py:220
  102.4 2.1 %fusion.3 = (bf16[1,2,64,1536]{3,2,1,0:T(8,128)(2,1)}, bf16[1,2,64,1536]{3,2,1,0:T(8,128)(2,1)}) fusion(bf16[2,2,64,1536]{3,2,1,0:T(8,128)(2,1)} %copy-done.6), kind=kLoop, calls=%fused_computation.5 | loop fusion | bytes 1572864 | tf_op jit(solution)/shard_map/slice | solution.py:250
  104.4 0.9 fusion
  105.4 8.0 %shard_map.55 = (f32[256,1536]{1,0:T(8,128)}, f32[256,1536]{1,0:T(8,128)}) custom-call(s32[1,2,6,2]{3,2,1,0:T(8,128)} %copy.9.lists_ref, s32[1,3]{1,0:T(1,128)} %density_ref.7, bf16[256,1536]{1,0:T(8,128)(2,1)} %bitcast.22, bf16[256,1536]{1,0:T(8,128)(2,1)} %bitcast.26, bf16[256,1536]{1,0:T(8,128)(2,1)} %bitcast.27, bf16[128,1536]{1,0:T(8,128)(2,1)} %bitcast.29, ...), custom_call_target="tpu_custom_call" | custom-call | flops 805306368 | bytes 6291456 | tf_op jit(solution)/shard_map/pallas_call | solution.py:197
  113.4 13.5 %shard_map.56 = (f32[256,1536]{1,0:T(8,128)}, f32[256,1536]{1,0:T(8,128)}) custom-call(s32[1,2,6,2]{3,2,1,0:T(8,128)} %copy.9.lists_ref, s32[1,3]{1,0:T(1,128)} %density_ref.7, bf16[256,1536]{1,0:T(8,128)(2,1)} %bitcast.23, bf16[256,1536]{1,0:T(8,128)(2,1)} %bitcast.9.refs_1_, bf16[256,1536]{1,0:T(8,128)(2,1)} %bitcast.34, bf16[256,1536]{1,0:T(8,128)(2,1)} %bitcast.32, ...), custom_call_target="tpu_custom_call" | custom-call | flops 1207959552 | bytes 7864320 | tf_op jit(solution)/shard_map/pallas_call | solution.py:197
  126.9 10.9 %shard_map.57 = (f32[256,1536]{1,0:T(8,128)}, f32[256,1536]{1,0:T(8,128)}) custom-call(s32[1,2,6,2]{3,2,1,0:T(8,128)} %copy.9.lists_ref, s32[1,3]{1,0:T(1,128)} %density_ref.7, bf16[256,1536]{1,0:T(8,128)(2,1)} %bitcast.24, bf16[256,1536]{1,0:T(8,128)(2,1)} %bitcast.7.refs_1_, bf16[256,1536]{1,0:T(8,128)(2,1)} %bitcast.8.refs_2_, ...), custom_call_target="tpu_custom_call" | custom-call | flops 402653184 | bytes 4718592 | tf_op jit(solution)/shard_map/pallas_call | solution.py:197
  137.9 0.9 copy-done.9
  138.8 9.4 %shard_map.58 = bf16[256,1536]{1,0:T(8,128)(2,1)} custom-call(s32[1,2,6,2]{3,2,1,0:T(8,128)} %copy.9.lists_ref, s32[1,3]{1,0:T(1,128)} %density_ref.7, bf16[256,1536]{1,0:T(8,128)(2,1)} %bitcast.25, bf16[256,1536]{1,0:T(8,128)(2,1)} %bitcast.1.refs_1_, bf16[256,1536]{1,0:T(8,128)(2,1)} %bitcast.2.refs_2_, bf16[256,1536]{1,0:T(8,128)(2,1)} %bitcast.3.refs_3_, ...), custom_call_target="tpu_custom_call" | custom-call | flops 805306368 | bytes 6291456 | tf_op jit(solution)/shard_map/pallas_call | solution.py:197
  (33 shorter events, 0.3 us)
Async XLA Ops:
  0.0 1.4 copy-start.1
  1.4 3.4 %copy-start = (bf16[1,4,64,1536]{3,2,1,0:T(8,128)(2,1)S(1)}, bf16[1,4,64,1536]{3,2,1,0:T(8,128)(2,1)}, u32[]{:S(2)}) copy-start(bf16[1,4,64,1536]{3,2,1,0:T(8,128)(2,1)} %param.6) | copy-start | bytes 2359300
  1.4 48.1 %copy-start.10 = (s32[1,2,6,2]{2,3,1,0:T(2,128)S(1)}, s32[1,2,6,2]{2,3,1,0:T(2,128)}, u32[]{:S(2)}) copy-start(s32[1,2,6,2]{2,3,1,0:T(2,128)} %param.8) | copy-start | bytes 292
  1.5 6.9 %collective-permute-start.14 = (bf16[2,2,64,1536]{3,2,1,0:T(8,128)(2,1)S(1)}, bf16[2,2,64,1536]{3,2,1,0:T(8,128)(2,1)S(1)}, u32[]{:S(2)}, u32[]{:S(2)}) collective-permute-start(bf16[2,2,64,1536]{3,2,1,0:T(8,128)(2,1)S(1)} %pad_maximum_fusion), channel_id=1, source_target_pairs={{0,1},{2,3},{4,5},{6,7},{8,9},{10,11},{12,13},{14,15},{16,17},{18,... | collective-permute-start | bytes 2359304 | tf_op jit(solution)/shard_map/ppermute | solution.py:220
  3.6 8.4 %collective-permute-start.15 = (bf16[2,2,64,1536]{3,2,1,0:T(8,128)(2,1)S(1)}, bf16[2,2,64,1536]{3,2,1,0:T(8,128)(2,1)S(1)}, u32[]{:S(2)}, u32[]{:S(2)}) collective-permute-start(bf16[2,2,64,1536]{3,2,1,0:T(8,128)(2,1)S(1)} %pad_maximum_fusion.1), channel_id=1, source_target_pairs={{1,0},{3,2},{5,4},{7,6},{9,8},{11,10},{13,12},{15,14},{17,16},{19,... | collective-permute-start | bytes 2359304 | tf_op jit(solution)/shard_map/ppermute | solution.py:220
  4.9 20.3 %collective-permute-start.2 = (bf16[1,4,64,1536]{3,2,1,0:T(8,128)(2,1)S(1)}, bf16[1,4,64,1536]{3,2,1,0:T(8,128)(2,1)S(1)}, u32[]{:S(2)}, u32[]{:S(2)}) collective-permute-start(bf16[1,4,64,1536]{3,2,1,0:T(8,128)(2,1)S(1)} %copy-done), channel_id=1, source_target_pairs={{0,4},{2,6},{4,0},{6,2},{8,12},{10,14},{12,8},{14,10},{16,20},{18,... | collective-permute-start | bytes 2359304 | tf_op jit(solution)/shard_map/ppermute | solution.py:220
  5.4 36.6 %collective-permute-start.4 = (bf16[1,4,64,1536]{3,2,1,0:T(8,128)(2,1)S(1)}, bf16[1,4,64,1536]{3,2,1,0:T(8,128)(2,1)S(1)}, u32[]{:S(2)}, u32[]{:S(2)}) collective-permute-start(bf16[1,4,64,1536]{3,2,1,0:T(8,128)(2,1)S(1)} %copy-done.1), channel_id=1, source_target_pairs={{0,4},{2,6},{4,0},{6,2},{8,12},{10,14},{12,8},{14,10},{16,20},{18,... | collective-permute-start | bytes 2359304 | tf_op jit(solution)/shard_map/ppermute | solution.py:220
  7.0 37.4 %collective-permute-start.11 = (bf16[1,4,64,1536]{3,2,1,0:T(8,128)(2,1)S(1)}, bf16[1,4,64,1536]{3,2,1,0:T(8,128)(2,1)S(1)}, u32[]{:S(2)}, u32[]{:S(2)}) collective-permute-start(bf16[1,4,64,1536]{3,2,1,0:T(8,128)(2,1)S(1)} %copy-done.1), channel_id=1, source_target_pairs={{0,2},{2,0},{4,6},{6,4},{8,10},{10,8},{12,14},{14,12},{16,18},{18,... | collective-permute-start | bytes 2359304 | tf_op jit(solution)/shard_map/ppermute | solution.py:220
  8.4 38.3 %copy-start.6 = (bf16[2,2,64,1536]{3,2,1,0:T(8,128)(2,1)}, bf16[2,2,64,1536]{3,2,1,0:T(8,128)(2,1)S(1)}, u32[]{:S(2)}) copy-start(bf16[2,2,64,1536]{3,2,1,0:T(8,128)(2,1)S(1)} %collective-permute-done.14) | copy-start | bytes 2359300
  8.4 38.3 %collective-permute-start.12 = (bf16[1,4,64,1536]{3,2,1,0:T(8,128)(2,1)S(1)}, bf16[1,4,64,1536]{3,2,1,0:T(8,128)(2,1)S(1)}, u32[]{:S(2)}, u32[]{:S(2)}) collective-permute-start(bf16[1,4,64,1536]{3,2,1,0:T(8,128)(2,1)S(1)} %copy-done), channel_id=1, source_target_pairs={{4,12},{6,14},{8,0},{10,2},{12,20},{14,22},{16,8},{18,10},{20,28},... | collective-permute-start | bytes 2359304 | tf_op jit(solution)/shard_map/ppermute | solution.py:220
  11.9 34.8 %copy-start.7 = (bf16[2,2,64,1536]{3,2,1,0:T(8,128)(2,1)}, bf16[2,2,64,1536]{3,2,1,0:T(8,128)(2,1)S(1)}, u32[]{:S(2)}) copy-start(bf16[2,2,64,1536]{3,2,1,0:T(8,128)(2,1)S(1)} %collective-permute-done.15) | copy-start | bytes 2359300
  12.0 38.3 %collective-permute-start.13 = (bf16[1,4,64,1536]{3,2,1,0:T(8,128)(2,1)S(1)}, bf16[1,4,64,1536]{3,2,1,0:T(8,128)(2,1)}, u32[]{:S(2)}, u32[]{:S(2)}) collective-permute-start(bf16[1,4,64,1536]{3,2,1,0:T(8,128)(2,1)S(1)} %copy-done.1), channel_id=1, source_target_pairs={{4,12},{6,14},{8,0},{10,2},{12,20},{14,22},{16,8},{18,10},{20,28},... | collective-permute-start | bytes 2359304 | tf_op jit(solution)/shard_map/ppermute | solution.py:220
  25.1 80.2 %copy-start.2 = (bf16[1,4,64,1536]{3,2,1,0:T(8,128)(2,1)}, bf16[1,4,64,1536]{3,2,1,0:T(8,128)(2,1)S(1)}, u32[]{:S(2)}) copy-start(bf16[1,4,64,1536]{3,2,1,0:T(8,128)(2,1)S(1)} %collective-permute-done.2) | copy-start | bytes 2359300
  25.1 27.2 %collective-permute-start.10 = (bf16[1,4,64,1536]{3,2,1,0:T(8,128)(2,1)S(1)}, bf16[1,4,64,1536]{3,2,1,0:T(8,128)(2,1)}, u32[]{:S(2)}, u32[]{:S(2)}) collective-permute-start(bf16[1,4,64,1536]{3,2,1,0:T(8,128)(2,1)S(1)} %copy-done), channel_id=1, source_target_pairs={{0,2},{2,0},{4,6},{6,4},{8,10},{10,8},{12,14},{14,12},{16,18},{18,... | collective-permute-start | bytes 2359304 | tf_op jit(solution)/shard_map/ppermute | solution.py:220
  42.0 63.4 %copy-start.3 = (bf16[1,4,64,1536]{3,2,1,0:T(8,128)(2,1)}, bf16[1,4,64,1536]{3,2,1,0:T(8,128)(2,1)S(1)}, u32[]{:S(2)}) copy-start(bf16[1,4,64,1536]{3,2,1,0:T(8,128)(2,1)S(1)} %collective-permute-done.4) | copy-start | bytes 2359300
  42.0 22.4 %collective-permute-start = (bf16[1,4,64,1536]{3,2,1,0:T(8,128)(2,1)S(1)}, bf16[1,4,64,1536]{3,2,1,0:T(8,128)(2,1)}, u32[]{:S(2)}, u32[]{:S(2)}) collective-permute-start(bf16[1,4,64,1536]{3,2,1,0:T(8,128)(2,1)S(1)} %copy-done), channel_id=1, source_target_pairs={{0,8},{2,10},{8,16},{10,18},{12,4},{14,6},{16,24},{18,26},{20,12},... | collective-permute-start | bytes 2359304 | tf_op jit(solution)/shard_map/ppermute | solution.py:220
  44.4 2.4 %copy-start.4 = (bf16[1,4,64,1536]{3,2,1,0:T(8,128)(2,1)}, bf16[1,4,64,1536]{3,2,1,0:T(8,128)(2,1)S(1)}, u32[]{:S(2)}) copy-start(bf16[1,4,64,1536]{3,2,1,0:T(8,128)(2,1)S(1)} %collective-permute-done.11) | copy-start | bytes 2359300
  44.4 36.9 %collective-permute-start.6 = (bf16[1,4,64,1536]{3,2,1,0:T(8,128)(2,1)S(1)}, bf16[1,4,64,1536]{3,2,1,0:T(8,128)(2,1)}, u32[]{:S(2)}, u32[]{:S(2)}) collective-permute-start(bf16[1,4,64,1536]{3,2,1,0:T(8,128)(2,1)S(1)} %collective-permute-done.2), channel_id=1, source_target_pairs={{0,8},{2,10},{8,16},{10,18},{12,4},{14,6},{16,24},{18,26},{20,12},... | collective-permute-start | bytes 2359304 | tf_op jit(solution)/shard_map/ppermute | solution.py:220
  46.8 0.9 copy-start.5
  47.7 50.4 %collective-permute-start.8 = (bf16[1,4,64,1536]{3,2,1,0:T(8,128)(2,1)S(1)}, bf16[1,4,64,1536]{3,2,1,0:T(8,128)(2,1)}, u32[]{:S(2)}, u32[]{:S(2)}) collective-permute-start(bf16[1,4,64,1536]{3,2,1,0:T(8,128)(2,1)S(1)} %collective-permute-done.4), channel_id=1, source_target_pairs={{0,8},{2,10},{8,16},{10,18},{12,4},{14,6},{16,24},{18,26},{20,12},... | collective-permute-start | bytes 2359304 | tf_op jit(solution)/shard_map/ppermute | solution.py:220
  50.3 54.1 %copy-start.8 = (bf16[2,2,64,1536]{3,2,1,0:T(8,128)(2,1)S(1)}, bf16[2,2,64,1536]{3,2,1,0:T(8,128)(2,1)}, u32[]{:S(2)}) copy-start(bf16[2,2,64,1536]{3,2,1,0:T(8,128)(2,1)} %copy-done.7) | copy-start | bytes 2359300
  50.3 87.6 %collective-permute-start.1 = (bf16[1,4,64,1536]{3,2,1,0:T(8,128)(2,1)S(1)}, bf16[1,4,64,1536]{3,2,1,0:T(8,128)(2,1)}, u32[]{:S(2)}, u32[]{:S(2)}) collective-permute-start(bf16[1,4,64,1536]{3,2,1,0:T(8,128)(2,1)S(1)} %copy-done.1), channel_id=1, source_target_pairs={{0,8},{2,10},{8,16},{10,18},{12,4},{14,6},{16,24},{18,26},{20,12},... | collective-permute-start | bytes 2359304 | tf_op jit(solution)/shard_map/ppermute | solution.py:220
  52.4 85.5 %collective-permute-start.3 = (bf16[1,4,64,1536]{3,2,1,0:T(8,128)(2,1)S(1)}, bf16[1,4,64,1536]{3,2,1,0:T(8,128)(2,1)}, u32[]{:S(2)}, u32[]{:S(2)}) collective-permute-start(bf16[1,4,64,1536]{3,2,1,0:T(8,128)(2,1)S(1)} %collective-permute-done.2), channel_id=1, source_target_pairs={{0,2},{6,4},{8,10},{14,12},{16,18},{22,20},{24,26},{30,28},{1,3},{... | collective-permute-start | bytes 2359304 | tf_op jit(solution)/shard_map/ppermute | solution.py:220
  64.4 73.5 %collective-permute-start.5 = (bf16[1,4,64,1536]{3,2,1,0:T(8,128)(2,1)S(1)}, bf16[1,4,64,1536]{3,2,1,0:T(8,128)(2,1)S(1)}, u32[]{:S(2)}, u32[]{:S(2)}) collective-permute-start(bf16[1,4,64,1536]{3,2,1,0:T(8,128)(2,1)S(1)} %collective-permute-done.4), channel_id=1, source_target_pairs={{0,2},{6,4},{8,10},{14,12},{16,18},{22,20},{24,26},{30,28},{1,3},{... | collective-permute-start | bytes 2359304 | tf_op jit(solution)/shard_map/ppermute | solution.py:220
  81.3 56.6 %collective-permute-start.7 = (bf16[1,4,64,1536]{3,2,1,0:T(8,128)(2,1)}, bf16[1,4,64,1536]{3,2,1,0:T(8,128)(2,1)}, u32[]{:S(2)}, u32[]{:S(2)}) collective-permute-start(bf16[1,4,64,1536]{3,2,1,0:T(8,128)(2,1)} %collective-permute-done.6), channel_id=1, source_target_pairs={{2,0},{4,6},{10,8},{12,14},{18,16},{20,22},{26,24},{28,30},{3,1},{... | collective-permute-start | bytes 2359304 | tf_op jit(solution)/shard_map/ppermute | solution.py:220
  98.1 39.8 %collective-permute-start.9 = (bf16[1,4,64,1536]{3,2,1,0:T(8,128)(2,1)}, bf16[1,4,64,1536]{3,2,1,0:T(8,128)(2,1)}, u32[]{:S(2)}, u32[]{:S(2)}) collective-permute-start(bf16[1,4,64,1536]{3,2,1,0:T(8,128)(2,1)} %collective-permute-done.8), channel_id=1, source_target_pairs={{2,0},{4,6},{10,8},{12,14},{18,16},{20,22},{26,24},{28,30},{3,1},{... | collective-permute-start | bytes 2359304 | tf_op jit(solution)/shard_map/ppermute | solution.py:220
  137.9 0.9 copy-start.9

commit v2 on v1

v2 whole, which is shorter than its diff:
```python
import math

import jax
import jax.numpy as jnp
from jax import lax
from jax.experimental import pallas as pl
from jax.experimental.pallas import tpu as pltpu
from jax.sharding import PartitionSpec as P


HEAD_DIM = 128
OFFSETS = 3
GROUP = 2 ** (OFFSETS - 1)
SUBLANES = 8
UNROLL = 4
VMEM_LIMIT = 16 * 2**20
NEG = -1e30
SCALE2 = math.log2(math.e) / math.sqrt(HEAD_DIM)


def routes(count):
    def pairs(target):
        out = []
        for t in range(count):
            to = target(t, t % GROUP)
            if to is not None and 0 <= to < count:
                out.append((t, to))
        return out

    up = GROUP // 2
    return {
        "x": pairs(lambda t, p: t ^ 1),
        "y": pairs(lambda t, p: t ^ 2),
        "o": pairs(lambda t, p: t - GROUP if p < up else t + GROUP),
        "b": pairs(lambda t, p: t + GROUP if p < up else t - GROUP),
        "g": pairs(lambda t, p: t ^ 1 if p in (0, GROUP - 1) else None),
        "e": pairs(lambda t, p: t ^ 1 if p not in (0, GROUP - 1) else None),
    }


def slot_of(name, p):
    low = (p < GROUP // 2).astype(jnp.int32)
    even = 1 - p % 2
    return {
        "X": even,
        "Y": 2 + low,
        "O": 4 + low,
        "B": 5 - low,
        "W": 3 - low,
        "GE": 1 - even,
    }[name]


def contract(a, b, dims):
    return lax.dot_general(a, b, (dims, ((), ())), preferred_element_type=jnp.float32)


def fold(value, op):
    return op(value.reshape(-1, SUBLANES, value.shape[1]), axis=0)


def flash(q, blocks, state, halves):
    lanes = q.shape[0] // halves
    scores = [contract(k, q, ((1,), (1,))) for k, _, _ in blocks]
    tops, shifts = [], []
    for half in range(halves):
        cols = slice(half * lanes, (half + 1) * lanes)
        top = None if state is None else state[0][:, cols]
        for s, (_, _, allow) in zip(scores, blocks):
            rows = s.shape[0] // len(allow[half])
            for kb, ok in enumerate(allow[half]):
                piece = fold(s[kb * rows : (kb + 1) * rows, cols], jnp.max)
                if ok is not None:
                    piece = jnp.where(ok, piece, NEG)
                top = piece if top is None else jnp.maximum(top, piece)
        top = jnp.max(top, axis=0, keepdims=True)
        tops.append(top)
        shifts.append(top * SCALE2)
    sums = [None] * halves
    acc = None
    for s, (_, v, allow) in zip(scores, blocks):
        parts = []
        for half in range(halves):
            cols = slice(half * lanes, (half + 1) * lanes)
            rows = s.shape[0] // len(allow[half])
            down = []
            for kb, ok in enumerate(allow[half]):
                off = shifts[half] if ok is None else jnp.where(ok, shifts[half], -NEG)
                w = jnp.exp2(s[kb * rows : (kb + 1) * rows, cols] * SCALE2 - off)
                part = fold(w, jnp.sum)
                sums[half] = part if sums[half] is None else sums[half] + part
                down.append(w.astype(jnp.bfloat16))
            parts.append(down[0] if len(down) == 1 else jnp.concatenate(down, axis=0))
        mixed = contract(v, jnp.concatenate(parts, axis=1), ((0,), (0,)))
        acc = mixed if acc is None else acc + mixed
    top = jnp.concatenate(tops, axis=1)
    total = jnp.concatenate(sums, axis=1)
    if state is not None:
        decay = jnp.exp2((state[0][0:1] - top) * SCALE2)
        total = total + state[1] * decay
        acc = acc + state[2] * decay
    return top, total, acc


def stage_call(q, entries, state, lists, density, final):
    tokens, features = q.shape
    heads = features // HEAD_DIM
    kinds = [kind for kind, _, _ in entries]
    halves = lists.shape[1]
    positions = lists.shape[3]
    frames = lax.axis_size("tm")
    bands = lax.axis_size("space")
    edge = tokens // halves
    n_in = 2 * len(entries)

    def kernel(lists_ref, density_ref, *refs):
        q_ref = refs[0]
        kv = refs[1 : 1 + n_in]
        rest = refs[1 + n_in :]
        old_refs = None
        if state is not None:
            old_refs = rest[:3]
            rest = rest[3:]
        t = lax.axis_index("tm")
        band = lax.axis_index("space")
        p = t % GROUP

        def allow_of(kind):
            if kind in ("own", "other"):
                return [[None]] * halves
            if kind == "before":
                return [[band > 0]] * halves
            if kind == "after":
                return [[band < bands - 1]] * halves
            slot = slot_of(kind, p)
            step = jnp.left_shift(1, slot // 2)
            there = t + jnp.where(slot % 2 == 0, -step, step)
            ok = (there >= 0) & (there < frames)
            live = density_ref[0, slot // 2]
            out = []
            for half in range(halves):
                row = []
                for kb in range(positions):
                    hit = (lists_ref[0, half, slot, 0] == kb) & (live > 0)
                    for i in range(1, positions):
                        hit = hit | ((lists_ref[0, half, slot, i] == kb) & (live > i))
                    row.append(ok & hit)
                out.append(row)
            return out

        rows_of = {
            "before": pl.ds(tokens - edge, edge),
            "after": pl.ds(0, edge),
            "other": pl.ds(pl.multiple_of(jnp.where(band > 0, tokens - edge, 0), edge), edge),
        }
        allows = [allow_of(kind) for kind in kinds if kind != "E"]
        wrap = (p == 0) | (p == GROUP - 1)

        def one_head(h, carry):
            cols = pl.ds(pl.multiple_of(h * HEAD_DIM, HEAD_DIM), HEAD_DIM)
            blocks = []
            for i, kind in enumerate(kinds):
                if kind == "E":
                    continue
                rows = rows_of.get(kind, slice(None))
                k, v = kv[2 * i][rows, cols], kv[2 * i + 1][rows, cols]
                if kind == "GE":
                    j = kinds.index("E")
                    k = jnp.where(wrap, kv[2 * j][:, cols], k)
                    v = jnp.where(wrap, kv[2 * j + 1][:, cols], v)
                blocks.append((k, v, allows[len(blocks)]))
            old = None if state is None else [ref[h] for ref in old_refs]
            top, total, acc = flash(q_ref[:, cols], blocks, old, halves)
            if final:
                scaled = acc * (1.0 / jnp.sum(total, axis=0, keepdims=True))
                rest[0][:, cols] = jnp.transpose(scaled).astype(jnp.bfloat16)
            else:
                rest[0][h] = jnp.broadcast_to(top, (SUBLANES, tokens))
                rest[1][h] = total
                rest[2][h] = acc
            return carry

        lax.fori_loop(0, heads, one_head, 0, unroll=UNROLL)

    smem = pl.BlockSpec(memory_space=pltpu.SMEM)
    vmem = pl.BlockSpec(memory_space=pltpu.VMEM)
    operands = [lists, density, q]
    keys = 0
    for kind, k, v in entries:
        operands += [k, v]
        keys += k.shape[0] if kind != "E" else 0
    if state is not None:
        operands += list(state)
    operands = operands[:2] + [
        pltpu.with_memory_space_constraint(value, pltpu.VMEM) for value in operands[2:]
    ]
    specs = [smem, smem] + [vmem] * (len(operands) - 2)
    if final:
        outs, out_specs = jax.ShapeDtypeStruct((tokens, features), jnp.bfloat16), vmem
    else:
        small = pltpu.VMEM((heads, SUBLANES, tokens), jnp.float32)
        large = pltpu.VMEM((heads, HEAD_DIM, tokens), jnp.float32)
        outs, out_specs = (small, small, large), (vmem, vmem, vmem)
    return pl.pallas_call(
        kernel,
        in_specs=specs,
        out_specs=out_specs,
        out_shape=outs,
        compiler_params=pltpu.CompilerParams(vmem_limit_bytes=VMEM_LIMIT),
        cost_estimate=pl.CostEstimate(
            flops=4 * tokens * keys * features,
            transcendentals=tokens * keys * heads,
            bytes_accessed=2 * features * (2 * keys + 4 * tokens),
        ),
    )(*operands)


def body(queries, keys, values, key_lists, density):
    _, rows_dev, width, features = queries.shape
    frames = lax.axis_size("tm")
    bands = lax.axis_size("space")
    route = routes(frames)
    up = [(i, i + 1) for i in range(bands - 1)]
    down = [(j, i) for i, j in up]

    def send(value, pairs, axis="tm"):
        return lax.ppermute(value, axis, pairs)

    def flat(value):
        return value.reshape(-1, features)

    y_k = send(keys, route["y"])
    x_k = send(keys, route["x"])
    o_k = send(keys, route["o"])
    b_k = send(keys, route["b"])
    y_v = send(values, route["y"])
    x_v = send(values, route["x"])
    o_v = send(values, route["o"])
    if bands == 2:
        s_k = send(keys, up + down, "space")
        s_v = send(values, up + down, "space")
        beside = [("other", flat(s_k), flat(s_v))]
    else:
        up_k = send(keys, up, "space")
        up_v = send(values, up, "space")
        down_k = send(keys, down, "space")
        down_v = send(values, down, "space")
        beside = [("before", flat(up_k), flat(up_v)), ("after", flat(down_k), flat(down_v))]
    w_k = send(y_k, route["b"])
    g_k = send(y_k, route["g"])
    w_v = send(y_v, route["b"])
    e_k = send(w_k, route["e"])
    g_v = send(y_v, route["g"])
    b_v = send(values, route["b"])
    e_v = send(w_v, route["e"])

    q = flat(queries)
    state = stage_call(
        q, [("own", flat(keys), flat(values))] + beside, None, key_lists, density, False
    )
    state = stage_call(
        q,
        [
            ("X", flat(x_k), flat(x_v)),
            ("Y", flat(y_k), flat(y_v)),
            ("O", flat(o_k), flat(o_v)),
        ],
        state,
        key_lists,
        density,
        False,
    )
    state = stage_call(
        q, [("W", flat(w_k), flat(w_v))], state, key_lists, density, False
    )
    result = stage_call(
        q,
        [
            ("B", flat(b_k), flat(b_v)),
            ("GE", flat(g_k), flat(g_v)),
            ("E", flat(e_k), flat(e_v)),
        ],
        state,
        key_lists,
        density,
        True,
    )
    return result.reshape(1, rows_dev, width, features)


def solution(mesh):
    in_specs = (
        P("tm", "space", None, None),
        P("tm", "space", None, None),
        P("tm", "space", None, None),
        P("tm", "space", None, None),
        P("tm", None),
    )
    out_specs = P("tm", "space", None, None)
    return jax.shard_map(body, mesh=mesh, in_specs=in_specs, out_specs=out_specs, check_vma=False)
```

time: 149 us -> 130 us (0.87)
  the two profiles are of different devices: /device:TPU:20 before, /device:TPU:12 now
where the time goes in v2:
time: 130 us
  waiting for transfers between devices  60.4 us (46%)
  starting transfers between devices  31.7 us (24%)
  Pallas kernels  24.9 us (19%)
  local copies, waits for them, and re-layouts  12.5 us (10%)
    ppermute x16, waiting for transfers between devices, send(): return lax.ppermute(value, axis, pairs)  60.4 us
    ppermute x16, starting transfers between devices, send(): return lax.ppermute(value, axis, pairs)  31.7 us
    pallas_call x4, Pallas kernels, stage_call(): pl.pallas_call(kernel, in_specs=specs, out_specs=out_specs, out_shape=out...  24.9 us
    unnamed x33, local copies, waits for them, and re-layouts  12.5 us
  transfers between devices with their start and end apart: 16, of which 5 were waited for; matrix products, arithmetic and copies ran while one was open for 1% of the time, Pallas kernels for 13%

profile of v2, /device:TPU:12, one launch (start us, length us, event | category | flops | bytes accessed | tf_op | source)
XLA Modules:
  0.0 129.8 jit_solution(15483318055468838177)
XLA Ops:
  1.0 1.5 %collective-permute-start.4 = (bf16[1,4,64,1536]{3,2,1,0:T(8,128)(2,1)}, bf16[1,4,64,1536]{3,2,1,0:T(8,128)(2,1)}, u32[]{:S(2)}, u32[]{:S(2)}) collective-permute-start(bf16[1,4,64,1536]{3,2,1,0:T(8,128)(2,1)} %param.7), channel_id=1, source_target_pairs={{0,4},{2,6},{4,0},{6,2},{8,12},{10,14},{12,8},{14,10},{16,20},{18,... | collective-permute-start | bytes 2359304 | tf_op jit(solution)/shard_map/ppermute | solution.py:227
  2.5 1.5 %collective-permute-start.11 = (bf16[1,4,64,1536]{3,2,1,0:T(8,128)(2,1)}, bf16[1,4,64,1536]{3,2,1,0:T(8,128)(2,1)S(1)}, u32[]{:S(2)}, u32[]{:S(2)}) collective-permute-start(bf16[1,4,64,1536]{3,2,1,0:T(8,128)(2,1)} %param.7), channel_id=1, source_target_pairs={{0,2},{2,0},{4,6},{6,4},{8,10},{10,8},{12,14},{14,12},{16,18},{18,... | collective-permute-start | bytes 2359304 | tf_op jit(solution)/shard_map/ppermute | solution.py:227
  4.0 0.9 copy-done.3
  4.9 3.5 %collective-permute-start.12 = (bf16[1,4,64,1536]{3,2,1,0:T(8,128)(2,1)}, bf16[1,4,64,1536]{3,2,1,0:T(8,128)(2,1)S(1)}, u32[]{:S(2)}, u32[]{:S(2)}) collective-permute-start(bf16[1,4,64,1536]{3,2,1,0:T(8,128)(2,1)} %param.6), channel_id=1, source_target_pairs={{4,12},{6,14},{8,0},{10,2},{12,20},{14,22},{16,8},{18,10},{20,28},... | collective-permute-start | bytes 2359304 | tf_op jit(solution)/shard_map/ppermute | solution.py:227
  8.4 0.9 copy-done.5
  9.4 3.5 %collective-permute-start.13 = (bf16[1,4,64,1536]{3,2,1,0:T(8,128)(2,1)}, bf16[1,4,64,1536]{3,2,1,0:T(8,128)(2,1)S(1)}, u32[]{:S(2)}, u32[]{:S(2)}) collective-permute-start(bf16[1,4,64,1536]{3,2,1,0:T(8,128)(2,1)} %param.7), channel_id=1, source_target_pairs={{4,12},{6,14},{8,0},{10,2},{12,20},{14,22},{16,8},{18,10},{20,28},... | collective-permute-start | bytes 2359304 | tf_op jit(solution)/shard_map/ppermute | solution.py:227
  12.9 8.4 %collective-permute-done.2 = bf16[1,4,64,1536]{3,2,1,0:T(8,128)(2,1)} collective-permute-done((bf16[1,4,64,1536]{3,2,1,0:T(8,128)(2,1)}, bf16[1,4,64,1536]{3,2,1,0:T(8,128)(2,1)}, u32[]{:S(2)}, u32[]{:S(2)}) %collective-permute-start.2) | collective-permute-done | bytes 786464 | tf_op jit(solution)/shard_map/ppermute | solution.py:227
  21.2 1.5 %collective-permute-start.10 = (bf16[1,4,64,1536]{3,2,1,0:T(8,128)(2,1)}, bf16[1,4,64,1536]{3,2,1,0:T(8,128)(2,1)S(1)}, u32[]{:S(2)}, u32[]{:S(2)}) collective-permute-start(bf16[1,4,64,1536]{3,2,1,0:T(8,128)(2,1)} %param.6), channel_id=1, source_target_pairs={{0,2},{2,0},{4,6},{6,4},{8,10},{10,8},{12,14},{14,12},{16,18},{18,... | collective-permute-start | bytes 2359304 | tf_op jit(solution)/shard_map/ppermute | solution.py:227
  22.7 14.4 %collective-permute-done.4 = bf16[1,4,64,1536]{3,2,1,0:T(8,128)(2,1)} collective-permute-done((bf16[1,4,64,1536]{3,2,1,0:T(8,128)(2,1)}, bf16[1,4,64,1536]{3,2,1,0:T(8,128)(2,1)}, u32[]{:S(2)}, u32[]{:S(2)}) %collective-permute-start.4) | collective-permute-done | bytes 786464 | tf_op jit(solution)/shard_map/ppermute | solution.py:227
  37.1 2.3 %collective-permute-start = (bf16[1,4,64,1536]{3,2,1,0:T(8,128)(2,1)}, bf16[1,4,64,1536]{3,2,1,0:T(8,128)(2,1)S(1)}, u32[]{:S(2)}, u32[]{:S(2)}) collective-permute-start(bf16[1,4,64,1536]{3,2,1,0:T(8,128)(2,1)} %param.6), channel_id=1, source_target_pairs={{0,8},{2,10},{8,16},{10,18},{12,4},{14,6},{16,24},{18,26},{20,12},... | collective-permute-start | bytes 2359304 | tf_op jit(solution)/shard_map/ppermute | solution.py:227
  39.5 0.9 copy-done.7
  40.4 1.9 %collective-permute-start.6 = (bf16[1,4,64,1536]{3,2,1,0:T(8,128)(2,1)}, bf16[1,4,64,1536]{3,2,1,0:T(8,128)(2,1)S(1)}, u32[]{:S(2)}, u32[]{:S(2)}) collective-permute-start(bf16[1,4,64,1536]{3,2,1,0:T(8,128)(2,1)} %collective-permute-done.2), channel_id=1, source_target_pairs={{0,8},{2,10},{8,16},{10,18},{12,4},{14,6},{16,24},{18,26},{20,12},... | collective-permute-start | bytes 2359304 | tf_op jit(solution)/shard_map/ppermute | solution.py:227
  42.3 0.9 copy-done.9
  43.2 1.9 %collective-permute-start.8 = (bf16[1,4,64,1536]{3,2,1,0:T(8,128)(2,1)}, bf16[1,4,64,1536]{3,2,1,0:T(8,128)(2,1)S(1)}, u32[]{:S(2)}, u32[]{:S(2)}) collective-permute-start(bf16[1,4,64,1536]{3,2,1,0:T(8,128)(2,1)} %collective-permute-done.4), channel_id=1, source_target_pairs={{0,8},{2,10},{8,16},{10,18},{12,4},{14,6},{16,24},{18,26},{20,12},... | collective-permute-start | bytes 2359304 | tf_op jit(solution)/shard_map/ppermute | solution.py:227
  45.2 0.9 copy-done.11
  46.1 1.9 %collective-permute-start.1 = (bf16[1,4,64,1536]{3,2,1,0:T(8,128)(2,1)}, bf16[1,4,64,1536]{3,2,1,0:T(8,128)(2,1)S(1)}, u32[]{:S(2)}, u32[]{:S(2)}) collective-permute-start(bf16[1,4,64,1536]{3,2,1,0:T(8,128)(2,1)} %param.7), channel_id=1, source_target_pairs={{0,8},{2,10},{8,16},{10,18},{12,4},{14,6},{16,24},{18,26},{20,12},... | collective-permute-start | bytes 2359304 | tf_op jit(solution)/shard_map/ppermute | solution.py:227
  48.9 1.3 collective-permute-start.3
  50.2 9.5 %collective-permute-done = bf16[1,4,64,1536]{3,2,1,0:T(8,128)(2,1)S(1)} collective-permute-done((bf16[1,4,64,1536]{3,2,1,0:T(8,128)(2,1)}, bf16[1,4,64,1536]{3,2,1,0:T(8,128)(2,1)S(1)}, u32[]{:S(2)}, u32[]{:S(2)}) %collective-permute-start) | collective-permute-done | bytes 786464 | tf_op jit(solution)/shard_map/ppermute | solution.py:227
  59.6 1.3 collective-permute-start.5
  60.9 15.6 %collective-permute-done.6 = bf16[1,4,64,1536]{3,2,1,0:T(8,128)(2,1)S(1)} collective-permute-done((bf16[1,4,64,1536]{3,2,1,0:T(8,128)(2,1)}, bf16[1,4,64,1536]{3,2,1,0:T(8,128)(2,1)S(1)}, u32[]{:S(2)}, u32[]{:S(2)}) %collective-permute-start.6) | collective-permute-done | bytes 786464 | tf_op jit(solution)/shard_map/ppermute | solution.py:227
  76.5 4.3 %collective-permute-start.7 = (bf16[1,4,64,1536]{3,2,1,0:T(8,128)(2,1)S(1)}, bf16[1,4,64,1536]{3,2,1,0:T(8,128)(2,1)}, u32[]{:S(2)}, u32[]{:S(2)}) collective-permute-start(bf16[1,4,64,1536]{3,2,1,0:T(8,128)(2,1)S(1)} %collective-permute-done.6), channel_id=1, source_target_pairs={{2,0},{4,6},{10,8},{12,14},{18,16},{20,22},{26,24},{28,30},{3,1},{... | collective-permute-start | bytes 2359304 | tf_op jit(solution)/shard_map/ppermute | solution.py:227
  80.8 12.6 %collective-permute-done.8 = bf16[1,4,64,1536]{3,2,1,0:T(8,128)(2,1)S(1)} collective-permute-done((bf16[1,4,64,1536]{3,2,1,0:T(8,128)(2,1)}, bf16[1,4,64,1536]{3,2,1,0:T(8,128)(2,1)S(1)}, u32[]{:S(2)}, u32[]{:S(2)}) %collective-permute-start.8) | collective-permute-done | bytes 786464 | tf_op jit(solution)/shard_map/ppermute | solution.py:227
  93.3 4.3 %collective-permute-start.9 = (bf16[1,4,64,1536]{3,2,1,0:T(8,128)(2,1)S(1)}, bf16[1,4,64,1536]{3,2,1,0:T(8,128)(2,1)}, u32[]{:S(2)}, u32[]{:S(2)}) collective-permute-start(bf16[1,4,64,1536]{3,2,1,0:T(8,128)(2,1)S(1)} %collective-permute-done.8), channel_id=1, source_target_pairs={{2,0},{4,6},{10,8},{12,14},{18,16},{20,22},{26,24},{28,30},{3,1},{... | collective-permute-start | bytes 2359304 | tf_op jit(solution)/shard_map/ppermute | solution.py:227
  98.4 1.1 copy-done
  99.5 1.1 copy-done.1
  100.7 1.1 copy-done.2
  101.8 1.1 copy-done.4
  102.9 1.1 copy-done.6
  104.7 5.1 %shard_map.55 = (f32[12,8,256]{2,1,0:T(8,128)S(1)}, f32[12,8,256]{2,1,0:T(8,128)S(1)}, f32[12,128,256]{2,1,0:T(8,128)S(1)}) custom-call(s32[1,2,6,2]{3,2,1,0:T(8,128)S(1)} %copy.9.lists_ref, s32[1,3]{1,0:T(1,128)S(1)} %copy-done.15, bf16[256,1536]{1,0:T(8,128)(2,1)S(1)} %bitcast.20, bf16[256,1536]{1,0:T(8,128)(2,1)S(1)} %bitcast.28, ...), custom_call_target="tpu_custom_call" | custom-call | flops 805306368 | bytes 6291456 | tf_op jit(solution)/shard_map/pallas_call | solution.py:204
  109.9 7.2 %shard_map.56 = (f32[12,8,256]{2,1,0:T(8,128)S(1)}, f32[12,8,256]{2,1,0:T(8,128)S(1)}, f32[12,128,256]{2,1,0:T(8,128)S(1)}) custom-call(s32[1,2,6,2]{3,2,1,0:T(8,128)S(1)} %copy.9.lists_ref, s32[1,3]{1,0:T(1,128)S(1)} %copy-done.15, bf16[256,1536]{1,0:T(8,128)(2,1)S(1)} %bitcast.21, bf16[256,1536]{1,0:T(8,128)(2,1)S(1)} %bitcast.35, ...), custom_call_target="tpu_custom_call" | custom-call | flops 1207959552 | bytes 7864320 | tf_op jit(solution)/shard_map/pallas_call | solution.py:204
  117.1 4.7 %shard_map.57 = (f32[12,8,256]{2,1,0:T(8,128)S(1)}, f32[12,8,256]{2,1,0:T(8,128)S(1)}, f32[12,128,256]{2,1,0:T(8,128)S(1)}) custom-call(s32[1,2,6,2]{3,2,1,0:T(8,128)S(1)} %copy.9.lists_ref, s32[1,3]{1,0:T(1,128)S(1)} %copy-done.15, bf16[256,1536]{1,0:T(8,128)(2,1)S(1)} %bitcast.22, bf16[256,1536]{1,0:T(8,128)(2,1)S(1)} %bitcast.25, ...), custom_call_target="tpu_custom_call" | custom-call | flops 402653184 | bytes 4718592 | tf_op jit(solution)/shard_map/pallas_call | solution.py:204
  121.9 7.9 %shard_map.58 = bf16[256,1536]{1,0:T(8,128)(2,1)} custom-call(s32[1,2,6,2]{3,2,1,0:T(8,128)S(1)} %copy.9.lists_ref, s32[1,3]{1,0:T(1,128)S(1)} %copy-done.15, bf16[256,1536]{1,0:T(8,128)(2,1)S(1)} %bitcast.23, bf16[256,1536]{1,0:T(8,128)(2,1)S(1)} %bitcast.24, bf16[256,1536]{1,0:T(8,128)(2,1)S(1)} %bitcast.27, bf16[256,1536]{1,0:T(8,128)(2,1)} %bitcast.3.refs_3_, ...), custom_call_target="tpu_custom_call" | custom-call | flops 805306368 | bytes 6291456 | tf_op jit(solution)/shard_map/pallas_call | solution.py:204
  (37 shorter events, 3.4 us)
Async XLA Ops:
  0.0 4.0 %collective-permute-start.14 = (bf16[1,4,64,1536]{3,2,1,0:T(8,128)(2,1)}, bf16[1,4,64,1536]{3,2,1,0:T(8,128)(2,1)S(1)}, u32[]{:S(2)}, u32[]{:S(2)}) collective-permute-start(bf16[1,4,64,1536]{3,2,1,0:T(8,128)(2,1)} %param.6), channel_id=1, source_target_pairs={{0,1},{1,0},{2,3},{3,2},{4,5},{5,4},{6,7},{7,6},{8,9},{9,8},{10,11... | collective-permute-start | bytes 2359304 | tf_op jit(solution)/shard_map/ppermute | solution.py:227
  0.0 8.4 %collective-permute-start.15 = (bf16[1,4,64,1536]{3,2,1,0:T(8,128)(2,1)}, bf16[1,4,64,1536]{3,2,1,0:T(8,128)(2,1)S(1)}, u32[]{:S(2)}, u32[]{:S(2)}) collective-permute-start(bf16[1,4,64,1536]{3,2,1,0:T(8,128)(2,1)} %param.7), channel_id=1, source_target_pairs={{0,1},{1,0},{2,3},{3,2},{4,5},{5,4},{6,7},{7,6},{8,9},{9,8},{10,11... | collective-permute-start | bytes 2359304 | tf_op jit(solution)/shard_map/ppermute | solution.py:227
  0.5 20.7 %collective-permute-start.2 = (bf16[1,4,64,1536]{3,2,1,0:T(8,128)(2,1)}, bf16[1,4,64,1536]{3,2,1,0:T(8,128)(2,1)}, u32[]{:S(2)}, u32[]{:S(2)}) collective-permute-start(bf16[1,4,64,1536]{3,2,1,0:T(8,128)(2,1)} %param.6), channel_id=1, source_target_pairs={{0,4},{2,6},{4,0},{6,2},{8,12},{10,14},{12,8},{14,10},{16,20},{18,... | collective-permute-start | bytes 2359304 | tf_op jit(solution)/shard_map/ppermute | solution.py:227
  1.0 36.1 %collective-permute-start.4 = (bf16[1,4,64,1536]{3,2,1,0:T(8,128)(2,1)}, bf16[1,4,64,1536]{3,2,1,0:T(8,128)(2,1)}, u32[]{:S(2)}, u32[]{:S(2)}) collective-permute-start(bf16[1,4,64,1536]{3,2,1,0:T(8,128)(2,1)} %param.7), channel_id=1, source_target_pairs={{0,4},{2,6},{4,0},{6,2},{8,12},{10,14},{12,8},{14,10},{16,20},{18,... | collective-permute-start | bytes 2359304 | tf_op jit(solution)/shard_map/ppermute | solution.py:227
  2.5 37.0 %collective-permute-start.11 = (bf16[1,4,64,1536]{3,2,1,0:T(8,128)(2,1)}, bf16[1,4,64,1536]{3,2,1,0:T(8,128)(2,1)S(1)}, u32[]{:S(2)}, u32[]{:S(2)}) collective-permute-start(bf16[1,4,64,1536]{3,2,1,0:T(8,128)(2,1)} %param.7), channel_id=1, source_target_pairs={{0,2},{2,0},{4,6},{6,4},{8,10},{10,8},{12,14},{14,12},{16,18},{18,... | collective-permute-start | bytes 2359304 | tf_op jit(solution)/shard_map/ppermute | solution.py:227
  4.0 0.9 copy-start.3
  4.9 37.4 %collective-permute-start.12 = (bf16[1,4,64,1536]{3,2,1,0:T(8,128)(2,1)}, bf16[1,4,64,1536]{3,2,1,0:T(8,128)(2,1)S(1)}, u32[]{:S(2)}, u32[]{:S(2)}) collective-permute-start(bf16[1,4,64,1536]{3,2,1,0:T(8,128)(2,1)} %param.6), channel_id=1, source_target_pairs={{4,12},{6,14},{8,0},{10,2},{12,20},{14,22},{16,8},{18,10},{20,28},... | collective-permute-start | bytes 2359304 | tf_op jit(solution)/shard_map/ppermute | solution.py:227
  8.4 0.9 copy-start.5
  9.4 35.8 %collective-permute-start.13 = (bf16[1,4,64,1536]{3,2,1,0:T(8,128)(2,1)}, bf16[1,4,64,1536]{3,2,1,0:T(8,128)(2,1)S(1)}, u32[]{:S(2)}, u32[]{:S(2)}) collective-permute-start(bf16[1,4,64,1536]{3,2,1,0:T(8,128)(2,1)} %param.7), channel_id=1, source_target_pairs={{4,12},{6,14},{8,0},{10,2},{12,20},{14,22},{16,8},{18,10},{20,28},... | collective-permute-start | bytes 2359304 | tf_op jit(solution)/shard_map/ppermute | solution.py:227
  21.2 26.7 %collective-permute-start.10 = (bf16[1,4,64,1536]{3,2,1,0:T(8,128)(2,1)}, bf16[1,4,64,1536]{3,2,1,0:T(8,128)(2,1)S(1)}, u32[]{:S(2)}, u32[]{:S(2)}) collective-permute-start(bf16[1,4,64,1536]{3,2,1,0:T(8,128)(2,1)} %param.6), channel_id=1, source_target_pairs={{0,2},{2,0},{4,6},{6,4},{8,10},{10,8},{12,14},{14,12},{16,18},{18,... | collective-permute-start | bytes 2359304 | tf_op jit(solution)/shard_map/ppermute | solution.py:227
  37.1 22.5 %collective-permute-start = (bf16[1,4,64,1536]{3,2,1,0:T(8,128)(2,1)}, bf16[1,4,64,1536]{3,2,1,0:T(8,128)(2,1)S(1)}, u32[]{:S(2)}, u32[]{:S(2)}) collective-permute-start(bf16[1,4,64,1536]{3,2,1,0:T(8,128)(2,1)} %param.6), channel_id=1, source_target_pairs={{0,8},{2,10},{8,16},{10,18},{12,4},{14,6},{16,24},{18,26},{20,12},... | collective-permute-start | bytes 2359304 | tf_op jit(solution)/shard_map/ppermute | solution.py:227
  39.5 0.9 copy-start.7
  40.4 36.1 %collective-permute-start.6 = (bf16[1,4,64,1536]{3,2,1,0:T(8,128)(2,1)}, bf16[1,4,64,1536]{3,2,1,0:T(8,128)(2,1)S(1)}, u32[]{:S(2)}, u32[]{:S(2)}) collective-permute-start(bf16[1,4,64,1536]{3,2,1,0:T(8,128)(2,1)} %collective-permute-done.2), channel_id=1, source_target_pairs={{0,8},{2,10},{8,16},{10,18},{12,4},{14,6},{16,24},{18,26},{20,12},... | collective-permute-start | bytes 2359304 | tf_op jit(solution)/shard_map/ppermute | solution.py:227
  42.3 0.9 copy-start.9
  43.2 50.1 %collective-permute-start.8 = (bf16[1,4,64,1536]{3,2,1,0:T(8,128)(2,1)}, bf16[1,4,64,1536]{3,2,1,0:T(8,128)(2,1)S(1)}, u32[]{:S(2)}, u32[]{:S(2)}) collective-permute-start(bf16[1,4,64,1536]{3,2,1,0:T(8,128)(2,1)} %collective-permute-done.4), channel_id=1, source_target_pairs={{0,8},{2,10},{8,16},{10,18},{12,4},{14,6},{16,24},{18,26},{20,12},... | collective-permute-start | bytes 2359304 | tf_op jit(solution)/shard_map/ppermute | solution.py:227
  45.2 0.9 copy-start.11
  46.1 75.8 %collective-permute-start.1 = (bf16[1,4,64,1536]{3,2,1,0:T(8,128)(2,1)}, bf16[1,4,64,1536]{3,2,1,0:T(8,128)(2,1)S(1)}, u32[]{:S(2)}, u32[]{:S(2)}) collective-permute-start(bf16[1,4,64,1536]{3,2,1,0:T(8,128)(2,1)} %param.7), channel_id=1, source_target_pairs={{0,8},{2,10},{8,16},{10,18},{12,4},{14,6},{16,24},{18,26},{20,12},... | collective-permute-start | bytes 2359304 | tf_op jit(solution)/shard_map/ppermute | solution.py:227
  48.0 0.9 copy-start.13
  48.9 73.0 %collective-permute-start.3 = (bf16[1,4,64,1536]{3,2,1,0:T(8,128)(2,1)}, bf16[1,4,64,1536]{3,2,1,0:T(8,128)(2,1)}, u32[]{:S(2)}, u32[]{:S(2)}) collective-permute-start(bf16[1,4,64,1536]{3,2,1,0:T(8,128)(2,1)} %collective-permute-done.2), channel_id=1, source_target_pairs={{0,2},{6,4},{8,10},{14,12},{16,18},{22,20},{24,26},{30,28},{1,3},{... | collective-permute-start | bytes 2359304 | tf_op jit(solution)/shard_map/ppermute | solution.py:227
  59.6 62.2 %collective-permute-start.5 = (bf16[1,4,64,1536]{3,2,1,0:T(8,128)(2,1)}, bf16[1,4,64,1536]{3,2,1,0:T(8,128)(2,1)}, u32[]{:S(2)}, u32[]{:S(2)}) collective-permute-start(bf16[1,4,64,1536]{3,2,1,0:T(8,128)(2,1)} %collective-permute-done.4), channel_id=1, source_target_pairs={{0,2},{6,4},{8,10},{14,12},{16,18},{22,20},{24,26},{30,28},{1,3},{... | collective-permute-start | bytes 2359304 | tf_op jit(solution)/shard_map/ppermute | solution.py:227
  76.5 45.4 %collective-permute-start.7 = (bf16[1,4,64,1536]{3,2,1,0:T(8,128)(2,1)S(1)}, bf16[1,4,64,1536]{3,2,1,0:T(8,128)(2,1)}, u32[]{:S(2)}, u32[]{:S(2)}) collective-permute-start(bf16[1,4,64,1536]{3,2,1,0:T(8,128)(2,1)S(1)} %collective-permute-done.6), channel_id=1, source_target_pairs={{2,0},{4,6},{10,8},{12,14},{18,16},{20,22},{26,24},{28,30},{3,1},{... | collective-permute-start | bytes 2359304 | tf_op jit(solution)/shard_map/ppermute | solution.py:227
  93.3 28.5 %collective-permute-start.9 = (bf16[1,4,64,1536]{3,2,1,0:T(8,128)(2,1)S(1)}, bf16[1,4,64,1536]{3,2,1,0:T(8,128)(2,1)}, u32[]{:S(2)}, u32[]{:S(2)}) collective-permute-start(bf16[1,4,64,1536]{3,2,1,0:T(8,128)(2,1)S(1)} %collective-permute-done.8), channel_id=1, source_target_pairs={{2,0},{4,6},{10,8},{12,14},{18,16},{20,22},{26,24},{28,30},{3,1},{... | collective-permute-start | bytes 2359304 | tf_op jit(solution)/shard_map/ppermute | solution.py:227
  98.4 1.1 copy-start
  99.5 1.1 copy-start.1
  100.7 1.1 copy-start.2
  101.8 1.1 copy-start.4
  102.9 1.1 copy-start.6
  104.1 0.7 copy-start.15
  104.7 5.1 %copy-start.8 = (bf16[1,4,64,1536]{3,2,1,0:T(8,128)(2,1)S(1)}, bf16[1,4,64,1536]{3,2,1,0:T(8,128)(2,1)}, u32[]{:S(2)}) copy-start(bf16[1,4,64,1536]{3,2,1,0:T(8,128)(2,1)} %copy-done.7) | copy-start | bytes 2359300
  104.7 5.1 %copy-start.10 = (bf16[1,4,64,1536]{3,2,1,0:T(8,128)(2,1)S(1)}, bf16[1,4,64,1536]{3,2,1,0:T(8,128)(2,1)}, u32[]{:S(2)}) copy-start(bf16[1,4,64,1536]{3,2,1,0:T(8,128)(2,1)} %copy-done.9) | copy-start | bytes 2359300
  104.7 5.2 %copy-start.12 = (bf16[1,4,64,1536]{3,2,1,0:T(8,128)(2,1)S(1)}, bf16[1,4,64,1536]{3,2,1,0:T(8,128)(2,1)}, u32[]{:S(2)}) copy-start(bf16[1,4,64,1536]{3,2,1,0:T(8,128)(2,1)} %copy-done.11) | copy-start | bytes 2359300
  104.7 5.2 %copy-start.14 = (bf16[1,4,64,1536]{3,2,1,0:T(8,128)(2,1)S(1)}, bf16[1,4,64,1536]{3,2,1,0:T(8,128)(2,1)}, u32[]{:S(2)}) copy-start(bf16[1,4,64,1536]{3,2,1,0:T(8,128)(2,1)} %copy-done.13) | copy-start | bytes 2359300

commit v3 on v2

--- a/solution.py
+++ b/solution.py
@@ -33,8 +33,10 @@
         "y": pairs(lambda t, p: t ^ 2),
         "o": pairs(lambda t, p: t - GROUP if p < up else t + GROUP),
         "b": pairs(lambda t, p: t + GROUP if p < up else t - GROUP),
-        "g": pairs(lambda t, p: t ^ 1 if p in (0, GROUP - 1) else None),
-        "e": pairs(lambda t, p: t ^ 1 if p not in (0, GROUP - 1) else None),
+        "in_x": pairs(lambda t, p: t ^ 1 if p in (0, GROUP - 1) else None),
+        "in_y": pairs(lambda t, p: t ^ 2 if p in (0, GROUP - 1) else None),
+        "out_x": pairs(lambda t, p: t ^ 1 if p not in (0, GROUP - 1) else None),
+        "out_y": pairs(lambda t, p: t ^ 2 if p not in (0, GROUP - 1) else None),
     }
 
 
@@ -105,13 +107,14 @@
 def stage_call(q, entries, state, lists, density, final):
     tokens, features = q.shape
     heads = features // HEAD_DIM
-    kinds = [kind for kind, _, _ in entries]
+    kinds = [entry[0] for entry in entries]
+    starts = [sum(len(e) - 1 for e in entries[:i]) for i in range(len(entries) + 1)]
     halves = lists.shape[1]
     positions = lists.shape[3]
     frames = lax.axis_size("tm")
     bands = lax.axis_size("space")
     edge = tokens // halves
-    n_in = 2 * len(entries)
+    n_in = starts[-1]
 
     def kernel(lists_ref, density_ref, *refs):
         q_ref = refs[0]
@@ -156,6 +159,10 @@
         allows = [allow_of(kind) for kind in kinds if kind != "E"]
         wrap = (p == 0) | (p == GROUP - 1)
 
+        def pair_of(i, rows, cols):
+            k, *parts = [ref[rows, cols] for ref in kv[starts[i] : starts[i + 1]]]
+            return k, parts[0] if len(parts) == 1 else jnp.concatenate(parts, axis=0)
+
         def one_head(h, carry):
             cols = pl.ds(pl.multiple_of(h * HEAD_DIM, HEAD_DIM), HEAD_DIM)
             blocks = []
@@ -163,11 +170,11 @@
                 if kind == "E":
                     continue
                 rows = rows_of.get(kind, slice(None))
-                k, v = kv[2 * i][rows, cols], kv[2 * i + 1][rows, cols]
+                k, v = pair_of(i, rows, cols)
                 if kind == "GE":
-                    j = kinds.index("E")
-                    k = jnp.where(wrap, kv[2 * j][:, cols], k)
-                    v = jnp.where(wrap, kv[2 * j + 1][:, cols], v)
+                    wrap_k, wrap_v = pair_of(kinds.index("E"), rows, cols)
+                    k = jnp.where(wrap, wrap_k, k)
+                    v = jnp.where(wrap, wrap_v, v)
                 blocks.append((k, v, allows[len(blocks)]))
             old = None if state is None else [ref[h] for ref in old_refs]
             top, total, acc = flash(q_ref[:, cols], blocks, old, halves)
@@ -186,8 +193,8 @@
     vmem = pl.BlockSpec(memory_space=pltpu.VMEM)
     operands = [lists, density, q]
     keys = 0
-    for kind, k, v in entries:
-        operands += [k, v]
+    for kind, k, *v in entries:
+        operands += [k, *v]
         keys += k.shape[0] if kind != "E" else 0
     if state is not None:
         operands += list(state)
@@ -229,13 +236,17 @@
     def flat(value):
         return value.reshape(-1, features)
 
+    half = rows_dev // 2
+    values0, values1 = values[:, :half], values[:, half:]
     y_k = send(keys, route["y"])
     x_k = send(keys, route["x"])
     o_k = send(keys, route["o"])
     b_k = send(keys, route["b"])
-    y_v = send(values, route["y"])
+    y_v1 = send(values1, route["y"])
     x_v = send(values, route["x"])
-    o_v = send(values, route["o"])
+    o_v0 = send(values0, route["o"])
+    y_v0 = send(values0, route["y"])
+    o_v1 = send(values1, route["o"])
     if bands == 2:
         s_k = send(keys, up + down, "space")
         s_v = send(values, up + down, "space")
@@ -246,13 +257,17 @@
         down_k = send(keys, down, "space")
         down_v = send(values, down, "space")
         beside = [("before", flat(up_k), flat(up_v)), ("after", flat(down_k), flat(down_v))]
+
     w_k = send(y_k, route["b"])
-    g_k = send(y_k, route["g"])
-    w_v = send(y_v, route["b"])
-    e_k = send(w_k, route["e"])
-    g_v = send(y_v, route["g"])
+    g_k = send(y_k, route["in_x"])
+    w_v1 = send(y_v1, route["b"])
+    f_v0 = send(o_v0, route["in_x"])
+    w_v0 = send(o_v0, route["y"])
+    e_k = send(w_k, route["out_x"])
+    g_v = send(x_v, route["in_y"])
     b_v = send(values, route["b"])
-    e_v = send(w_v, route["e"])
+    e_v0 = send(f_v0, route["out_y"])
+    e_v1 = send(w_v1, route["out_x"])
 
     q = flat(queries)
     state = stage_call(
@@ -262,8 +277,7 @@
         q,
         [
             ("X", flat(x_k), flat(x_v)),
-            ("Y", flat(y_k), flat(y_v)),
-            ("O", flat(o_k), flat(o_v)),
+            ("Y", flat(y_k), flat(y_v0), flat(y_v1)),
         ],
         state,
         key_lists,
@@ -271,14 +285,22 @@
         False,
     )
     state = stage_call(
-        q, [("W", flat(w_k), flat(w_v))], state, key_lists, density, False
+        q,
+        [
+            ("O", flat(o_k), flat(o_v0), flat(o_v1)),
+            ("W", flat(w_k), flat(w_v0), flat(w_v1)),
+        ],
+        state,
+        key_lists,
+        density,
+        False,
     )
     result = stage_call(
         q,
         [
             ("B", flat(b_k), flat(b_v)),
             ("GE", flat(g_k), flat(g_v)),
-            ("E", flat(e_k), flat(e_v)),
+            ("E", flat(e_k), flat(e_v0), flat(e_v1)),
         ],
         state,
         key_lists,

time: 130 us -> 136 us (1.046)
  starting transfers between devices: 31.7 us -> 45.1 us
  waiting for transfers between devices: 60.4 us -> 52.1 us
    ppermute x16 -> x21, starting transfers between devices: 31.7 us -> 45.1 us  [send(): return lax.ppermute(value, axis, pairs)]
    ppermute x16 -> x21, waiting for transfers between devices: 60.4 us -> 52.1 us  [send(): return lax.ppermute(value, axis, pairs)]
    unnamed x33 -> x47, local copies, waits for them, and re-layouts: 12.5 us -> 10.9 us
  transfers between devices with their start and end apart: 16 -> 21, of which waited for: 5 -> 8; matrix products, arithmetic and copies ran while one was open for 1% -> 0% of each run, Pallas kernels for 13% -> 13%
where the time goes in v3:
time: 136 us; the launch traced here: 135 us
  waiting for transfers between devices  52.1 us (38%)
  starting transfers between devices  45.1 us (33%)
  Pallas kernels  25.4 us (19%)
  local copies, waits for them, and re-layouts  12.2 us (9%)
    ppermute x21, waiting for transfers between devices, send(): return lax.ppermute(value, axis, pairs)  52.1 us
    ppermute x21, starting transfers between devices, send(): return lax.ppermute(value, axis, pairs)  45.1 us
    pallas_call x4, Pallas kernels, stage_call(): pl.pallas_call(kernel, in_specs=specs, out_specs=out_specs, out_shape=out...  25.4 us
    unnamed x47, local copies, waits for them, and re-layouts  10.9 us
  transfers between devices with their start and end apart: 21, of which 8 were waited for; matrix products, arithmetic and copies ran while one was open for 0% of the time, Pallas kernels for 13%

profile of v3, /device:TPU:12, one launch (start us, length us, event | category | flops | bytes accessed | tf_op | source)
XLA Modules:
  0.0 135.0 jit_solution(15804367893591911129)
XLA Ops:
  0.0 1.3 fusion
  1.9 1.5 %collective-permute-start.18 = (bf16[1,2,64,1536]{3,2,1,0:T(8,128)(2,1)S(1)}, bf16[1,2,64,1536]{3,2,1,0:T(8,128)(2,1)S(1)}, u32[]{:S(2)}, u32[]{:S(2)}) collective-permute-start(bf16[1,2,64,1536]{3,2,1,0:T(8,128)(2,1)S(1)} %get-tuple-element.24), channel_id=1, source_target_pairs={{0,4},{2,6},{4,0},{6,2},{8,12},{10,14},{12,8},{14,10},{16,20},{18,... | collective-permute-start | bytes 1179656 | tf_op jit(solution)/shard_map/ppermute | solution.py:234
  3.4 3.5 %collective-permute-start.8 = (bf16[1,2,64,1536]{3,2,1,0:T(8,128)(2,1)S(1)}, bf16[1,2,64,1536]{3,2,1,0:T(8,128)(2,1)S(1)}, u32[]{:S(2)}, u32[]{:S(2)}) collective-permute-start(bf16[1,2,64,1536]{3,2,1,0:T(8,128)(2,1)S(1)} %get-tuple-element.24), channel_id=1, source_target_pairs={{4,12},{6,14},{8,0},{10,2},{12,20},{14,22},{16,8},{18,10},{20,28},... | collective-permute-start | bytes 1179656 | tf_op jit(solution)/shard_map/ppermute | solution.py:234
  6.9 3.5 %collective-permute-start.15 = (bf16[1,2,64,1536]{3,2,1,0:T(8,128)(2,1)S(1)}, bf16[1,2,64,1536]{3,2,1,0:T(8,128)(2,1)S(1)}, u32[]{:S(2)}, u32[]{:S(2)}) collective-permute-start(bf16[1,2,64,1536]{3,2,1,0:T(8,128)(2,1)S(1)} %get-tuple-element.23), channel_id=1, source_target_pairs={{4,12},{6,14},{8,0},{10,2},{12,20},{14,22},{16,8},{18,10},{20,28},... | collective-permute-start | bytes 1179656 | tf_op jit(solution)/shard_map/ppermute | solution.py:234
  10.5 2.9 %collective-permute-done.11 = bf16[1,2,64,1536]{3,2,1,0:T(8,128)(2,1)S(1)} collective-permute-done((bf16[1,2,64,1536]{3,2,1,0:T(8,128)(2,1)S(1)}, bf16[1,2,64,1536]{3,2,1,0:T(8,128)(2,1)S(1)}, u32[]{:S(2)}, u32[]{:S(2)}) %collective-permute-start.11) | collective-permute-done | bytes 393248 | tf_op jit(solution)/shard_map/ppermute | solution.py:234
  13.4 7.3 %collective-permute-done.18 = bf16[1,2,64,1536]{3,2,1,0:T(8,128)(2,1)S(1)} collective-permute-done((bf16[1,2,64,1536]{3,2,1,0:T(8,128)(2,1)S(1)}, bf16[1,2,64,1536]{3,2,1,0:T(8,128)(2,1)S(1)}, u32[]{:S(2)}, u32[]{:S(2)}) %collective-permute-start.18) | collective-permute-done | bytes 393248 | tf_op jit(solution)/shard_map/ppermute | solution.py:234
  21.9 1.5 %collective-permute-start.4 = (bf16[1,4,64,1536]{3,2,1,0:T(8,128)(2,1)S(1)}, bf16[1,4,64,1536]{3,2,1,0:T(8,128)(2,1)}, u32[]{:S(2)}, u32[]{:S(2)}) collective-permute-start(bf16[1,4,64,1536]{3,2,1,0:T(8,128)(2,1)S(1)} %copy-done.1), channel_id=1, source_target_pairs={{0,2},{2,0},{4,6},{6,4},{8,10},{10,8},{12,14},{14,12},{16,18},{18,... | collective-permute-start | bytes 2359304 | tf_op jit(solution)/shard_map/ppermute | solution.py:234
  24.8 1.5 %collective-permute-start.17 = (bf16[1,4,64,1536]{3,2,1,0:T(8,128)(2,1)}, bf16[1,4,64,1536]{3,2,1,0:T(8,128)(2,1)S(1)}, u32[]{:S(2)}, u32[]{:S(2)}) collective-permute-start(bf16[1,4,64,1536]{3,2,1,0:T(8,128)(2,1)} %param.6), channel_id=1, source_target_pairs={{0,2},{2,0},{4,6},{6,4},{8,10},{10,8},{12,14},{14,12},{16,18},{18,... | collective-permute-start | bytes 2359304 | tf_op jit(solution)/shard_map/ppermute | solution.py:234
  26.3 0.9 copy-done.3
  27.2 3.5 %collective-permute-start.14 = (bf16[1,4,64,1536]{3,2,1,0:T(8,128)(2,1)}, bf16[1,4,64,1536]{3,2,1,0:T(8,128)(2,1)S(1)}, u32[]{:S(2)}, u32[]{:S(2)}) collective-permute-start(bf16[1,4,64,1536]{3,2,1,0:T(8,128)(2,1)} %param.6), channel_id=1, source_target_pairs={{4,12},{6,14},{8,0},{10,2},{12,20},{14,22},{16,8},{18,10},{20,28},... | collective-permute-start | bytes 2359304 | tf_op jit(solution)/shard_map/ppermute | solution.py:234
  31.6 10.5 %collective-permute-done.2 = bf16[1,4,64,1536]{3,2,1,0:T(8,128)(2,1)} collective-permute-done((bf16[1,4,64,1536]{3,2,1,0:T(8,128)(2,1)}, bf16[1,4,64,1536]{3,2,1,0:T(8,128)(2,1)}, u32[]{:S(2)}, u32[]{:S(2)}) %collective-permute-start.2) | collective-permute-done | bytes 786464 | tf_op jit(solution)/shard_map/ppermute | solution.py:234
  42.1 2.3 %collective-permute-start.12 = (bf16[1,2,64,1536]{3,2,1,0:T(8,128)(2,1)S(1)}, bf16[1,2,64,1536]{3,2,1,0:T(8,128)(2,1)}, u32[]{:S(2)}, u32[]{:S(2)}) collective-permute-start(bf16[1,2,64,1536]{3,2,1,0:T(8,128)(2,1)S(1)} %collective-permute-done.11), channel_id=1, source_target_pairs={{0,8},{2,10},{8,16},{10,18},{12,4},{14,6},{16,24},{18,26},{20,12},... | collective-permute-start | bytes 1179656 | tf_op jit(solution)/shard_map/ppermute | solution.py:234
  45.2 1.9 %collective-permute-start.6 = (bf16[1,4,64,1536]{3,2,1,0:T(8,128)(2,1)}, bf16[1,4,64,1536]{3,2,1,0:T(8,128)(2,1)}, u32[]{:S(2)}, u32[]{:S(2)}) collective-permute-start(bf16[1,4,64,1536]{3,2,1,0:T(8,128)(2,1)} %collective-permute-done.2), channel_id=1, source_target_pairs={{0,8},{2,10},{8,16},{10,18},{12,4},{14,6},{16,24},{18,26},{20,12},... | collective-permute-start | bytes 2359304 | tf_op jit(solution)/shard_map/ppermute | solution.py:234
  47.1 9.8 %collective-permute-done.17 = bf16[1,4,64,1536]{3,2,1,0:T(8,128)(2,1)S(1)} collective-permute-done((bf16[1,4,64,1536]{3,2,1,0:T(8,128)(2,1)}, bf16[1,4,64,1536]{3,2,1,0:T(8,128)(2,1)S(1)}, u32[]{:S(2)}, u32[]{:S(2)}) %collective-permute-start.17) | collective-permute-done | bytes 786464 | tf_op jit(solution)/shard_map/ppermute | solution.py:234
  57.8 2.4 %collective-permute-start = (bf16[1,4,64,1536]{3,2,1,0:T(8,128)(2,1)}, bf16[1,4,64,1536]{3,2,1,0:T(8,128)(2,1)S(1)}, u32[]{:S(2)}, u32[]{:S(2)}) collective-permute-start(bf16[1,4,64,1536]{3,2,1,0:T(8,128)(2,1)} %param.6), channel_id=1, source_target_pairs={{0,8},{2,10},{8,16},{10,18},{12,4},{14,6},{16,24},{18,26},{20,12},... | collective-permute-start | bytes 2359304 | tf_op jit(solution)/shard_map/ppermute | solution.py:234
  61.0 1.9 %collective-permute-start.1 = (bf16[1,4,64,1536]{3,2,1,0:T(8,128)(2,1)S(1)}, bf16[1,4,64,1536]{3,2,1,0:T(8,128)(2,1)S(1)}, u32[]{:S(2)}, u32[]{:S(2)}) collective-permute-start(bf16[1,4,64,1536]{3,2,1,0:T(8,128)(2,1)S(1)} %copy-done.1), channel_id=1, source_target_pairs={{0,8},{2,10},{8,16},{10,18},{12,4},{14,6},{16,24},{18,26},{20,12},... | collective-permute-start | bytes 2359304 | tf_op jit(solution)/shard_map/ppermute | solution.py:234
  62.9 1.3 collective-permute-start.9
  65.9 1.3 collective-permute-start.3
  67.1 9.7 %collective-permute-done.9 = bf16[1,2,64,1536]{3,2,1,0:T(8,128)(2,1)} collective-permute-done((bf16[1,2,64,1536]{3,2,1,0:T(8,128)(2,1)S(1)}, bf16[1,2,64,1536]{3,2,1,0:T(8,128)(2,1)}, u32[]{:S(2)}, u32[]{:S(2)}) %collective-permute-start.9) | collective-permute-done | bytes 393248 | tf_op jit(solution)/shard_map/ppermute | solution.py:234
  76.9 1.3 collective-permute-start.5
  78.2 9.9 %collective-permute-start.7 = (bf16[1,4,64,1536]{3,2,1,0:T(8,128)(2,1)}, bf16[1,4,64,1536]{3,2,1,0:T(8,128)(2,1)}, u32[]{:S(2)}, u32[]{:S(2)}) collective-permute-start(bf16[1,4,64,1536]{3,2,1,0:T(8,128)(2,1)} %collective-permute-done.6), channel_id=1, source_target_pairs={{2,0},{4,6},{10,8},{12,14},{18,16},{20,22},{26,24},{28,30},{3,1},{... | collective-permute-start | bytes 2359304 | tf_op jit(solution)/shard_map/ppermute | solution.py:234
  88.1 1.6 %collective-permute-done = bf16[1,4,64,1536]{3,2,1,0:T(8,128)(2,1)S(1)} collective-permute-done((bf16[1,4,64,1536]{3,2,1,0:T(8,128)(2,1)}, bf16[1,4,64,1536]{3,2,1,0:T(8,128)(2,1)S(1)}, u32[]{:S(2)}, u32[]{:S(2)}) %collective-permute-start) | collective-permute-done | bytes 786464 | tf_op jit(solution)/shard_map/ppermute | solution.py:234
  89.7 2.4 %collective-permute-start.10 = (bf16[1,2,64,1536]{3,2,1,0:T(8,128)(2,1)}, bf16[1,2,64,1536]{3,2,1,0:T(8,128)(2,1)S(1)}, u32[]{:S(2)}, u32[]{:S(2)}) collective-permute-start(bf16[1,2,64,1536]{3,2,1,0:T(8,128)(2,1)} %collective-permute-done.9), channel_id=1, source_target_pairs={{2,6},{4,0},{10,14},{12,8},{18,22},{20,16},{26,30},{28,24},{3,7},{... | collective-permute-start | bytes 1179656 | tf_op jit(solution)/shard_map/ppermute | solution.py:234
  92.1 9.6 %collective-permute-done.1 = bf16[1,4,64,1536]{3,2,1,0:T(8,128)(2,1)S(1)} collective-permute-done((bf16[1,4,64,1536]{3,2,1,0:T(8,128)(2,1)S(1)}, bf16[1,4,64,1536]{3,2,1,0:T(8,128)(2,1)S(1)}, u32[]{:S(2)}, u32[]{:S(2)}) %collective-permute-start.1) | collective-permute-done | bytes 786464 | tf_op jit(solution)/shard_map/ppermute | solution.py:234
  101.7 4.2 %collective-permute-start.13 = (bf16[1,2,64,1536]{3,2,1,0:T(8,128)(2,1)}, bf16[1,2,64,1536]{3,2,1,0:T(8,128)(2,1)}, u32[]{:S(2)}, u32[]{:S(2)}) collective-permute-start(bf16[1,2,64,1536]{3,2,1,0:T(8,128)(2,1)} %collective-permute-done.12), channel_id=1, source_target_pairs={{2,0},{4,6},{10,8},{12,14},{18,16},{20,22},{26,24},{28,30},{3,1},{... | collective-permute-start | bytes 1179656 | tf_op jit(solution)/shard_map/ppermute | solution.py:234
  106.0 1.1 copy-done.2
  107.2 1.1 copy-done.4
  108.3 1.1 copy-done.6
  109.4 5.1 %shard_map.55 = (f32[12,8,256]{2,1,0:T(8,128)S(1)}, f32[12,8,256]{2,1,0:T(8,128)S(1)}, f32[12,128,256]{2,1,0:T(8,128)S(1)}) custom-call(s32[1,2,6,2]{3,2,1,0:T(8,128)S(1)} %copy.9.lists_ref, s32[1,3]{1,0:T(1,128)S(1)} %copy-done.21, bf16[256,1536]{1,0:T(8,128)(2,1)S(1)} %bitcast.24, bf16[256,1536]{1,0:T(8,128)(2,1)S(1)} %bitcast.31, ...), custom_call_target="tpu_custom_call" | custom-call | flops 805306368 | bytes 6291456 | tf_op jit(solution)/shard_map/pallas_call | solution.py:211
  114.6 6.4 %shard_map.56 = (f32[12,8,256]{2,1,0:T(8,128)S(1)}, f32[12,8,256]{2,1,0:T(8,128)S(1)}, f32[12,128,256]{2,1,0:T(8,128)S(1)}) custom-call(s32[1,2,6,2]{3,2,1,0:T(8,128)S(1)} %copy.9.lists_ref, s32[1,3]{1,0:T(1,128)S(1)} %copy-done.21, bf16[256,1536]{1,0:T(8,128)(2,1)S(1)} %bitcast.25, bf16[256,1536]{1,0:T(8,128)(2,1)S(1)} %bitcast.35, ...), custom_call_target="tpu_custom_call" | custom-call | flops 805306368 | bytes 6291456 | tf_op jit(solution)/shard_map/pallas_call | solution.py:211
  121.1 6.2 %shard_map.57 = (f32[12,8,256]{2,1,0:T(8,128)S(1)}, f32[12,8,256]{2,1,0:T(8,128)S(1)}, f32[12,128,256]{2,1,0:T(8,128)S(1)}) custom-call(s32[1,2,6,2]{3,2,1,0:T(8,128)S(1)} %copy.9.lists_ref, s32[1,3]{1,0:T(1,128)S(1)} %copy-done.21, bf16[256,1536]{1,0:T(8,128)(2,1)S(1)} %bitcast.26, bf16[256,1536]{1,0:T(8,128)(2,1)S(1)} %bitcast.34, ...), custom_call_target="tpu_custom_call" | custom-call | flops 805306368 | bytes 6291456 | tf_op jit(solution)/shard_map/pallas_call | solution.py:211
  127.3 7.7 %shard_map.58 = bf16[256,1536]{1,0:T(8,128)(2,1)} custom-call(s32[1,2,6,2]{3,2,1,0:T(8,128)S(1)} %copy.9.lists_ref, s32[1,3]{1,0:T(1,128)S(1)} %copy-done.21, bf16[256,1536]{1,0:T(8,128)(2,1)S(1)} %bitcast.27, bf16[256,1536]{1,0:T(8,128)(2,1)S(1)} %bitcast.29, bf16[256,1536]{1,0:T(8,128)(2,1)S(1)} %bitcast.30, bf16[256,1536]{1,0:T(8,128)(2,1)} %bitcast.3.refs_3_, ...), custom_call_target="tpu_custom_call" | custom-call | flops 805306368 | bytes 6291456 | tf_op jit(solution)/shard_map/pallas_call | solution.py:211
  (62 shorter events, 8.3 us)
Async XLA Ops:
  0.0 13.4 %copy-start.1 = (bf16[1,4,64,1536]{3,2,1,0:T(8,128)(2,1)S(1)}, bf16[1,4,64,1536]{3,2,1,0:T(8,128)(2,1)}, u32[]{:S(2)}) copy-start(bf16[1,4,64,1536]{3,2,1,0:T(8,128)(2,1)} %param.7) | copy-start | bytes 2359300
  0.0 105.9 %copy-start.22 = (s32[1,2,6,2]{2,3,1,0:T(2,128)S(1)}, s32[1,2,6,2]{2,3,1,0:T(2,128)}, u32[]{:S(2)}) copy-start(s32[1,2,6,2]{2,3,1,0:T(2,128)} %param.8) | copy-start | bytes 292
  0.0 106.0 %copy-start = (bf16[1,4,64,1536]{3,2,1,0:T(8,128)(2,1)S(1)}, bf16[1,4,64,1536]{3,2,1,0:T(8,128)(2,1)}, u32[]{:S(2)}) copy-start(bf16[1,4,64,1536]{3,2,1,0:T(8,128)(2,1)} %param.5) | copy-start | bytes 2359300
  0.0 106.0 %copy-start.21 = (s32[1,3]{1,0:T(1,128)S(1)}, s32[1,3]{1,0:T(1,128)}, u32[]{:S(2)}) copy-start(s32[1,3]{1,0:T(1,128)} %density_ref.7) | copy-start | bytes 40
  1.3 12.1 %collective-permute-start.11 = (bf16[1,2,64,1536]{3,2,1,0:T(8,128)(2,1)S(1)}, bf16[1,2,64,1536]{3,2,1,0:T(8,128)(2,1)S(1)}, u32[]{:S(2)}, u32[]{:S(2)}) collective-permute-start(bf16[1,2,64,1536]{3,2,1,0:T(8,128)(2,1)S(1)} %get-tuple-element.23), channel_id=1, source_target_pairs={{0,4},{2,6},{4,0},{6,2},{8,12},{10,14},{12,8},{14,10},{16,20},{18,... | collective-permute-start | bytes 1179656 | tf_op jit(solution)/shard_map/ppermute | solution.py:234
  1.9 18.8 %collective-permute-start.18 = (bf16[1,2,64,1536]{3,2,1,0:T(8,128)(2,1)S(1)}, bf16[1,2,64,1536]{3,2,1,0:T(8,128)(2,1)S(1)}, u32[]{:S(2)}, u32[]{:S(2)}) collective-permute-start(bf16[1,2,64,1536]{3,2,1,0:T(8,128)(2,1)S(1)} %get-tuple-element.24), channel_id=1, source_target_pairs={{0,4},{2,6},{4,0},{6,2},{8,12},{10,14},{12,8},{14,10},{16,20},{18,... | collective-permute-start | bytes 1179656 | tf_op jit(solution)/shard_map/ppermute | solution.py:234
  3.4 18.5 %collective-permute-start.8 = (bf16[1,2,64,1536]{3,2,1,0:T(8,128)(2,1)S(1)}, bf16[1,2,64,1536]{3,2,1,0:T(8,128)(2,1)S(1)}, u32[]{:S(2)}, u32[]{:S(2)}) collective-permute-start(bf16[1,2,64,1536]{3,2,1,0:T(8,128)(2,1)S(1)} %get-tuple-element.24), channel_id=1, source_target_pairs={{4,12},{6,14},{8,0},{10,2},{12,20},{14,22},{16,8},{18,10},{20,28},... | collective-permute-start | bytes 1179656 | tf_op jit(solution)/shard_map/ppermute | solution.py:234
  6.9 17.1 %collective-permute-start.15 = (bf16[1,2,64,1536]{3,2,1,0:T(8,128)(2,1)S(1)}, bf16[1,2,64,1536]{3,2,1,0:T(8,128)(2,1)S(1)}, u32[]{:S(2)}, u32[]{:S(2)}) collective-permute-start(bf16[1,2,64,1536]{3,2,1,0:T(8,128)(2,1)S(1)} %get-tuple-element.23), channel_id=1, source_target_pairs={{4,12},{6,14},{8,0},{10,2},{12,20},{14,22},{16,8},{18,10},{20,28},... | collective-permute-start | bytes 1179656 | tf_op jit(solution)/shard_map/ppermute | solution.py:234
  10.4 15.9 %collective-permute-start.19 = (bf16[1,4,64,1536]{3,2,1,0:T(8,128)(2,1)}, bf16[1,4,64,1536]{3,2,1,0:T(8,128)(2,1)S(1)}, u32[]{:S(2)}, u32[]{:S(2)}) collective-permute-start(bf16[1,4,64,1536]{3,2,1,0:T(8,128)(2,1)} %param.6), channel_id=1, source_target_pairs={{0,1},{1,0},{2,3},{3,2},{4,5},{5,4},{6,7},{7,6},{8,9},{9,8},{10,11... | collective-permute-start | bytes 2359304 | tf_op jit(solution)/shard_map/ppermute | solution.py:234
  13.4 17.3 %collective-permute-start.20 = (bf16[1,4,64,1536]{3,2,1,0:T(8,128)(2,1)S(1)}, bf16[1,4,64,1536]{3,2,1,0:T(8,128)(2,1)S(1)}, u32[]{:S(2)}, u32[]{:S(2)}) collective-permute-start(bf16[1,4,64,1536]{3,2,1,0:T(8,128)(2,1)S(1)} %copy-done.1), channel_id=1, source_target_pairs={{0,1},{1,0},{2,3},{3,2},{4,5},{5,4},{6,7},{7,6},{8,9},{9,8},{10,11... | collective-permute-start | bytes 2359304 | tf_op jit(solution)/shard_map/ppermute | solution.py:234
  21.4 20.7 %collective-permute-start.2 = (bf16[1,4,64,1536]{3,2,1,0:T(8,128)(2,1)}, bf16[1,4,64,1536]{3,2,1,0:T(8,128)(2,1)}, u32[]{:S(2)}, u32[]{:S(2)}) collective-permute-start(bf16[1,4,64,1536]{3,2,1,0:T(8,128)(2,1)} %param.6), channel_id=1, source_target_pairs={{0,4},{2,6},{4,0},{6,2},{8,12},{10,14},{12,8},{14,10},{16,20},{18,... | collective-permute-start | bytes 2359304 | tf_op jit(solution)/shard_map/ppermute | solution.py:234
  21.9 23.3 %collective-permute-start.4 = (bf16[1,4,64,1536]{3,2,1,0:T(8,128)(2,1)S(1)}, bf16[1,4,64,1536]{3,2,1,0:T(8,128)(2,1)}, u32[]{:S(2)}, u32[]{:S(2)}) collective-permute-start(bf16[1,4,64,1536]{3,2,1,0:T(8,128)(2,1)S(1)} %copy-done.1), channel_id=1, source_target_pairs={{0,2},{2,0},{4,6},{6,4},{8,10},{10,8},{12,14},{14,12},{16,18},{18,... | collective-permute-start | bytes 2359304 | tf_op jit(solution)/shard_map/ppermute | solution.py:234
  24.8 32.1 %collective-permute-start.17 = (bf16[1,4,64,1536]{3,2,1,0:T(8,128)(2,1)}, bf16[1,4,64,1536]{3,2,1,0:T(8,128)(2,1)S(1)}, u32[]{:S(2)}, u32[]{:S(2)}) collective-permute-start(bf16[1,4,64,1536]{3,2,1,0:T(8,128)(2,1)} %param.6), channel_id=1, source_target_pairs={{0,2},{2,0},{4,6},{6,4},{8,10},{10,8},{12,14},{14,12},{16,18},{18,... | collective-permute-start | bytes 2359304 | tf_op jit(solution)/shard_map/ppermute | solution.py:234
  27.2 37.8 %collective-permute-start.14 = (bf16[1,4,64,1536]{3,2,1,0:T(8,128)(2,1)}, bf16[1,4,64,1536]{3,2,1,0:T(8,128)(2,1)S(1)}, u32[]{:S(2)}, u32[]{:S(2)}) collective-permute-start(bf16[1,4,64,1536]{3,2,1,0:T(8,128)(2,1)} %param.6), channel_id=1, source_target_pairs={{4,12},{6,14},{8,0},{10,2},{12,20},{14,22},{16,8},{18,10},{20,28},... | collective-permute-start | bytes 2359304 | tf_op jit(solution)/shard_map/ppermute | solution.py:234
  31.6 28.6 %collective-permute-start.16 = (bf16[1,2,64,1536]{3,2,1,0:T(8,128)(2,1)S(1)}, bf16[1,2,64,1536]{3,2,1,0:T(8,128)(2,1)S(1)}, u32[]{:S(2)}, u32[]{:S(2)}) collective-permute-start(bf16[1,2,64,1536]{3,2,1,0:T(8,128)(2,1)S(1)} %collective-permute-done.8), channel_id=1, source_target_pairs={{0,4},{2,6},{4,0},{6,2},{8,12},{10,14},{12,8},{14,10},{16,20},{18,... | collective-permute-start | bytes 1179656 | tf_op jit(solution)/shard_map/ppermute | solution.py:234
  42.1 20.8 %collective-permute-start.12 = (bf16[1,2,64,1536]{3,2,1,0:T(8,128)(2,1)S(1)}, bf16[1,2,64,1536]{3,2,1,0:T(8,128)(2,1)}, u32[]{:S(2)}, u32[]{:S(2)}) collective-permute-start(bf16[1,2,64,1536]{3,2,1,0:T(8,128)(2,1)S(1)} %collective-permute-done.11), channel_id=1, source_target_pairs={{0,8},{2,10},{8,16},{10,18},{12,4},{14,6},{16,24},{18,26},{20,12},... | collective-permute-start | bytes 1179656 | tf_op jit(solution)/shard_map/ppermute | solution.py:234
  45.2 32.9 %collective-permute-start.6 = (bf16[1,4,64,1536]{3,2,1,0:T(8,128)(2,1)}, bf16[1,4,64,1536]{3,2,1,0:T(8,128)(2,1)}, u32[]{:S(2)}, u32[]{:S(2)}) collective-permute-start(bf16[1,4,64,1536]{3,2,1,0:T(8,128)(2,1)} %collective-permute-done.2), channel_id=1, source_target_pairs={{0,8},{2,10},{8,16},{10,18},{12,4},{14,6},{16,24},{18,26},{20,12},... | collective-permute-start | bytes 2359304 | tf_op jit(solution)/shard_map/ppermute | solution.py:234
  57.8 31.9 %collective-permute-start = (bf16[1,4,64,1536]{3,2,1,0:T(8,128)(2,1)}, bf16[1,4,64,1536]{3,2,1,0:T(8,128)(2,1)S(1)}, u32[]{:S(2)}, u32[]{:S(2)}) collective-permute-start(bf16[1,4,64,1536]{3,2,1,0:T(8,128)(2,1)} %param.6), channel_id=1, source_target_pairs={{0,8},{2,10},{8,16},{10,18},{12,4},{14,6},{16,24},{18,26},{20,12},... | collective-permute-start | bytes 2359304 | tf_op jit(solution)/shard_map/ppermute | solution.py:234
  61.0 40.8 %collective-permute-start.1 = (bf16[1,4,64,1536]{3,2,1,0:T(8,128)(2,1)S(1)}, bf16[1,4,64,1536]{3,2,1,0:T(8,128)(2,1)S(1)}, u32[]{:S(2)}, u32[]{:S(2)}) collective-permute-start(bf16[1,4,64,1536]{3,2,1,0:T(8,128)(2,1)S(1)} %copy-done.1), channel_id=1, source_target_pairs={{0,8},{2,10},{8,16},{10,18},{12,4},{14,6},{16,24},{18,26},{20,12},... | collective-permute-start | bytes 2359304 | tf_op jit(solution)/shard_map/ppermute | solution.py:234
  62.9 14.0 %collective-permute-start.9 = (bf16[1,2,64,1536]{3,2,1,0:T(8,128)(2,1)S(1)}, bf16[1,2,64,1536]{3,2,1,0:T(8,128)(2,1)}, u32[]{:S(2)}, u32[]{:S(2)}) collective-permute-start(bf16[1,2,64,1536]{3,2,1,0:T(8,128)(2,1)S(1)} %collective-permute-done.8), channel_id=1, source_target_pairs={{0,2},{6,4},{8,10},{14,12},{16,18},{22,20},{24,26},{30,28},{1,3},{... | collective-permute-start | bytes 1179656 | tf_op jit(solution)/shard_map/ppermute | solution.py:234
  65.9 61.4 %collective-permute-start.3 = (bf16[1,4,64,1536]{3,2,1,0:T(8,128)(2,1)}, bf16[1,4,64,1536]{3,2,1,0:T(8,128)(2,1)}, u32[]{:S(2)}, u32[]{:S(2)}) collective-permute-start(bf16[1,4,64,1536]{3,2,1,0:T(8,128)(2,1)} %collective-permute-done.2), channel_id=1, source_target_pairs={{0,2},{6,4},{8,10},{14,12},{16,18},{22,20},{24,26},{30,28},{1,3},{... | collective-permute-start | bytes 2359304 | tf_op jit(solution)/shard_map/ppermute | solution.py:234
  76.9 50.4 %collective-permute-start.5 = (bf16[1,4,64,1536]{3,2,1,0:T(8,128)(2,1)}, bf16[1,4,64,1536]{3,2,1,0:T(8,128)(2,1)}, u32[]{:S(2)}, u32[]{:S(2)}) collective-permute-start(bf16[1,4,64,1536]{3,2,1,0:T(8,128)(2,1)} %collective-permute-done.4), channel_id=1, source_target_pairs={{0,4},{6,2},{8,12},{14,10},{16,20},{22,18},{24,28},{30,26},{1,5},{... | collective-permute-start | bytes 2359304 | tf_op jit(solution)/shard_map/ppermute | solution.py:234
  78.2 49.1 %collective-permute-start.7 = (bf16[1,4,64,1536]{3,2,1,0:T(8,128)(2,1)}, bf16[1,4,64,1536]{3,2,1,0:T(8,128)(2,1)}, u32[]{:S(2)}, u32[]{:S(2)}) collective-permute-start(bf16[1,4,64,1536]{3,2,1,0:T(8,128)(2,1)} %collective-permute-done.6), channel_id=1, source_target_pairs={{2,0},{4,6},{10,8},{12,14},{18,16},{20,22},{26,24},{28,30},{3,1},{... | collective-permute-start | bytes 2359304 | tf_op jit(solution)/shard_map/ppermute | solution.py:234
  89.7 37.6 %collective-permute-start.10 = (bf16[1,2,64,1536]{3,2,1,0:T(8,128)(2,1)}, bf16[1,2,64,1536]{3,2,1,0:T(8,128)(2,1)S(1)}, u32[]{:S(2)}, u32[]{:S(2)}) collective-permute-start(bf16[1,2,64,1536]{3,2,1,0:T(8,128)(2,1)} %collective-permute-done.9), channel_id=1, source_target_pairs={{2,6},{4,0},{10,14},{12,8},{18,22},{20,16},{26,30},{28,24},{3,7},{... | collective-permute-start | bytes 1179656 | tf_op jit(solution)/shard_map/ppermute | solution.py:234
  101.7 25.5 %collective-permute-start.13 = (bf16[1,2,64,1536]{3,2,1,0:T(8,128)(2,1)}, bf16[1,2,64,1536]{3,2,1,0:T(8,128)(2,1)}, u32[]{:S(2)}, u32[]{:S(2)}) collective-permute-start(bf16[1,2,64,1536]{3,2,1,0:T(8,128)(2,1)} %collective-permute-done.12), channel_id=1, source_target_pairs={{2,0},{4,6},{10,8},{12,14},{18,16},{20,22},{26,24},{28,30},{3,1},{... | collective-permute-start | bytes 1179656 | tf_op jit(solution)/shard_map/ppermute | solution.py:234
  109.4 5.1 %copy-start.10 = (bf16[1,4,64,1536]{3,2,1,0:T(8,128)(2,1)S(1)}, bf16[1,4,64,1536]{3,2,1,0:T(8,128)(2,1)}, u32[]{:S(2)}) copy-start(bf16[1,4,64,1536]{3,2,1,0:T(8,128)(2,1)} %copy-done.9) | copy-start | bytes 2359300
  109.4 5.1 %copy-start.14 = (bf16[1,2,64,1536]{3,2,1,0:T(8,128)(2,1)S(1)}, bf16[1,2,64,1536]{3,2,1,0:T(8,128)(2,1)}, u32[]{:S(2)}) copy-start(bf16[1,2,64,1536]{3,2,1,0:T(8,128)(2,1)} %copy-done.13) | copy-start | bytes 1179652
  109.4 5.2 %copy-start.18 = (bf16[1,2,64,1536]{3,2,1,0:T(8,128)(2,1)S(1)}, bf16[1,2,64,1536]{3,2,1,0:T(8,128)(2,1)}, u32[]{:S(2)}) copy-start(bf16[1,2,64,1536]{3,2,1,0:T(8,128)(2,1)} %copy-done.17) | copy-start | bytes 1179652
  114.6 6.5 %copy-start.8 = (bf16[1,4,64,1536]{3,2,1,0:T(8,128)(2,1)S(1)}, bf16[1,4,64,1536]{3,2,1,0:T(8,128)(2,1)}, u32[]{:S(2)}) copy-start(bf16[1,4,64,1536]{3,2,1,0:T(8,128)(2,1)} %copy-done.7) | copy-start | bytes 2359300
  114.6 6.5 %copy-start.12 = (bf16[1,2,64,1536]{3,2,1,0:T(8,128)(2,1)S(1)}, bf16[1,2,64,1536]{3,2,1,0:T(8,128)(2,1)}, u32[]{:S(2)}) copy-start(bf16[1,2,64,1536]{3,2,1,0:T(8,128)(2,1)} %copy-done.11) | copy-start | bytes 1179652
  114.6 6.5 %copy-start.16 = (bf16[1,2,64,1536]{3,2,1,0:T(8,128)(2,1)S(1)}, bf16[1,2,64,1536]{3,2,1,0:T(8,128)(2,1)}, u32[]{:S(2)}) copy-start(bf16[1,2,64,1536]{3,2,1,0:T(8,128)(2,1)} %copy-done.15) | copy-start | bytes 1179652
  114.6 6.5 %copy-start.20 = (bf16[1,2,64,1536]{3,2,1,0:T(8,128)(2,1)S(1)}, bf16[1,2,64,1536]{3,2,1,0:T(8,128)(2,1)}, u32[]{:S(2)}) copy-start(bf16[1,2,64,1536]{3,2,1,0:T(8,128)(2,1)} %copy-done.19) | copy-start | bytes 1179652
  (12 other events, 10.8 us)

commit v4 on v3

v4 whole, which is shorter than its diff:
```python
import math

import jax
import jax.numpy as jnp
from jax import lax
from jax.experimental import pallas as pl
from jax.experimental.pallas import tpu as pltpu
from jax.sharding import PartitionSpec as P


HEAD_DIM = 128
OFFSETS = 3
GROUP = 2 ** (OFFSETS - 1)
SUBLANES = 8
UNROLL = 2
VMEM_LIMIT = 16 * 2**20
NEG = -1e30
SCALE2 = math.log2(math.e) / math.sqrt(HEAD_DIM)


def routes(count):
    def pairs(target):
        out = []
        for t in range(count):
            to = target(t, t % GROUP)
            if to is not None and 0 <= to < count:
                out.append((t, to))
        return out

    up = GROUP // 2
    return {
        "x": pairs(lambda t, p: t ^ 1),
        "y": pairs(lambda t, p: t ^ 2),
        "o": pairs(lambda t, p: t - GROUP if p < up else t + GROUP),
        "b": pairs(lambda t, p: t + GROUP if p < up else t - GROUP),
        "in_x": pairs(lambda t, p: t ^ 1 if p in (0, GROUP - 1) else None),
        "in_y": pairs(lambda t, p: t ^ 2 if p in (0, GROUP - 1) else None),
        "out_x": pairs(lambda t, p: t ^ 1 if p not in (0, GROUP - 1) else None),
        "out_y": pairs(lambda t, p: t ^ 2 if p not in (0, GROUP - 1) else None),
    }


def slot_of(name, p):
    low = (p < GROUP // 2).astype(jnp.int32)
    even = 1 - p % 2
    return {
        "X": even,
        "Y": 2 + low,
        "O": 4 + low,
        "B": 5 - low,
        "W": 3 - low,
        "GE": 1 - even,
    }[name]


def contract(a, b, dims):
    return lax.dot_general(a, b, (dims, ((), ())), preferred_element_type=jnp.float32)


def fold_max(value):
    return jnp.max(value.reshape(-1, SUBLANES, value.shape[1]), axis=0)


def join(parts, axis):
    return parts[0] if len(parts) == 1 else jnp.concatenate(parts, axis=axis)


def stage_call(q, entries, state, lists, density, final):
    tokens, features = q.shape
    heads = features // HEAD_DIM
    kinds = [entry[0] for entry in entries]
    starts = [0]
    for _, k, v in entries:
        starts += [starts[-1] + len(k), starts[-1] + len(k) + len(v)]
    halves = lists.shape[1]
    positions = lists.shape[3]
    frames = lax.axis_size("tm")
    bands = lax.axis_size("space")
    edge = tokens // halves
    n_in = starts[-1]

    def kernel(lists_ref, density_ref, *refs):
        q_ref = refs[0]
        kv = refs[1 : 1 + n_in]
        rest, scratch = refs[1 + n_in : -4], refs[-4:]
        old_refs = None
        if state is not None:
            old_refs = rest[:3]
            rest = rest[3:]
        t = lax.axis_index("tm")
        band = lax.axis_index("space")
        p = t % GROUP

        def allow_of(kind):
            if kind in ("own", "other"):
                return [[None]] * halves
            if kind == "before":
                return [[band > 0]] * halves
            if kind == "after":
                return [[band < bands - 1]] * halves
            slot = slot_of(kind, p)
            step = jnp.left_shift(1, slot // 2)
            there = t + jnp.where(slot % 2 == 0, -step, step)
            ok = (there >= 0) & (there < frames)
            live = density_ref[0, slot // 2]
            out = []
            for half in range(halves):
                row = []
                for kb in range(positions):
                    hit = (lists_ref[0, half, slot, 0] == kb) & (live > 0)
                    for i in range(1, positions):
                        hit = hit | ((lists_ref[0, half, slot, i] == kb) & (live > i))
                    row.append(ok & hit)
                out.append(row)
            return out

        rows_of = {
            "before": pl.ds(tokens - edge, edge),
            "after": pl.ds(0, edge),
            "other": pl.ds(pl.multiple_of(jnp.where(band > 0, tokens - edge, 0), edge), edge),
        }
        inner = (p > 0) & (p < GROUP - 1)
        bands_of = []
        for kind in kinds:
            allow = allow_of(kind)
            rows = (edge if kind in rows_of else tokens) // len(allow[0])
            for kb in range(len(allow[0])):
                row = bands_of[-1][0] + bands_of[-1][1] if bands_of else 0
                bands_of.append((row, rows, [allow[half][kb] for half in range(halves)]))

        def columns(h):
            return pl.ds(pl.multiple_of(h * HEAD_DIM, HEAD_DIM), HEAD_DIM)

        def stacked(h, part):
            cols = columns(h)
            pieces = []
            for i, kind in enumerate(kinds):
                rows = rows_of.get(kind, slice(None))
                refs_i = kv[starts[2 * i + part] : starts[2 * i + part + 1]]
                if kind == "GE" and part == 0:
                    whole, low, high = [ref[:, cols] for ref in refs_i]
                    high = jnp.where(inner, jnp.zeros_like(high), high)
                    piece = whole + join([low, high], 0)
                else:
                    piece = join([ref[rows, cols] for ref in refs_i], 0)
                pieces.append(piece)
            return join(pieces, 0)

        def scores(h, dst):
            s = contract(stacked(h, 0), q_ref[:, columns(h)], ((1,), (1,)))
            dst[...] = s
            tops = []
            for half in range(halves):
                cols = slice(half * edge, (half + 1) * edge)
                top = None if state is None else old_refs[0][h][:, cols]
                for row, rows, allow in bands_of:
                    piece = fold_max(s[row : row + rows, cols])
                    if allow[half] is not None:
                        piece = jnp.where(allow[half], piece, NEG)
                    top = piece if top is None else jnp.maximum(top, piece)
                tops.append(jnp.max(top, axis=0, keepdims=True))
            return join(tops, 1)

        def weigh(src, dst, top):
            for half in range(halves):
                cols = slice(half * edge, (half + 1) * edge)
                shift = top[:, cols] * SCALE2
                for row, rows, allow in bands_of:
                    off = shift if allow[half] is None else jnp.where(allow[half], shift, -NEG)
                    w = jnp.exp2(src[row : row + rows, cols] * SCALE2 - off)
                    dst[row : row + rows, cols] = w.astype(jnp.bfloat16)

        def mix(h, src, top):
            v = jnp.transpose(stacked(h, 1))
            ones = jnp.ones((2 * SUBLANES, v.shape[1]), jnp.bfloat16)
            mixed = contract(join([v, ones], 0), src[...], ((1,), (0,)))
            acc, total = mixed[:HEAD_DIM], mixed[HEAD_DIM : HEAD_DIM + SUBLANES]
            if state is not None:
                decay = jnp.exp2((old_refs[0][h][0:1] - top) * SCALE2)
                total = total + old_refs[1][h] * decay
                acc = acc + old_refs[2][h] * decay
            if final:
                scaled = acc * (1.0 / total[0:1])
                rest[0][:, columns(h)] = jnp.transpose(scaled.astype(jnp.bfloat16))
            else:
                rest[0][h] = jnp.broadcast_to(top, (SUBLANES, tokens))
                rest[1][h] = total
                rest[2][h] = acc

        s_refs, w_refs = scratch[:2], scratch[2:]

        def step(h, ready, next_ready, ahead):
            if ready is not None:
                for n in range(2):
                    mix(h + n, w_refs[n], ready[n])
            if next_ready is not None:
                for n in range(2):
                    weigh(s_refs[n], w_refs[n], next_ready[n])
            if ahead:
                return tuple(scores(h + 4 + n, s_refs[n]) for n in range(2))
            return None

        first = step(-4, None, None, True)
        second = step(-2, None, first, True)
        first, second = lax.fori_loop(
            0,
            heads // 2 - 2,
            lambda i, tops: (tops[1], step(2 * i, tops[0], tops[1], True)),
            (first, second),
            unroll=UNROLL,
        )
        step(heads - 4, first, second, False)
        step(heads - 2, second, None, False)

    smem = pl.BlockSpec(memory_space=pltpu.SMEM)
    vmem = pl.BlockSpec(memory_space=pltpu.VMEM)
    operands = [lists, density, q]
    keys = 0
    for kind, k, v in entries:
        operands += [*k, *v]
        keys += edge if kind in ("before", "after", "other") else tokens
    if state is not None:
        operands += list(state)
    operands = operands[:2] + [
        pltpu.with_memory_space_constraint(value, pltpu.VMEM) for value in operands[2:]
    ]
    specs = [smem, smem] + [vmem] * (len(operands) - 2)
    if final:
        outs, out_specs = jax.ShapeDtypeStruct((tokens, features), jnp.bfloat16), vmem
    else:
        small = pltpu.VMEM((heads, SUBLANES, tokens), jnp.float32)
        large = pltpu.VMEM((heads, HEAD_DIM, tokens), jnp.float32)
        outs, out_specs = (small, small, large), (vmem, vmem, vmem)
    return pl.pallas_call(
        kernel,
        in_specs=specs,
        out_specs=out_specs,
        out_shape=outs,
        scratch_shapes=[pltpu.VMEM((keys, tokens), jnp.float32)] * 2
        + [pltpu.VMEM((keys, tokens), jnp.bfloat16)] * 2,
        compiler_params=pltpu.CompilerParams(vmem_limit_bytes=VMEM_LIMIT),
        cost_estimate=pl.CostEstimate(
            flops=4 * tokens * keys * features,
            transcendentals=tokens * keys * heads,
            bytes_accessed=2 * features * (2 * keys + 4 * tokens),
        ),
    )(*operands)


def split_call(keys, values):
    half = keys.shape[1] // 2
    part = pltpu.VMEM((1, half) + keys.shape[2:], keys.dtype)

    def kernel(k_ref, v_ref, *rest):
        outs, sems = rest[:-1], rest[-1]
        sources = [
            k_ref.at[:, half:],
            k_ref.at[:, :half],
            v_ref.at[:, :half],
            v_ref.at[:, half:],
        ]
        copies = [
            pltpu.make_async_copy(src, dst, sems.at[n])
            for n, (src, dst) in enumerate(zip(sources, outs))
        ]
        for copy in copies:
            copy.start()
        for copy in copies:
            copy.wait()

    return pl.pallas_call(
        kernel,
        in_specs=[pl.BlockSpec(memory_space=pl.ANY)] * 2,
        out_specs=[pl.BlockSpec(memory_space=pltpu.VMEM)] * 4,
        out_shape=[part] * 4,
        compiler_params=pltpu.CompilerParams(vmem_limit_bytes=VMEM_LIMIT),
        scratch_shapes=[pltpu.SemaphoreType.DMA((4,))],
        name="split",
    )(keys, values)


def body(queries, keys, values, key_lists, density):
    _, rows_dev, width, features = queries.shape
    frames = lax.axis_size("tm")
    bands = lax.axis_size("space")
    route = routes(frames)
    up = [(i, i + 1) for i in range(bands - 1)]
    down = [(j, i) for i, j in up]

    def send(value, pairs, axis="tm"):
        return lax.ppermute(value, axis, pairs)

    def flat(value):
        return value.reshape(-1, features)

    b_k = send(keys, route["b"])
    x_k = send(keys, route["x"])
    x_v = send(values, route["x"])
    keys1, keys0, values0, values1 = split_call(keys, values)
    y_k1 = send(keys1, route["y"])
    y_v0 = send(values0, route["y"])
    y_v1 = send(values1, route["y"])
    y_k0 = send(keys0, route["y"])
    o_k0 = send(keys0, route["o"])
    o_k1 = send(keys1, route["o"])
    o_v = send(values, route["o"])
    if bands == 2:
        s_k = send(keys, up + down, "space")
        s_v = send(values, up + down, "space")
        beside = [("other", (flat(s_k),), (flat(s_v),))]
    else:
        up_k = send(keys, up, "space")
        up_v = send(values, up, "space")
        down_k = send(keys, down, "space")
        down_v = send(values, down, "space")
        beside = [
            ("before", (flat(up_k),), (flat(up_v),)),
            ("after", (flat(down_k),), (flat(down_v),)),
        ]

    p = lax.axis_index("tm") % GROUP
    inner = (p > 0) & (p < GROUP - 1)
    w_k1 = send(y_k1, route["b"])
    w_v0 = send(y_v0, route["b"])
    w_v1 = send(y_v1, route["b"])
    w_k0 = send(o_k0, route["y"])
    r_k = send(jnp.where(inner, w_k1, o_k0), route["x"])
    r_v0 = send(jnp.where(inner, w_v0, y_v0), route["x"])
    r_v1 = send(jnp.where(inner, w_v1, y_v1), route["x"])
    g_k = send(x_k, route["in_y"])
    b_v = send(values, route["b"])
    e_k0 = send(r_k, route["out_y"])

    q = flat(queries)
    state = stage_call(
        q,
        [("own", (flat(keys),), (flat(values),))] + beside,
        None,
        key_lists,
        density,
        False,
    )
    state = stage_call(
        q,
        [
            ("X", (flat(x_k),), (flat(x_v),)),
            ("Y", (flat(y_k0), flat(y_k1)), (flat(y_v0), flat(y_v1))),
        ],
        state,
        key_lists,
        density,
        False,
    )
    state = stage_call(
        q,
        [
            ("O", (flat(o_k0), flat(o_k1)), (flat(o_v),)),
            ("W", (flat(w_k0), flat(w_k1)), (flat(w_v0), flat(w_v1))),
        ],
        state,
        key_lists,
        density,
        False,
    )
    result = stage_call(
        q,
        [
            ("B", (flat(b_k),), (flat(b_v),)),
            ("GE", (flat(g_k), flat(e_k0), flat(r_k)), (flat(r_v0), flat(r_v1))),
        ],
        state,
        key_lists,
        density,
        True,
    )
    return result.reshape(1, rows_dev, width, features)


def solution(mesh):
    in_specs = (
        P("tm", "space", None, None),
        P("tm", "space", None, None),
        P("tm", "space", None, None),
        P("tm", "space", None, None),
        P("tm", None),
    )
    out_specs = P("tm", "space", None, None)
    return jax.shard_map(body, mesh=mesh, in_specs=in_specs, out_specs=out_specs, check_vma=False)
```

time: 136 us -> 115 us (0.85)
  the two profiles are of different devices: /device:TPU:12 before, /device:TPU:0 now
where the time goes in v4:
time: 115 us
  waiting for transfers between devices  48.7 us (42%)
  starting transfers between devices  40.2 us (35%)
  Pallas kernels  18.6 us (16%)
  local copies, waits for them, and re-layouts  5.43 us (5%)
  other arithmetic  1.67 us (1%)
    ppermute x22, waiting for transfers between devices, send(): return lax.ppermute(value, axis, pairs)  48.7 us
    ppermute x22, starting transfers between devices, send(): return lax.ppermute(value, axis, pairs)  40.2 us
    pallas_call x4, Pallas kernels, stage_call(): pl.pallas_call(kernel, in_specs=specs, out_specs=out_specs, out_shape=out...  16.5 us
    unnamed x35, local copies, waits for them, and re-layouts  5.43 us
  transfers between devices with their start and end apart: 22, of which 8 were waited for; matrix products, arithmetic and copies ran while one was open for 2% of the time, Pallas kernels for 10%

profile of v4, /device:TPU:0, one launch (start us, length us, event | category | flops | bytes accessed | tf_op | source)
XLA Modules:
  0.0 114.9 jit_solution(669170852100080474)
XLA Ops:
  0.0 2.1 %split.1 = (bf16[1,2,64,1536]{3,2,1,0:T(8,128)(2,1)}, bf16[1,2,64,1536]{3,2,1,0:T(8,128)(2,1)S(1)}, bf16[1,2,64,1536]{3,2,1,0:T(8,128)(2,1)S(1)}, bf16[1,2,64,1536]{3,2,1,0:T(8,128)(2,1)S(1)}) custom-call(bf16[1,4,64,1536]{3,2,1,0:T(8,128)(2,1)} %k_ref.1, bf16[1,4,64,1536]{3,2,1,0:T(8,128)(2,1)} %v_ref.1), custom_call_target="tpu_custom_call" | custom-call | tf_op jit(solution)/shard_map/split/pallas_call | solution.py:271
  2.1 3.1 %collective-permute-start.4 = (bf16[1,2,64,1536]{3,2,1,0:T(8,128)(2,1)}, bf16[1,2,64,1536]{3,2,1,0:T(8,128)(2,1)S(1)}, u32[]{:S(2)}, u32[]{:S(2)}) collective-permute-start(bf16[1,2,64,1536]{3,2,1,0:T(8,128)(2,1)} %get-tuple-element.18), channel_id=1, source_target_pairs={{0,4},{2,6},{4,0},{6,2},{8,12},{10,14},{12,8},{14,10},{16,20},{18,... | collective-permute-start | bytes 1179656 | tf_op jit(solution)/shard_map/ppermute | solution.py:291
  5.3 1.9 %collective-permute-start.12 = (bf16[1,2,64,1536]{3,2,1,0:T(8,128)(2,1)S(1)}, bf16[1,2,64,1536]{3,2,1,0:T(8,128)(2,1)S(1)}, u32[]{:S(2)}, u32[]{:S(2)}) collective-permute-start(bf16[1,2,64,1536]{3,2,1,0:T(8,128)(2,1)S(1)} %get-tuple-element.21), channel_id=1, source_target_pairs={{0,4},{2,6},{4,0},{6,2},{8,12},{10,14},{12,8},{14,10},{16,20},{18,... | collective-permute-start | bytes 1179656 | tf_op jit(solution)/shard_map/ppermute | solution.py:291
  7.3 1.3 %collective-permute-start.6 = (bf16[1,2,64,1536]{3,2,1,0:T(8,128)(2,1)S(1)}, bf16[1,2,64,1536]{3,2,1,0:T(8,128)(2,1)S(1)}, u32[]{:S(2)}, u32[]{:S(2)}) collective-permute-start(bf16[1,2,64,1536]{3,2,1,0:T(8,128)(2,1)S(1)} %get-tuple-element.19), channel_id=1, source_target_pairs={{4,12},{6,14},{8,0},{10,2},{12,20},{14,22},{16,8},{18,10},{20,28},... | collective-permute-start | bytes 1179656 | tf_op jit(solution)/shard_map/ppermute | solution.py:291
  8.6 6.8 %collective-permute-done.4 = bf16[1,2,64,1536]{3,2,1,0:T(8,128)(2,1)S(1)} collective-permute-done((bf16[1,2,64,1536]{3,2,1,0:T(8,128)(2,1)}, bf16[1,2,64,1536]{3,2,1,0:T(8,128)(2,1)S(1)}, u32[]{:S(2)}, u32[]{:S(2)}) %collective-permute-start.4) | collective-permute-done | bytes 393248 | tf_op jit(solution)/shard_map/ppermute | solution.py:291
  15.4 1.3 %collective-permute-start.15 = (bf16[1,2,64,1536]{3,2,1,0:T(8,128)(2,1)}, bf16[1,2,64,1536]{3,2,1,0:T(8,128)(2,1)}, u32[]{:S(2)}, u32[]{:S(2)}) collective-permute-start(bf16[1,2,64,1536]{3,2,1,0:T(8,128)(2,1)} %get-tuple-element.18), channel_id=1, source_target_pairs={{4,12},{6,14},{8,0},{10,2},{12,20},{14,22},{16,8},{18,10},{20,28},... | collective-permute-start | bytes 1179656 | tf_op jit(solution)/shard_map/ppermute | solution.py:291
  16.7 7.1 %collective-permute-done.9 = bf16[1,2,64,1536]{3,2,1,0:T(8,128)(2,1)S(1)} collective-permute-done((bf16[1,2,64,1536]{3,2,1,0:T(8,128)(2,1)S(1)}, bf16[1,2,64,1536]{3,2,1,0:T(8,128)(2,1)S(1)}, u32[]{:S(2)}, u32[]{:S(2)}) %collective-permute-start.9) | collective-permute-done | bytes 393248 | tf_op jit(solution)/shard_map/ppermute | solution.py:291
  23.8 4.0 %collective-permute-start.5 = (bf16[1,2,64,1536]{3,2,1,0:T(8,128)(2,1)S(1)}, bf16[1,2,64,1536]{3,2,1,0:T(8,128)(2,1)S(1)}, u32[]{:S(2)}, u32[]{:S(2)}) collective-permute-start(bf16[1,2,64,1536]{3,2,1,0:T(8,128)(2,1)S(1)} %collective-permute-done.4), channel_id=1, source_target_pairs={{0,8},{2,10},{8,16},{10,18},{12,4},{14,6},{16,24},{18,26},{20,12},... | collective-permute-start | bytes 1179656 | tf_op jit(solution)/shard_map/ppermute | solution.py:291
  28.5 3.7 %collective-permute-done.12 = bf16[1,2,64,1536]{3,2,1,0:T(8,128)(2,1)S(1)} collective-permute-done((bf16[1,2,64,1536]{3,2,1,0:T(8,128)(2,1)S(1)}, bf16[1,2,64,1536]{3,2,1,0:T(8,128)(2,1)S(1)}, u32[]{:S(2)}, u32[]{:S(2)}) %collective-permute-start.12) | collective-permute-done | bytes 393248 | tf_op jit(solution)/shard_map/ppermute | solution.py:291
  32.2 7.6 %collective-permute-done.19 = bf16[1,2,64,1536]{3,2,1,0:T(8,128)(2,1)S(1)} collective-permute-done((bf16[1,2,64,1536]{3,2,1,0:T(8,128)(2,1)S(1)}, bf16[1,2,64,1536]{3,2,1,0:T(8,128)(2,1)S(1)}, u32[]{:S(2)}, u32[]{:S(2)}) %collective-permute-start.19) | collective-permute-done | bytes 393248 | tf_op jit(solution)/shard_map/ppermute | solution.py:291
  40.6 1.7 %collective-permute-start.2 = (bf16[1,4,64,1536]{3,2,1,0:T(8,128)(2,1)}, bf16[1,4,64,1536]{3,2,1,0:T(8,128)(2,1)}, u32[]{:S(2)}, u32[]{:S(2)}) collective-permute-start(bf16[1,4,64,1536]{3,2,1,0:T(8,128)(2,1)} %k_ref.1), channel_id=1, source_target_pairs={{0,2},{2,0},{4,6},{6,4},{8,10},{10,8},{12,14},{14,12},{16,18},{18,... | collective-permute-start | bytes 2359304 | tf_op jit(solution)/shard_map/ppermute | solution.py:291
  42.7 3.7 %collective-permute-start.10 = (bf16[1,2,64,1536]{3,2,1,0:T(8,128)(2,1)S(1)}, bf16[1,2,64,1536]{3,2,1,0:T(8,128)(2,1)S(1)}, u32[]{:S(2)}, u32[]{:S(2)}) collective-permute-start(bf16[1,2,64,1536]{3,2,1,0:T(8,128)(2,1)S(1)} %collective-permute-done.9), channel_id=1, source_target_pairs={{0,8},{2,10},{8,16},{10,18},{12,4},{14,6},{16,24},{18,26},{20,12},... | collective-permute-start | bytes 1179656 | tf_op jit(solution)/shard_map/ppermute | solution.py:291
  46.5 0.9 copy-done.1
  47.3 1.3 %collective-permute-start.16 = (bf16[1,4,64,1536]{3,2,1,0:T(8,128)(2,1)}, bf16[1,4,64,1536]{3,2,1,0:T(8,128)(2,1)S(1)}, u32[]{:S(2)}, u32[]{:S(2)}) collective-permute-start(bf16[1,4,64,1536]{3,2,1,0:T(8,128)(2,1)} %v_ref.1), channel_id=1, source_target_pairs={{4,12},{6,14},{8,0},{10,2},{12,20},{14,22},{16,8},{18,10},{20,28},... | collective-permute-start | bytes 2359304 | tf_op jit(solution)/shard_map/ppermute | solution.py:291
  48.6 4.6 %collective-permute-start = (bf16[1,4,64,1536]{3,2,1,0:T(8,128)(2,1)}, bf16[1,4,64,1536]{3,2,1,0:T(8,128)(2,1)S(1)}, u32[]{:S(2)}, u32[]{:S(2)}) collective-permute-start(bf16[1,4,64,1536]{3,2,1,0:T(8,128)(2,1)} %k_ref.1), channel_id=1, source_target_pairs={{0,8},{2,10},{8,16},{10,18},{12,4},{14,6},{16,24},{18,26},{20,12},... | collective-permute-start | bytes 2359304 | tf_op jit(solution)/shard_map/ppermute | solution.py:291
  53.2 8.0 %collective-permute-done.2 = bf16[1,4,64,1536]{3,2,1,0:T(8,128)(2,1)} collective-permute-done((bf16[1,4,64,1536]{3,2,1,0:T(8,128)(2,1)}, bf16[1,4,64,1536]{3,2,1,0:T(8,128)(2,1)}, u32[]{:S(2)}, u32[]{:S(2)}) %collective-permute-start.2) | collective-permute-done | bytes 786464 | tf_op jit(solution)/shard_map/ppermute | solution.py:291
  61.3 1.7 %collective-permute-start.17 = (bf16[1,2,64,1536]{3,2,1,0:T(8,128)(2,1)S(1)}, bf16[1,2,64,1536]{3,2,1,0:T(8,128)(2,1)S(1)}, u32[]{:S(2)}, u32[]{:S(2)}) collective-permute-start(bf16[1,2,64,1536]{3,2,1,0:T(8,128)(2,1)S(1)} %collective-permute-done.6), channel_id=1, source_target_pairs={{0,4},{2,6},{4,0},{6,2},{8,12},{10,14},{12,8},{14,10},{16,20},{18,... | collective-permute-start | bytes 1179656 | tf_op jit(solution)/shard_map/ppermute | solution.py:291
  63.0 3.5 %collective-permute-start.13 = (bf16[1,2,64,1536]{3,2,1,0:T(8,128)(2,1)S(1)}, bf16[1,2,64,1536]{3,2,1,0:T(8,128)(2,1)S(1)}, u32[]{:S(2)}, u32[]{:S(2)}) collective-permute-start(bf16[1,2,64,1536]{3,2,1,0:T(8,128)(2,1)S(1)} %collective-permute-done.12), channel_id=1, source_target_pairs={{0,8},{2,10},{8,16},{10,18},{12,4},{14,6},{16,24},{18,26},{20,12},... | collective-permute-start | bytes 1179656 | tf_op jit(solution)/shard_map/ppermute | solution.py:291
  67.4 10.2 %collective-permute-done.18 = bf16[1,4,64,1536]{3,2,1,0:T(8,128)(2,1)S(1)} collective-permute-done((bf16[1,4,64,1536]{3,2,1,0:T(8,128)(2,1)}, bf16[1,4,64,1536]{3,2,1,0:T(8,128)(2,1)S(1)}, u32[]{:S(2)}, u32[]{:S(2)}) %collective-permute-start.18) | collective-permute-done | bytes 786464 | tf_op jit(solution)/shard_map/ppermute | solution.py:291
  77.6 4.6 %collective-permute-start.1 = (bf16[1,4,64,1536]{3,2,1,0:T(8,128)(2,1)}, bf16[1,4,64,1536]{3,2,1,0:T(8,128)(2,1)}, u32[]{:S(2)}, u32[]{:S(2)}) collective-permute-start(bf16[1,4,64,1536]{3,2,1,0:T(8,128)(2,1)} %v_ref.1), channel_id=1, source_target_pairs={{0,8},{2,10},{8,16},{10,18},{12,4},{14,6},{16,24},{18,26},{20,12},... | collective-permute-start | bytes 2359304 | tf_op jit(solution)/shard_map/ppermute | solution.py:291
  82.2 1.5 %collective-permute-start.7 = (bf16[1,2,64,1536]{3,2,1,0:T(8,128)(2,1)S(1)}, bf16[1,2,64,1536]{3,2,1,0:T(8,128)(2,1)S(1)}, u32[]{:S(2)}, u32[]{:S(2)}) collective-permute-start(bf16[1,2,64,1536]{3,2,1,0:T(8,128)(2,1)S(1)} %broadcast_select_fusion.2), channel_id=1, source_target_pairs={{0,2},{2,0},{4,6},{6,4},{8,10},{10,8},{12,14},{14,12},{16,18},{18,... | collective-permute-start | bytes 1179656 | tf_op jit(solution)/shard_map/ppermute | solution.py:291
  83.7 2.2 %collective-permute-start.3 = (bf16[1,4,64,1536]{3,2,1,0:T(8,128)(2,1)}, bf16[1,4,64,1536]{3,2,1,0:T(8,128)(2,1)}, u32[]{:S(2)}, u32[]{:S(2)}) collective-permute-start(bf16[1,4,64,1536]{3,2,1,0:T(8,128)(2,1)} %collective-permute-done.2), channel_id=1, source_target_pairs={{0,4},{6,2},{8,12},{14,10},{16,20},{22,18},{24,28},{30,26},{1,5},{... | collective-permute-start | bytes 2359304 | tf_op jit(solution)/shard_map/ppermute | solution.py:291
  86.7 0.9 copy-done.7
  88.5 2.0 %collective-permute-start.14 = (bf16[1,2,64,1536]{3,2,1,0:T(8,128)(2,1)}, bf16[1,2,64,1536]{3,2,1,0:T(8,128)(2,1)}, u32[]{:S(2)}, u32[]{:S(2)}) collective-permute-start(bf16[1,2,64,1536]{3,2,1,0:T(8,128)(2,1)} %broadcast_select_fusion), channel_id=1, source_target_pairs={{0,2},{2,0},{4,6},{6,4},{8,10},{10,8},{12,14},{14,12},{16,18},{18,... | collective-permute-start | bytes 1179656 | tf_op jit(solution)/shard_map/ppermute | solution.py:291
  90.5 3.7 %collective-permute-done.7 = bf16[1,2,64,1536]{3,2,1,0:T(8,128)(2,1)S(1)} collective-permute-done((bf16[1,2,64,1536]{3,2,1,0:T(8,128)(2,1)S(1)}, bf16[1,2,64,1536]{3,2,1,0:T(8,128)(2,1)S(1)}, u32[]{:S(2)}, u32[]{:S(2)}) %collective-permute-start.7) | collective-permute-done | bytes 393248 | tf_op jit(solution)/shard_map/ppermute | solution.py:291
  94.2 1.3 %collective-permute-start.8 = (bf16[1,2,64,1536]{3,2,1,0:T(8,128)(2,1)S(1)}, bf16[1,2,64,1536]{3,2,1,0:T(8,128)(2,1)}, u32[]{:S(2)}, u32[]{:S(2)}) collective-permute-start(bf16[1,2,64,1536]{3,2,1,0:T(8,128)(2,1)S(1)} %collective-permute-done.7), channel_id=1, source_target_pairs={{2,6},{4,0},{10,14},{12,8},{18,22},{20,16},{26,30},{28,24},{3,7},{... | collective-permute-start | bytes 1179656 | tf_op jit(solution)/shard_map/ppermute | solution.py:291
  95.6 1.1 copy-done.2
  96.7 3.7 %shard_map.55 = (f32[12,8,256]{2,1,0:T(8,128)S(1)}, f32[12,8,256]{2,1,0:T(8,128)S(1)}, f32[12,128,256]{2,1,0:T(8,128)S(1)}) custom-call(s32[1,2,6,2]{3,2,1,0:T(8,128)S(1)} %copy.9.lists_ref, s32[1,3]{1,0:T(1,128)S(1)} %copy-done.15, bf16[256,1536]{1,0:T(8,128)(2,1)S(1)} %bitcast.26, bf16[256,1536]{1,0:T(8,128)(2,1)} %bitcast.21.refs_1_, ...), custom_call_target="tpu_custom_call" | custom-call | flops 603979776 | bytes 5505024 | tf_op jit(solution)/shard_map/pallas_call | solution.py:234
  100.5 3.8 %shard_map.56 = (f32[12,8,256]{2,1,0:T(8,128)S(1)}, f32[12,8,256]{2,1,0:T(8,128)S(1)}, f32[12,128,256]{2,1,0:T(8,128)S(1)}) custom-call(s32[1,2,6,2]{3,2,1,0:T(8,128)S(1)} %copy.9.lists_ref, s32[1,3]{1,0:T(1,128)S(1)} %copy-done.15, bf16[256,1536]{1,0:T(8,128)(2,1)S(1)} %bitcast.27, bf16[256,1536]{1,0:T(8,128)(2,1)} %bitcast.15.refs_1_, ...), custom_call_target="tpu_custom_call" | custom-call | flops 805306368 | bytes 6291456 | tf_op jit(solution)/shard_map/pallas_call | solution.py:234
  104.4 3.6 %shard_map.57 = (f32[12,8,256]{2,1,0:T(8,128)S(1)}, f32[12,8,256]{2,1,0:T(8,128)S(1)}, f32[12,128,256]{2,1,0:T(8,128)S(1)}) custom-call(s32[1,2,6,2]{3,2,1,0:T(8,128)S(1)} %copy.9.lists_ref, s32[1,3]{1,0:T(1,128)S(1)} %copy-done.15, bf16[256,1536]{1,0:T(8,128)(2,1)S(1)} %bitcast.28, bf16[128,1536]{1,0:T(8,128)(2,1)S(1)} %bitcast.31, ...), custom_call_target="tpu_custom_call" | custom-call | flops 805306368 | bytes 6291456 | tf_op jit(solution)/shard_map/pallas_call | solution.py:234
  108.0 1.5 %collective-permute-done.14 = bf16[1,2,64,1536]{3,2,1,0:T(8,128)(2,1)} collective-permute-done((bf16[1,2,64,1536]{3,2,1,0:T(8,128)(2,1)}, bf16[1,2,64,1536]{3,2,1,0:T(8,128)(2,1)}, u32[]{:S(2)}, u32[]{:S(2)}) %collective-permute-start.14) | collective-permute-done | bytes 393248 | tf_op jit(solution)/shard_map/ppermute | solution.py:291
  109.5 5.3 %shard_map.58 = bf16[256,1536]{1,0:T(8,128)(2,1)} custom-call(s32[1,2,6,2]{3,2,1,0:T(8,128)S(1)} %copy.9.lists_ref, s32[1,3]{1,0:T(1,128)S(1)} %copy-done.15, bf16[256,1536]{1,0:T(8,128)(2,1)S(1)} %bitcast.29, bf16[256,1536]{1,0:T(8,128)(2,1)S(1)} %bitcast.37, bf16[256,1536]{1,0:T(8,128)(2,1)} %bitcast.2.refs_2_, bf16[256,1536]{1,0:T(8,128)(2,1)} %bitcast.3.refs_3_, ...), custom_call_target="tpu_custom_call" | custom-call | flops 805306368 | bytes 6291456 | tf_op jit(solution)/shard_map/pallas_call | solution.py:234
  (55 shorter events, 4.8 us)
Async XLA Ops:
  2.1 13.2 %collective-permute-start.4 = (bf16[1,2,64,1536]{3,2,1,0:T(8,128)(2,1)}, bf16[1,2,64,1536]{3,2,1,0:T(8,128)(2,1)S(1)}, u32[]{:S(2)}, u32[]{:S(2)}) collective-permute-start(bf16[1,2,64,1536]{3,2,1,0:T(8,128)(2,1)} %get-tuple-element.18), channel_id=1, source_target_pairs={{0,4},{2,6},{4,0},{6,2},{8,12},{10,14},{12,8},{14,10},{16,20},{18,... | collective-permute-start | bytes 1179656 | tf_op jit(solution)/shard_map/ppermute | solution.py:291
  5.2 18.6 %collective-permute-start.9 = (bf16[1,2,64,1536]{3,2,1,0:T(8,128)(2,1)S(1)}, bf16[1,2,64,1536]{3,2,1,0:T(8,128)(2,1)S(1)}, u32[]{:S(2)}, u32[]{:S(2)}) collective-permute-start(bf16[1,2,64,1536]{3,2,1,0:T(8,128)(2,1)S(1)} %get-tuple-element.20), channel_id=1, source_target_pairs={{0,4},{2,6},{4,0},{6,2},{8,12},{10,14},{12,8},{14,10},{16,20},{18,... | collective-permute-start | bytes 1179656 | tf_op jit(solution)/shard_map/ppermute | solution.py:291
  5.3 26.9 %collective-permute-start.12 = (bf16[1,2,64,1536]{3,2,1,0:T(8,128)(2,1)S(1)}, bf16[1,2,64,1536]{3,2,1,0:T(8,128)(2,1)S(1)}, u32[]{:S(2)}, u32[]{:S(2)}) collective-permute-start(bf16[1,2,64,1536]{3,2,1,0:T(8,128)(2,1)S(1)} %get-tuple-element.21), channel_id=1, source_target_pairs={{0,4},{2,6},{4,0},{6,2},{8,12},{10,14},{12,8},{14,10},{16,20},{18,... | collective-permute-start | bytes 1179656 | tf_op jit(solution)/shard_map/ppermute | solution.py:291
  7.2 32.6 %collective-permute-start.19 = (bf16[1,2,64,1536]{3,2,1,0:T(8,128)(2,1)S(1)}, bf16[1,2,64,1536]{3,2,1,0:T(8,128)(2,1)S(1)}, u32[]{:S(2)}, u32[]{:S(2)}) collective-permute-start(bf16[1,2,64,1536]{3,2,1,0:T(8,128)(2,1)S(1)} %get-tuple-element.19), channel_id=1, source_target_pairs={{0,4},{2,6},{4,0},{6,2},{8,12},{10,14},{12,8},{14,10},{16,20},{18,... | collective-permute-start | bytes 1179656 | tf_op jit(solution)/shard_map/ppermute | solution.py:291
  7.3 33.3 %collective-permute-start.6 = (bf16[1,2,64,1536]{3,2,1,0:T(8,128)(2,1)S(1)}, bf16[1,2,64,1536]{3,2,1,0:T(8,128)(2,1)S(1)}, u32[]{:S(2)}, u32[]{:S(2)}) collective-permute-start(bf16[1,2,64,1536]{3,2,1,0:T(8,128)(2,1)S(1)} %get-tuple-element.19), channel_id=1, source_target_pairs={{4,12},{6,14},{8,0},{10,2},{12,20},{14,22},{16,8},{18,10},{20,28},... | collective-permute-start | bytes 1179656 | tf_op jit(solution)/shard_map/ppermute | solution.py:291
  15.4 26.9 %collective-permute-start.15 = (bf16[1,2,64,1536]{3,2,1,0:T(8,128)(2,1)}, bf16[1,2,64,1536]{3,2,1,0:T(8,128)(2,1)}, u32[]{:S(2)}, u32[]{:S(2)}) collective-permute-start(bf16[1,2,64,1536]{3,2,1,0:T(8,128)(2,1)} %get-tuple-element.18), channel_id=1, source_target_pairs={{4,12},{6,14},{8,0},{10,2},{12,20},{14,22},{16,8},{18,10},{20,28},... | collective-permute-start | bytes 1179656 | tf_op jit(solution)/shard_map/ppermute | solution.py:291
  23.8 18.9 %collective-permute-start.5 = (bf16[1,2,64,1536]{3,2,1,0:T(8,128)(2,1)S(1)}, bf16[1,2,64,1536]{3,2,1,0:T(8,128)(2,1)S(1)}, u32[]{:S(2)}, u32[]{:S(2)}) collective-permute-start(bf16[1,2,64,1536]{3,2,1,0:T(8,128)(2,1)S(1)} %collective-permute-done.4), channel_id=1, source_target_pairs={{0,8},{2,10},{8,16},{10,18},{12,4},{14,6},{16,24},{18,26},{20,12},... | collective-permute-start | bytes 1179656 | tf_op jit(solution)/shard_map/ppermute | solution.py:291
  32.2 14.2 %collective-permute-start.20 = (bf16[1,4,64,1536]{3,2,1,0:T(8,128)(2,1)}, bf16[1,4,64,1536]{3,2,1,0:T(8,128)(2,1)S(1)}, u32[]{:S(2)}, u32[]{:S(2)}) collective-permute-start(bf16[1,4,64,1536]{3,2,1,0:T(8,128)(2,1)} %k_ref.1), channel_id=1, source_target_pairs={{0,1},{1,0},{2,3},{3,2},{4,5},{5,4},{6,7},{7,6},{8,9},{9,8},{10,11... | collective-permute-start | bytes 2359304 | tf_op jit(solution)/shard_map/ppermute | solution.py:291
  40.6 8.1 %collective-permute-start.21 = (bf16[1,4,64,1536]{3,2,1,0:T(8,128)(2,1)}, bf16[1,4,64,1536]{3,2,1,0:T(8,128)(2,1)}, u32[]{:S(2)}, u32[]{:S(2)}) collective-permute-start(bf16[1,4,64,1536]{3,2,1,0:T(8,128)(2,1)} %v_ref.1), channel_id=1, source_target_pairs={{0,1},{1,0},{2,3},{3,2},{4,5},{5,4},{6,7},{7,6},{8,9},{9,8},{10,11... | collective-permute-start | bytes 2359304 | tf_op jit(solution)/shard_map/ppermute | solution.py:291
  40.6 20.7 %collective-permute-start.2 = (bf16[1,4,64,1536]{3,2,1,0:T(8,128)(2,1)}, bf16[1,4,64,1536]{3,2,1,0:T(8,128)(2,1)}, u32[]{:S(2)}, u32[]{:S(2)}) collective-permute-start(bf16[1,4,64,1536]{3,2,1,0:T(8,128)(2,1)} %k_ref.1), channel_id=1, source_target_pairs={{0,2},{2,0},{4,6},{6,4},{8,10},{10,8},{12,14},{14,12},{16,18},{18,... | collective-permute-start | bytes 2359304 | tf_op jit(solution)/shard_map/ppermute | solution.py:291
  42.3 53.2 %copy-start.16 = (s32[1,2,6,2]{2,3,1,0:T(2,128)S(1)}, s32[1,2,6,2]{2,3,1,0:T(2,128)}, u32[]{:S(2)}) copy-start(s32[1,2,6,2]{2,3,1,0:T(2,128)} %param.8) | copy-start | bytes 292
  42.3 53.3 %copy-start = (bf16[1,4,64,1536]{3,2,1,0:T(8,128)(2,1)S(1)}, bf16[1,4,64,1536]{3,2,1,0:T(8,128)(2,1)}, u32[]{:S(2)}) copy-start(bf16[1,4,64,1536]{3,2,1,0:T(8,128)(2,1)} %param.5) | copy-start | bytes 2359300
  42.3 53.3 %copy-start.15 = (s32[1,3]{1,0:T(1,128)S(1)}, s32[1,3]{1,0:T(1,128)}, u32[]{:S(2)}) copy-start(s32[1,3]{1,0:T(1,128)} %density_ref.7) | copy-start | bytes 40
  42.3 35.3 %collective-permute-start.18 = (bf16[1,4,64,1536]{3,2,1,0:T(8,128)(2,1)}, bf16[1,4,64,1536]{3,2,1,0:T(8,128)(2,1)S(1)}, u32[]{:S(2)}, u32[]{:S(2)}) collective-permute-start(bf16[1,4,64,1536]{3,2,1,0:T(8,128)(2,1)} %v_ref.1), channel_id=1, source_target_pairs={{0,2},{2,0},{4,6},{6,4},{8,10},{10,8},{12,14},{14,12},{16,18},{18,... | collective-permute-start | bytes 2359304 | tf_op jit(solution)/shard_map/ppermute | solution.py:291
  42.7 20.4 %collective-permute-start.10 = (bf16[1,2,64,1536]{3,2,1,0:T(8,128)(2,1)S(1)}, bf16[1,2,64,1536]{3,2,1,0:T(8,128)(2,1)S(1)}, u32[]{:S(2)}, u32[]{:S(2)}) collective-permute-start(bf16[1,2,64,1536]{3,2,1,0:T(8,128)(2,1)S(1)} %collective-permute-done.9), channel_id=1, source_target_pairs={{0,8},{2,10},{8,16},{10,18},{12,4},{14,6},{16,24},{18,26},{20,12},... | collective-permute-start | bytes 1179656 | tf_op jit(solution)/shard_map/ppermute | solution.py:291
  47.3 39.3 %collective-permute-start.16 = (bf16[1,4,64,1536]{3,2,1,0:T(8,128)(2,1)}, bf16[1,4,64,1536]{3,2,1,0:T(8,128)(2,1)S(1)}, u32[]{:S(2)}, u32[]{:S(2)}) collective-permute-start(bf16[1,4,64,1536]{3,2,1,0:T(8,128)(2,1)} %v_ref.1), channel_id=1, source_target_pairs={{4,12},{6,14},{8,0},{10,2},{12,20},{14,22},{16,8},{18,10},{20,28},... | collective-permute-start | bytes 2359304 | tf_op jit(solution)/shard_map/ppermute | solution.py:291
  48.6 39.0 %collective-permute-start = (bf16[1,4,64,1536]{3,2,1,0:T(8,128)(2,1)}, bf16[1,4,64,1536]{3,2,1,0:T(8,128)(2,1)S(1)}, u32[]{:S(2)}, u32[]{:S(2)}) collective-permute-start(bf16[1,4,64,1536]{3,2,1,0:T(8,128)(2,1)} %k_ref.1), channel_id=1, source_target_pairs={{0,8},{2,10},{8,16},{10,18},{12,4},{14,6},{16,24},{18,26},{20,12},... | collective-permute-start | bytes 2359304 | tf_op jit(solution)/shard_map/ppermute | solution.py:291
  61.3 20.9 %collective-permute-start.17 = (bf16[1,2,64,1536]{3,2,1,0:T(8,128)(2,1)S(1)}, bf16[1,2,64,1536]{3,2,1,0:T(8,128)(2,1)S(1)}, u32[]{:S(2)}, u32[]{:S(2)}) collective-permute-start(bf16[1,2,64,1536]{3,2,1,0:T(8,128)(2,1)S(1)} %collective-permute-done.6), channel_id=1, source_target_pairs={{0,4},{2,6},{4,0},{6,2},{8,12},{10,14},{12,8},{14,10},{16,20},{18,... | collective-permute-start | bytes 1179656 | tf_op jit(solution)/shard_map/ppermute | solution.py:291
  63.0 20.6 %collective-permute-start.13 = (bf16[1,2,64,1536]{3,2,1,0:T(8,128)(2,1)S(1)}, bf16[1,2,64,1536]{3,2,1,0:T(8,128)(2,1)S(1)}, u32[]{:S(2)}, u32[]{:S(2)}) collective-permute-start(bf16[1,2,64,1536]{3,2,1,0:T(8,128)(2,1)S(1)} %collective-permute-done.12), channel_id=1, source_target_pairs={{0,8},{2,10},{8,16},{10,18},{12,4},{14,6},{16,24},{18,26},{20,12},... | collective-permute-start | bytes 1179656 | tf_op jit(solution)/shard_map/ppermute | solution.py:291
  77.6 10.0 %copy-start.5 = (bf16[1,4,64,1536]{3,2,1,0:T(8,128)(2,1)}, bf16[1,4,64,1536]{3,2,1,0:T(8,128)(2,1)S(1)}, u32[]{:S(2)}) copy-start(bf16[1,4,64,1536]{3,2,1,0:T(8,128)(2,1)S(1)} %collective-permute-done.18) | copy-start | bytes 2359300
  77.6 30.4 %collective-permute-start.1 = (bf16[1,4,64,1536]{3,2,1,0:T(8,128)(2,1)}, bf16[1,4,64,1536]{3,2,1,0:T(8,128)(2,1)}, u32[]{:S(2)}, u32[]{:S(2)}) collective-permute-start(bf16[1,4,64,1536]{3,2,1,0:T(8,128)(2,1)} %v_ref.1), channel_id=1, source_target_pairs={{0,8},{2,10},{8,16},{10,18},{12,4},{14,6},{16,24},{18,26},{20,12},... | collective-permute-start | bytes 2359304 | tf_op jit(solution)/shard_map/ppermute | solution.py:291
  82.2 12.0 %copy-start.13 = (bf16[1,2,64,1536]{3,2,1,0:T(8,128)(2,1)}, bf16[1,2,64,1536]{3,2,1,0:T(8,128)(2,1)S(1)}, u32[]{:S(2)}) copy-start(bf16[1,2,64,1536]{3,2,1,0:T(8,128)(2,1)S(1)} %collective-permute-done.17) | copy-start | bytes 1179652
  82.2 12.0 %collective-permute-start.7 = (bf16[1,2,64,1536]{3,2,1,0:T(8,128)(2,1)S(1)}, bf16[1,2,64,1536]{3,2,1,0:T(8,128)(2,1)S(1)}, u32[]{:S(2)}, u32[]{:S(2)}) collective-permute-start(bf16[1,2,64,1536]{3,2,1,0:T(8,128)(2,1)S(1)} %broadcast_select_fusion.2), channel_id=1, source_target_pairs={{0,2},{2,0},{4,6},{6,4},{8,10},{10,8},{12,14},{14,12},{16,18},{18,... | collective-permute-start | bytes 1179656 | tf_op jit(solution)/shard_map/ppermute | solution.py:291
  83.7 25.9 %collective-permute-start.3 = (bf16[1,4,64,1536]{3,2,1,0:T(8,128)(2,1)}, bf16[1,4,64,1536]{3,2,1,0:T(8,128)(2,1)}, u32[]{:S(2)}, u32[]{:S(2)}) collective-permute-start(bf16[1,4,64,1536]{3,2,1,0:T(8,128)(2,1)} %collective-permute-done.2), channel_id=1, source_target_pairs={{0,4},{6,2},{8,12},{14,10},{16,20},{22,18},{24,28},{30,26},{1,5},{... | collective-permute-start | bytes 2359304 | tf_op jit(solution)/shard_map/ppermute | solution.py:291
  87.6 20.4 %collective-permute-start.11 = (bf16[1,2,64,1536]{3,2,1,0:T(8,128)(2,1)}, bf16[1,2,64,1536]{3,2,1,0:T(8,128)(2,1)}, u32[]{:S(2)}, u32[]{:S(2)}) collective-permute-start(bf16[1,2,64,1536]{3,2,1,0:T(8,128)(2,1)} %broadcast_select_fusion.1), channel_id=1, source_target_pairs={{0,2},{2,0},{4,6},{6,4},{8,10},{10,8},{12,14},{14,12},{16,18},{18,... | collective-permute-start | bytes 1179656 | tf_op jit(solution)/shard_map/ppermute | solution.py:291
  88.5 21.1 %collective-permute-start.14 = (bf16[1,2,64,1536]{3,2,1,0:T(8,128)(2,1)}, bf16[1,2,64,1536]{3,2,1,0:T(8,128)(2,1)}, u32[]{:S(2)}, u32[]{:S(2)}) collective-permute-start(bf16[1,2,64,1536]{3,2,1,0:T(8,128)(2,1)} %broadcast_select_fusion), channel_id=1, source_target_pairs={{0,2},{2,0},{4,6},{6,4},{8,10},{10,8},{12,14},{14,12},{16,18},{18,... | collective-permute-start | bytes 1179656 | tf_op jit(solution)/shard_map/ppermute | solution.py:291
  94.2 15.4 %collective-permute-start.8 = (bf16[1,2,64,1536]{3,2,1,0:T(8,128)(2,1)S(1)}, bf16[1,2,64,1536]{3,2,1,0:T(8,128)(2,1)}, u32[]{:S(2)}, u32[]{:S(2)}) collective-permute-start(bf16[1,2,64,1536]{3,2,1,0:T(8,128)(2,1)S(1)} %collective-permute-done.7), channel_id=1, source_target_pairs={{2,6},{4,0},{10,14},{12,8},{18,22},{20,16},{26,30},{28,24},{3,7},{... | collective-permute-start | bytes 1179656 | tf_op jit(solution)/shard_map/ppermute | solution.py:291
  96.7 3.8 %copy-start.10 = (bf16[1,2,64,1536]{3,2,1,0:T(8,128)(2,1)S(1)}, bf16[1,2,64,1536]{3,2,1,0:T(8,128)(2,1)}, u32[]{:S(2)}) copy-start(bf16[1,2,64,1536]{3,2,1,0:T(8,128)(2,1)} %copy-done.9) | copy-start | bytes 1179652
  96.7 3.8 %copy-start.12 = (bf16[1,2,64,1536]{3,2,1,0:T(8,128)(2,1)S(1)}, bf16[1,2,64,1536]{3,2,1,0:T(8,128)(2,1)}, u32[]{:S(2)}) copy-start(bf16[1,2,64,1536]{3,2,1,0:T(8,128)(2,1)} %copy-done.11) | copy-start | bytes 1179652
  100.5 3.8 %copy-start.8 = (bf16[1,4,64,1536]{3,2,1,0:T(8,128)(2,1)S(1)}, bf16[1,4,64,1536]{3,2,1,0:T(8,128)(2,1)}, u32[]{:S(2)}) copy-start(bf16[1,4,64,1536]{3,2,1,0:T(8,128)(2,1)} %copy-done.7) | copy-start | bytes 2359300
  100.5 3.8 %copy-start.14 = (bf16[1,2,64,1536]{3,2,1,0:T(8,128)(2,1)S(1)}, bf16[1,2,64,1536]{3,2,1,0:T(8,128)(2,1)}, u32[]{:S(2)}) copy-start(bf16[1,2,64,1536]{3,2,1,0:T(8,128)(2,1)} %copy-done.13) | copy-start | bytes 1179652
  104.3 5.2 %copy-start.4 = (bf16[1,4,64,1536]{3,2,1,0:T(8,128)(2,1)S(1)}, bf16[1,4,64,1536]{3,2,1,0:T(8,128)(2,1)}, u32[]{:S(2)}) copy-start(bf16[1,4,64,1536]{3,2,1,0:T(8,128)(2,1)} %copy-done.3) | copy-start | bytes 2359300
  (7 other events, 9.1 us)

commit v5 on v4

--- a/solution.py
+++ b/solution.py
@@ -73,7 +73,7 @@
     for _, k, v in entries:
         starts += [starts[-1] + len(k), starts[-1] + len(k) + len(v)]
     halves = lists.shape[1]
-    positions = lists.shape[3]
+    positions = lists.shape[2]
     frames = lax.axis_size("tm")
     bands = lax.axis_size("space")
     edge = tokens // halves
@@ -107,9 +107,9 @@
             for half in range(halves):
                 row = []
                 for kb in range(positions):
-                    hit = (lists_ref[0, half, slot, 0] == kb) & (live > 0)
+                    hit = (lists_ref[0, half, 0, slot] == kb) & (live > 0)
                     for i in range(1, positions):
-                        hit = hit | ((lists_ref[0, half, slot, i] == kb) & (live > i))
+                        hit = hit | ((lists_ref[0, half, i, slot] == kb) & (live > i))
                     row.append(ok & hit)
                 out.append(row)
             return out
@@ -119,7 +119,7 @@
             "after": pl.ds(0, edge),
             "other": pl.ds(pl.multiple_of(jnp.where(band > 0, tokens - edge, 0), edge), edge),
         }
-        inner = (p > 0) & (p < GROUP - 1)
+        inner = is_inner(t)
         bands_of = []
         for kind in kinds:
             allow = allow_of(kind)
@@ -247,21 +247,46 @@
     )(*operands)
 
 
-def split_call(keys, values):
-    half = keys.shape[1] // 2
-    part = pltpu.VMEM((1, half) + keys.shape[2:], keys.dtype)
-
-    def kernel(k_ref, v_ref, *rest):
-        outs, sems = rest[:-1], rest[-1]
-        sources = [
-            k_ref.at[:, half:],
-            k_ref.at[:, :half],
-            v_ref.at[:, :half],
-            v_ref.at[:, half:],
-        ]
+def is_inner(frame):
+    p = frame % GROUP
+    return (p > 0) & (p < GROUP - 1)
+
+
+def pick_call(inner_value, outer_value):
+    def kernel(inner_ref, outer_ref, out_ref):
+        inner = is_inner(lax.axis_index("tm"))
+
+        @pl.when(inner)
+        def _():
+            out_ref[...] = inner_ref[...]
+
+        @pl.when(jnp.logical_not(inner))
+        def _():
+            out_ref[...] = outer_ref[...]
+
+    vmem = pl.BlockSpec(memory_space=pltpu.VMEM)
+    operands = [
+        pltpu.with_memory_space_constraint(value, pltpu.VMEM)
+        for value in (inner_value, outer_value)
+    ]
+    return pl.pallas_call(
+        kernel,
+        in_specs=[vmem, vmem],
+        out_specs=vmem,
+        out_shape=pltpu.VMEM(inner_value.shape, inner_value.dtype),
+        compiler_params=pltpu.CompilerParams(vmem_limit_bytes=VMEM_LIMIT // 2),
+        name="pick",
+    )(*operands)
+
+
+def split_call(value):
+    half = value.shape[1] // 2
+    part = pltpu.VMEM((1, half) + value.shape[2:], value.dtype)
+
+    def kernel(ref, low, high, sems):
         copies = [
-            pltpu.make_async_copy(src, dst, sems.at[n])
-            for n, (src, dst) in enumerate(zip(sources, outs))
+            pltpu.make_async_copy(ref.at[:, :half], low, sems.at[0]),
+            pltpu.make_async_copy(ref.at[:, half:], high, sems.at[1]),
         ]
         for copy in copies:
             copy.start()
@@ -270,13 +295,12 @@
 
     return pl.pallas_call(
         kernel,
-        in_specs=[pl.BlockSpec(memory_space=pl.ANY)] * 2,
-        out_specs=[pl.BlockSpec(memory_space=pltpu.VMEM)] * 4,
-        out_shape=[part] * 4,
+        in_specs=[pl.BlockSpec(memory_space=pl.ANY)],
+        out_specs=[pl.BlockSpec(memory_space=pltpu.VMEM)] * 2,
+        out_shape=[part] * 2,
+        scratch_shapes=[pltpu.SemaphoreType.DMA((2,))],
         compiler_params=pltpu.CompilerParams(vmem_limit_bytes=VMEM_LIMIT),
-        scratch_shapes=[pltpu.SemaphoreType.DMA((4,))],
-        name="split",
-    )(keys, values)
+    )(value)
 
 
 def body(queries, keys, values, key_lists, density):
@@ -296,7 +320,8 @@
     b_k = send(keys, route["b"])
     x_k = send(keys, route["x"])
     x_v = send(values, route["x"])
-    keys1, keys0, values0, values1 = split_call(keys, values)
+    keys0, keys1 = split_call(keys)
+    values0, values1 = split_call(values)
     y_k1 = send(keys1, route["y"])
     y_v0 = send(values0, route["y"])
     y_v1 = send(values1, route["y"])
@@ -318,36 +343,29 @@
             ("after", (flat(down_k),), (flat(down_v),)),
         ]
 
-    p = lax.axis_index("tm") % GROUP
-    inner = (p > 0) & (p < GROUP - 1)
     w_k1 = send(y_k1, route["b"])
     w_v0 = send(y_v0, route["b"])
     w_v1 = send(y_v1, route["b"])
     w_k0 = send(o_k0, route["y"])
-    r_k = send(jnp.where(inner, w_k1, o_k0), route["x"])
-    r_v0 = send(jnp.where(inner, w_v0, y_v0), route["x"])
-    r_v1 = send(jnp.where(inner, w_v1, y_v1), route["x"])
+    r_k = send(pick_call(w_k1, o_k0), route["x"])
+    r_v0 = send(pick_call(w_v0, y_v0), route["x"])
+    r_v1 = send(pick_call(w_v1, y_v1), route["x"])
     g_k = send(x_k, route["in_y"])
     b_v = send(values, route["b"])
     e_k0 = send(r_k, route["out_y"])
 
     q = flat(queries)
+    lists = jnp.swapaxes(key_lists, 2, 3)
     state = stage_call(
         q,
-        [("own", (flat(keys),), (flat(values),))] + beside,
-        None,
-        key_lists,
-        density,
-        False,
-    )
-    state = stage_call(
-        q,
-        [
+        [("own", (flat(keys0), flat(keys1)), (flat(values0), flat(values1)))]
+        + beside
+        + [
             ("X", (flat(x_k),), (flat(x_v),)),
             ("Y", (flat(y_k0), flat(y_k1)), (flat(y_v0), flat(y_v1))),
         ],
-        state,
-        key_lists,
+        None,
+        lists,
         density,
         False,
     )
@@ -358,20 +376,20 @@
             ("W", (flat(w_k0), flat(w_k1)), (flat(w_v0), flat(w_v1))),
         ],
         state,
-        key_lists,
+        lists,
+        density,
+        False,
+    )
+    state = stage_call(
+        q,
+        [("GE", (flat(g_k), flat(e_k0), flat(r_k)), (flat(r_v0), flat(r_v1)))],
+        state,
+        lists,
         density,
         False,
     )
     result = stage_call(
-        q,
-        [
-            ("B", (flat(b_k),), (flat(b_v),)),
-            ("GE", (flat(g_k), flat(e_k0), flat(r_k)), (flat(r_v0), flat(r_v1))),
-        ],
-        state,
-        key_lists,
-        density,
-        True,
+        q, [("B", (flat(b_k),), (flat(b_v),))], state, lists, density, True
     )
     return result.reshape(1, rows_dev, width, features)
 

time: 115 us -> 113 us (0.983)
  the two profiles are of different devices: /device:TPU:0 before, /device:TPU:24 now
where the time goes in v5:
time: 113 us; the launch traced here: 112 us
  waiting for transfers between devices  62.2 us (55%)
  starting transfers between devices  34 us (30%)
  Pallas kernels  14.7 us (13%)
  local copies, waits for them, and re-layouts  1.15 us (1%)
    ppermute x22, waiting for transfers between devices, send(): return lax.ppermute(value, axis, pairs)  62.2 us
    ppermute x22, starting transfers between devices, send(): return lax.ppermute(value, axis, pairs)  34 us
    pallas_call x4, Pallas kernels, stage_call(): pl.pallas_call(kernel, in_specs=specs, out_specs=out_specs, out_shape=out...  13 us
  transfers between devices with their start and end apart: 22, of which 11 were waited for; matrix products, arithmetic and copies ran while one was open for 0% of the time, Pallas kernels for 10%

profile of v5, /device:TPU:24, one launch (start us, length us, event | category | flops | bytes accessed | tf_op | source)
XLA Modules:
  0.0 112.2 jit_solution(13216948277856042086)
XLA Ops:
  0.0 1.1 %copy-done.1 = bf16[1,4,64,1536]{3,2,1,0:T(8,128)(2,1)S(1)} copy-done((bf16[1,4,64,1536]{3,2,1,0:T(8,128)(2,1)S(1)}, bf16[1,4,64,1536]{3,2,1,0:T(8,128)(2,1)}, u32[]{:S(2)}) %copy-start.1) | copy-done | bytes 786456
  1.5 1.6 %collective-permute-start.4 = (bf16[1,2,64,1536]{3,2,1,0:T(8,128)(2,1)S(1)}, bf16[1,2,64,1536]{3,2,1,0:T(8,128)(2,1)S(1)}, u32[]{:S(2)}, u32[]{:S(2)}) collective-permute-start(bf16[1,2,64,1536]{3,2,1,0:T(8,128)(2,1)S(1)} %get-tuple-element.18), channel_id=1, source_target_pairs={{0,4},{2,6},{4,0},{6,2},{8,12},{10,14},{12,8},{14,10},{16,20},{18,... | collective-permute-start | bytes 1179656 | tf_op jit(solution)/shard_map/ppermute | solution.py:315
  3.1 1.1 %shard_map.56 = (bf16[1,2,64,1536]{3,2,1,0:T(8,128)(2,1)S(1)}, bf16[1,2,64,1536]{3,2,1,0:T(8,128)(2,1)S(1)}) custom-call(bf16[1,4,64,1536]{3,2,1,0:T(8,128)(2,1)} %ref.3), custom_call_target="tpu_custom_call" | custom-call | tf_op jit(solution)/shard_map/pallas_call | solution.py:296
  4.8 1.5 %collective-permute-start.12 = (bf16[1,2,64,1536]{3,2,1,0:T(8,128)(2,1)S(1)}, bf16[1,2,64,1536]{3,2,1,0:T(8,128)(2,1)S(1)}, u32[]{:S(2)}, u32[]{:S(2)}) collective-permute-start(bf16[1,2,64,1536]{3,2,1,0:T(8,128)(2,1)S(1)} %get-tuple-element.21), channel_id=1, source_target_pairs={{0,4},{2,6},{4,0},{6,2},{8,12},{10,14},{12,8},{14,10},{16,20},{18,... | collective-permute-start | bytes 1179656 | tf_op jit(solution)/shard_map/ppermute | solution.py:315
  6.4 1.5 %collective-permute-start.2 = (bf16[1,4,64,1536]{3,2,1,0:T(8,128)(2,1)S(1)}, bf16[1,4,64,1536]{3,2,1,0:T(8,128)(2,1)S(1)}, u32[]{:S(2)}, u32[]{:S(2)}) collective-permute-start(bf16[1,4,64,1536]{3,2,1,0:T(8,128)(2,1)S(1)} %copy-done.2), channel_id=1, source_target_pairs={{0,2},{2,0},{4,6},{6,4},{8,10},{10,8},{12,14},{14,12},{16,18},{18,... | collective-permute-start | bytes 2359304 | tf_op jit(solution)/shard_map/ppermute | solution.py:315
  7.8 5.7 %collective-permute-done.4 = bf16[1,2,64,1536]{3,2,1,0:T(8,128)(2,1)S(1)} collective-permute-done((bf16[1,2,64,1536]{3,2,1,0:T(8,128)(2,1)S(1)}, bf16[1,2,64,1536]{3,2,1,0:T(8,128)(2,1)S(1)}, u32[]{:S(2)}, u32[]{:S(2)}) %collective-permute-start.4) | collective-permute-done | bytes 393248 | tf_op jit(solution)/shard_map/ppermute | solution.py:315
  13.6 1.5 %collective-permute-start.21 = (bf16[1,2,64,1536]{3,2,1,0:T(8,128)(2,1)S(1)}, bf16[1,2,64,1536]{3,2,1,0:T(8,128)(2,1)S(1)}, u32[]{:S(2)}, u32[]{:S(2)}) collective-permute-start(bf16[1,2,64,1536]{3,2,1,0:T(8,128)(2,1)S(1)} %get-tuple-element.19), channel_id=1, source_target_pairs={{0,4},{2,6},{4,0},{6,2},{8,12},{10,14},{12,8},{14,10},{16,20},{18,... | collective-permute-start | bytes 1179656 | tf_op jit(solution)/shard_map/ppermute | solution.py:315
  15.1 6.9 %collective-permute-done.9.outer_ref = bf16[1,2,64,1536]{3,2,1,0:T(8,128)(2,1)S(1)} collective-permute-done((bf16[1,2,64,1536]{3,2,1,0:T(8,128)(2,1)S(1)}, bf16[1,2,64,1536]{3,2,1,0:T(8,128)(2,1)S(1)}, u32[]{:S(2)}, u32[]{:S(2)}) %collective-permute-start.9) | collective-permute-done | bytes 393248 | tf_op jit(solution)/shard_map/ppermute | solution.py:315
  22.0 2.4 %collective-permute-start.6 = (bf16[1,2,64,1536]{3,2,1,0:T(8,128)(2,1)S(1)}, bf16[1,2,64,1536]{3,2,1,0:T(8,128)(2,1)S(1)}, u32[]{:S(2)}, u32[]{:S(2)}) collective-permute-start(bf16[1,2,64,1536]{3,2,1,0:T(8,128)(2,1)S(1)} %get-tuple-element.19), channel_id=1, source_target_pairs={{4,12},{6,14},{8,0},{10,2},{12,20},{14,22},{16,8},{18,10},{20,28},... | collective-permute-start | bytes 1179656 | tf_op jit(solution)/shard_map/ppermute | solution.py:315
  24.4 6.1 %collective-permute-done.12.outer_ref = bf16[1,2,64,1536]{3,2,1,0:T(8,128)(2,1)S(1)} collective-permute-done((bf16[1,2,64,1536]{3,2,1,0:T(8,128)(2,1)S(1)}, bf16[1,2,64,1536]{3,2,1,0:T(8,128)(2,1)S(1)}, u32[]{:S(2)}, u32[]{:S(2)}) %collective-permute-start.12) | collective-permute-done | bytes 393248 | tf_op jit(solution)/shard_map/ppermute | solution.py:315
  30.4 2.4 %collective-permute-start.15 = (bf16[1,2,64,1536]{3,2,1,0:T(8,128)(2,1)S(1)}, bf16[1,2,64,1536]{3,2,1,0:T(8,128)(2,1)S(1)}, u32[]{:S(2)}, u32[]{:S(2)}) collective-permute-start(bf16[1,2,64,1536]{3,2,1,0:T(8,128)(2,1)S(1)} %get-tuple-element.18), channel_id=1, source_target_pairs={{4,12},{6,14},{8,0},{10,2},{12,20},{14,22},{16,8},{18,10},{20,28},... | collective-permute-start | bytes 1179656 | tf_op jit(solution)/shard_map/ppermute | solution.py:315
  32.8 4.9 %collective-permute-done.21 = bf16[1,2,64,1536]{3,2,1,0:T(8,128)(2,1)S(1)} collective-permute-done((bf16[1,2,64,1536]{3,2,1,0:T(8,128)(2,1)S(1)}, bf16[1,2,64,1536]{3,2,1,0:T(8,128)(2,1)S(1)}, u32[]{:S(2)}, u32[]{:S(2)}) %collective-permute-start.21) | collective-permute-done | bytes 393248 | tf_op jit(solution)/shard_map/ppermute | solution.py:315
  37.7 1.5 %collective-permute-start.20 = (bf16[1,4,64,1536]{3,2,1,0:T(8,128)(2,1)}, bf16[1,4,64,1536]{3,2,1,0:T(8,128)(2,1)S(1)}, u32[]{:S(2)}, u32[]{:S(2)}) collective-permute-start(bf16[1,4,64,1536]{3,2,1,0:T(8,128)(2,1)} %ref.3), channel_id=1, source_target_pairs={{0,2},{2,0},{4,6},{6,4},{8,10},{10,8},{12,14},{14,12},{16,18},{18,... | collective-permute-start | bytes 2359304 | tf_op jit(solution)/shard_map/ppermute | solution.py:315
  39.2 1.3 %collective-permute-start.5 = (bf16[1,2,64,1536]{3,2,1,0:T(8,128)(2,1)S(1)}, bf16[1,2,64,1536]{3,2,1,0:T(8,128)(2,1)S(1)}, u32[]{:S(2)}, u32[]{:S(2)}) collective-permute-start(bf16[1,2,64,1536]{3,2,1,0:T(8,128)(2,1)S(1)} %collective-permute-done.4), channel_id=1, source_target_pairs={{0,8},{2,10},{8,16},{10,18},{12,4},{14,6},{16,24},{18,26},{20,12},... | collective-permute-start | bytes 1179656 | tf_op jit(solution)/shard_map/ppermute | solution.py:315
  40.5 1.3 %collective-permute-start.10 = (bf16[1,2,64,1536]{3,2,1,0:T(8,128)(2,1)S(1)}, bf16[1,2,64,1536]{3,2,1,0:T(8,128)(2,1)S(1)}, u32[]{:S(2)}, u32[]{:S(2)}) collective-permute-start(bf16[1,2,64,1536]{3,2,1,0:T(8,128)(2,1)S(1)} %collective-permute-done.9.outer_ref), channel_id=1, source_target_pairs={{0,8},{2,10},{8,16},{10,18},{12,4},{14,6},{16,24},{18,26},{20,12},... | collective-permute-start | bytes 1179656 | tf_op jit(solution)/shard_map/ppermute | solution.py:315
  41.8 5.6 %collective-permute-start.16 = (bf16[1,4,64,1536]{3,2,1,0:T(8,128)(2,1)}, bf16[1,4,64,1536]{3,2,1,0:T(8,128)(2,1)S(1)}, u32[]{:S(2)}, u32[]{:S(2)}) collective-permute-start(bf16[1,4,64,1536]{3,2,1,0:T(8,128)(2,1)} %ref.3), channel_id=1, source_target_pairs={{4,12},{6,14},{8,0},{10,2},{12,20},{14,22},{16,8},{18,10},{20,28},... | collective-permute-start | bytes 2359304 | tf_op jit(solution)/shard_map/ppermute | solution.py:315
  47.5 6.0 %collective-permute-done.5.inner_ref = bf16[1,2,64,1536]{3,2,1,0:T(8,128)(2,1)S(1)} collective-permute-done((bf16[1,2,64,1536]{3,2,1,0:T(8,128)(2,1)S(1)}, bf16[1,2,64,1536]{3,2,1,0:T(8,128)(2,1)S(1)}, u32[]{:S(2)}, u32[]{:S(2)}) %collective-permute-start.5) | collective-permute-done | bytes 393248 | tf_op jit(solution)/shard_map/ppermute | solution.py:315
  53.5 1.1 collective-permute-start.17
  54.5 6.2 %collective-permute-done.10.inner_ref = bf16[1,2,64,1536]{3,2,1,0:T(8,128)(2,1)S(1)} collective-permute-done((bf16[1,2,64,1536]{3,2,1,0:T(8,128)(2,1)S(1)}, bf16[1,2,64,1536]{3,2,1,0:T(8,128)(2,1)S(1)}, u32[]{:S(2)}, u32[]{:S(2)}) %collective-permute-start.10) | collective-permute-done | bytes 393248 | tf_op jit(solution)/shard_map/ppermute | solution.py:315
  60.8 1.3 %collective-permute-start.13 = (bf16[1,2,64,1536]{3,2,1,0:T(8,128)(2,1)S(1)}, bf16[1,2,64,1536]{3,2,1,0:T(8,128)(2,1)S(1)}, u32[]{:S(2)}, u32[]{:S(2)}) collective-permute-start(bf16[1,2,64,1536]{3,2,1,0:T(8,128)(2,1)S(1)} %collective-permute-done.12.outer_ref), channel_id=1, source_target_pairs={{0,8},{2,10},{8,16},{10,18},{12,4},{14,6},{16,24},{18,26},{20,12},... | collective-permute-start | bytes 1179656 | tf_op jit(solution)/shard_map/ppermute | solution.py:315
  62.8 1.5 %collective-permute-start.11 = (bf16[1,2,64,1536]{3,2,1,0:T(8,128)(2,1)S(1)}, bf16[1,2,64,1536]{3,2,1,0:T(8,128)(2,1)S(1)}, u32[]{:S(2)}, u32[]{:S(2)}) collective-permute-start(bf16[1,2,64,1536]{3,2,1,0:T(8,128)(2,1)S(1)} %pick.4), channel_id=1, source_target_pairs={{0,2},{2,0},{4,6},{6,4},{8,10},{10,8},{12,14},{14,12},{16,18},{18,... | collective-permute-start | bytes 1179656 | tf_op jit(solution)/shard_map/ppermute | solution.py:315
  64.3 4.5 %collective-permute-start.3 = (bf16[1,4,64,1536]{3,2,1,0:T(8,128)(2,1)S(1)}, bf16[1,4,64,1536]{3,2,1,0:T(8,128)(2,1)S(1)}, u32[]{:S(2)}, u32[]{:S(2)}) collective-permute-start(bf16[1,4,64,1536]{3,2,1,0:T(8,128)(2,1)S(1)} %collective-permute-done.2), channel_id=1, source_target_pairs={{0,4},{6,2},{8,12},{14,10},{16,20},{22,18},{24,28},{30,26},{1,5},{... | collective-permute-start | bytes 2359304 | tf_op jit(solution)/shard_map/ppermute | solution.py:315
  68.9 3.8 %collective-permute-done.13.inner_ref = bf16[1,2,64,1536]{3,2,1,0:T(8,128)(2,1)S(1)} collective-permute-done((bf16[1,2,64,1536]{3,2,1,0:T(8,128)(2,1)S(1)}, bf16[1,2,64,1536]{3,2,1,0:T(8,128)(2,1)S(1)}, u32[]{:S(2)}, u32[]{:S(2)}) %collective-permute-start.13) | collective-permute-done | bytes 393248 | tf_op jit(solution)/shard_map/ppermute | solution.py:315
  72.7 1.3 %collective-permute-start = (bf16[1,4,64,1536]{3,2,1,0:T(8,128)(2,1)S(1)}, bf16[1,4,64,1536]{3,2,1,0:T(8,128)(2,1)S(1)}, u32[]{:S(2)}, u32[]{:S(2)}) collective-permute-start(bf16[1,4,64,1536]{3,2,1,0:T(8,128)(2,1)S(1)} %copy-done.2), channel_id=1, source_target_pairs={{0,8},{2,10},{8,16},{10,18},{12,4},{14,6},{16,24},{18,26},{20,12},... | collective-permute-start | bytes 2359304 | tf_op jit(solution)/shard_map/ppermute | solution.py:315
  74.0 1.3 %collective-permute-start.1 = (bf16[1,4,64,1536]{3,2,1,0:T(8,128)(2,1)}, bf16[1,4,64,1536]{3,2,1,0:T(8,128)(2,1)S(1)}, u32[]{:S(2)}, u32[]{:S(2)}) collective-permute-start(bf16[1,4,64,1536]{3,2,1,0:T(8,128)(2,1)} %ref.3), channel_id=1, source_target_pairs={{0,8},{2,10},{8,16},{10,18},{12,4},{14,6},{16,24},{18,26},{20,12},... | collective-permute-start | bytes 2359304 | tf_op jit(solution)/shard_map/ppermute | solution.py:315
  75.4 7.3 %collective-permute-done.11 = bf16[1,2,64,1536]{3,2,1,0:T(8,128)(2,1)S(1)} collective-permute-done((bf16[1,2,64,1536]{3,2,1,0:T(8,128)(2,1)S(1)}, bf16[1,2,64,1536]{3,2,1,0:T(8,128)(2,1)S(1)}, u32[]{:S(2)}, u32[]{:S(2)}) %collective-permute-start.11) | collective-permute-done | bytes 393248 | tf_op jit(solution)/shard_map/ppermute | solution.py:315
  82.7 1.3 %collective-permute-start.8 = (bf16[1,2,64,1536]{3,2,1,0:T(8,128)(2,1)S(1)}, bf16[1,2,64,1536]{3,2,1,0:T(8,128)(2,1)S(1)}, u32[]{:S(2)}, u32[]{:S(2)}) collective-permute-start(bf16[1,2,64,1536]{3,2,1,0:T(8,128)(2,1)S(1)} %collective-permute-done.7), channel_id=1, source_target_pairs={{2,6},{4,0},{10,14},{12,8},{18,22},{20,16},{26,30},{28,24},{3,7},{... | collective-permute-start | bytes 1179656 | tf_op jit(solution)/shard_map/ppermute | solution.py:315
  84.0 4.4 %shard_map.57 = (f32[12,8,256]{2,1,0:T(8,128)S(1)}, f32[12,8,256]{2,1,0:T(8,128)S(1)}, f32[12,128,256]{2,1,0:T(8,128)S(1)}) custom-call(s32[1,2,2,6]{3,2,1,0:T(2,128)S(1)} %bitcast.59, s32[1,3]{1,0:T(1,128)S(1)} %copy-done.4, bf16[256,1536]{1,0:T(8,128)(2,1)S(1)} %bitcast.29, bf16[128,1536]{1,0:T(8,128)(2,1)S(1)} %bitcast.51, ...), custom_call_target="tpu_custom_call" | custom-call | flops 1409286144 | bytes 8650752 | tf_op jit(solution)/shard_map/pallas_call | solution.py:234
  88.4 3.1 %shard_map.58 = (f32[12,8,256]{2,1,0:T(8,128)S(1)}, f32[12,8,256]{2,1,0:T(8,128)S(1)}, f32[12,128,256]{2,1,0:T(8,128)S(1)}) custom-call(s32[1,2,2,6]{3,2,1,0:T(2,128)S(1)} %bitcast.60, s32[1,3]{1,0:T(1,128)S(1)} %copy-done.4, bf16[256,1536]{1,0:T(8,128)(2,1)S(1)} %bitcast.30, bf16[128,1536]{1,0:T(8,128)(2,1)S(1)} %bitcast.35, ...), custom_call_target="tpu_custom_call" | custom-call | flops 805306368 | bytes 6291456 | tf_op jit(solution)/shard_map/pallas_call | solution.py:234
  92.3 2.2 %shard_map.59 = (f32[12,8,256]{2,1,0:T(8,128)S(1)}, f32[12,8,256]{2,1,0:T(8,128)S(1)}, f32[12,128,256]{2,1,0:T(8,128)S(1)}) custom-call(s32[1,2,2,6]{3,2,1,0:T(2,128)S(1)} %bitcast.61, s32[1,3]{1,0:T(1,128)S(1)} %copy-done.4, bf16[256,1536]{1,0:T(8,128)(2,1)S(1)} %bitcast.31, bf16[256,1536]{1,0:T(8,128)(2,1)S(1)} %bitcast.41, ...), custom_call_target="tpu_custom_call" | custom-call | flops 402653184 | bytes 4718592 | tf_op jit(solution)/shard_map/pallas_call | solution.py:234
  95.0 14.0 %collective-permute-done.1 = bf16[1,4,64,1536]{3,2,1,0:T(8,128)(2,1)S(1)} collective-permute-done((bf16[1,4,64,1536]{3,2,1,0:T(8,128)(2,1)}, bf16[1,4,64,1536]{3,2,1,0:T(8,128)(2,1)S(1)}, u32[]{:S(2)}, u32[]{:S(2)}) %collective-permute-start.1) | collective-permute-done | bytes 786464 | tf_op jit(solution)/shard_map/ppermute | solution.py:315
  109.0 3.2 %shard_map.60 = bf16[256,1536]{1,0:T(8,128)(2,1)} custom-call(s32[1,2,2,6]{3,2,1,0:T(2,128)S(1)} %bitcast.62, s32[1,3]{1,0:T(1,128)S(1)} %copy-done.4, bf16[256,1536]{1,0:T(8,128)(2,1)S(1)} %bitcast.32, bf16[256,1536]{1,0:T(8,128)(2,1)S(1)} %bitcast.39, bf16[256,1536]{1,0:T(8,128)(2,1)S(1)} %bitcast.40, f32[12,8,256]{2,1,0:T(8,128)S(1)} %get-tuple-element.28.refs_3_, ...), custom_call_target="tpu_custom_call" | custom-call | flops 402653184 | bytes 4718592 | tf_op jit(solution)/shard_map/pallas_call | solution.py:234
  (31 shorter events, 3.0 us)
Async XLA Ops:
  0.0 1.1 %copy-start.1 = (bf16[1,4,64,1536]{3,2,1,0:T(8,128)(2,1)S(1)}, bf16[1,4,64,1536]{3,2,1,0:T(8,128)(2,1)}, u32[]{:S(2)}) copy-start(bf16[1,4,64,1536]{3,2,1,0:T(8,128)(2,1)} %ref.2) | copy-start | bytes 2359300
  1.1 5.2 %copy-start.2 = (bf16[1,4,64,1536]{3,2,1,0:T(8,128)(2,1)S(1)}, bf16[1,4,64,1536]{3,2,1,0:T(8,128)(2,1)}, u32[]{:S(2)}) copy-start(bf16[1,4,64,1536]{3,2,1,0:T(8,128)(2,1)} %ref.2) | copy-start | bytes 2359300
  1.5 12.1 %collective-permute-start.4 = (bf16[1,2,64,1536]{3,2,1,0:T(8,128)(2,1)S(1)}, bf16[1,2,64,1536]{3,2,1,0:T(8,128)(2,1)S(1)}, u32[]{:S(2)}, u32[]{:S(2)}) collective-permute-start(bf16[1,2,64,1536]{3,2,1,0:T(8,128)(2,1)S(1)} %get-tuple-element.18), channel_id=1, source_target_pairs={{0,4},{2,6},{4,0},{6,2},{8,12},{10,14},{12,8},{14,10},{16,20},{18,... | collective-permute-start | bytes 1179656 | tf_op jit(solution)/shard_map/ppermute | solution.py:315
  4.3 17.8 %collective-permute-start.9 = (bf16[1,2,64,1536]{3,2,1,0:T(8,128)(2,1)S(1)}, bf16[1,2,64,1536]{3,2,1,0:T(8,128)(2,1)S(1)}, u32[]{:S(2)}, u32[]{:S(2)}) collective-permute-start(bf16[1,2,64,1536]{3,2,1,0:T(8,128)(2,1)S(1)} %get-tuple-element.20), channel_id=1, source_target_pairs={{0,4},{2,6},{4,0},{6,2},{8,12},{10,14},{12,8},{14,10},{16,20},{18,... | collective-permute-start | bytes 1179656 | tf_op jit(solution)/shard_map/ppermute | solution.py:315
  4.8 25.6 %collective-permute-start.12 = (bf16[1,2,64,1536]{3,2,1,0:T(8,128)(2,1)S(1)}, bf16[1,2,64,1536]{3,2,1,0:T(8,128)(2,1)S(1)}, u32[]{:S(2)}, u32[]{:S(2)}) collective-permute-start(bf16[1,2,64,1536]{3,2,1,0:T(8,128)(2,1)S(1)} %get-tuple-element.21), channel_id=1, source_target_pairs={{0,4},{2,6},{4,0},{6,2},{8,12},{10,14},{12,8},{14,10},{16,20},{18,... | collective-permute-start | bytes 1179656 | tf_op jit(solution)/shard_map/ppermute | solution.py:315
  6.4 34.2 %collective-permute-start.2 = (bf16[1,4,64,1536]{3,2,1,0:T(8,128)(2,1)S(1)}, bf16[1,4,64,1536]{3,2,1,0:T(8,128)(2,1)S(1)}, u32[]{:S(2)}, u32[]{:S(2)}) collective-permute-start(bf16[1,4,64,1536]{3,2,1,0:T(8,128)(2,1)S(1)} %copy-done.2), channel_id=1, source_target_pairs={{0,2},{2,0},{4,6},{6,4},{8,10},{10,8},{12,14},{14,12},{16,18},{18,... | collective-permute-start | bytes 2359304 | tf_op jit(solution)/shard_map/ppermute | solution.py:315
  7.8 34.0 %collective-permute-start.18 = (bf16[1,4,64,1536]{3,2,1,0:T(8,128)(2,1)S(1)}, bf16[1,4,64,1536]{3,2,1,0:T(8,128)(2,1)S(1)}, u32[]{:S(2)}, u32[]{:S(2)}) collective-permute-start(bf16[1,4,64,1536]{3,2,1,0:T(8,128)(2,1)S(1)} %copy-done.2), channel_id=1, source_target_pairs={{0,1},{1,0},{2,3},{3,2},{4,5},{5,4},{6,7},{7,6},{8,9},{9,8},{10,11... | collective-permute-start | bytes 2359304 | tf_op jit(solution)/shard_map/ppermute | solution.py:315
  13.6 70.4 %copy-start = (bf16[1,4,64,1536]{3,2,1,0:T(8,128)(2,1)S(1)}, bf16[1,4,64,1536]{3,2,1,0:T(8,128)(2,1)}, u32[]{:S(2)}) copy-start(bf16[1,4,64,1536]{3,2,1,0:T(8,128)(2,1)} %param.5) | copy-start | bytes 2359300
  13.6 70.4 %copy-start.3 = (s32[1,2,6,2]{2,3,1,0:T(2,128)S(1)}, s32[1,2,6,2]{2,3,1,0:T(2,128)}, u32[]{:S(2)}) copy-start(s32[1,2,6,2]{2,3,1,0:T(2,128)} %param.8) | copy-start | bytes 292
  13.6 70.4 %copy-start.4 = (s32[1,3]{1,0:T(1,128)S(1)}, s32[1,3]{1,0:T(1,128)}, u32[]{:S(2)}) copy-start(s32[1,3]{1,0:T(1,128)} %density_ref.7) | copy-start | bytes 40
  13.6 24.1 %collective-permute-start.21 = (bf16[1,2,64,1536]{3,2,1,0:T(8,128)(2,1)S(1)}, bf16[1,2,64,1536]{3,2,1,0:T(8,128)(2,1)S(1)}, u32[]{:S(2)}, u32[]{:S(2)}) collective-permute-start(bf16[1,2,64,1536]{3,2,1,0:T(8,128)(2,1)S(1)} %get-tuple-element.19), channel_id=1, source_target_pairs={{0,4},{2,6},{4,0},{6,2},{8,12},{10,14},{12,8},{14,10},{16,20},{18,... | collective-permute-start | bytes 1179656 | tf_op jit(solution)/shard_map/ppermute | solution.py:315
  22.0 15.7 %collective-permute-start.6 = (bf16[1,2,64,1536]{3,2,1,0:T(8,128)(2,1)S(1)}, bf16[1,2,64,1536]{3,2,1,0:T(8,128)(2,1)S(1)}, u32[]{:S(2)}, u32[]{:S(2)}) collective-permute-start(bf16[1,2,64,1536]{3,2,1,0:T(8,128)(2,1)S(1)} %get-tuple-element.19), channel_id=1, source_target_pairs={{4,12},{6,14},{8,0},{10,2},{12,20},{14,22},{16,8},{18,10},{20,28},... | collective-permute-start | bytes 1179656 | tf_op jit(solution)/shard_map/ppermute | solution.py:315
  30.4 8.8 %collective-permute-start.15 = (bf16[1,2,64,1536]{3,2,1,0:T(8,128)(2,1)S(1)}, bf16[1,2,64,1536]{3,2,1,0:T(8,128)(2,1)S(1)}, u32[]{:S(2)}, u32[]{:S(2)}) collective-permute-start(bf16[1,2,64,1536]{3,2,1,0:T(8,128)(2,1)S(1)} %get-tuple-element.18), channel_id=1, source_target_pairs={{4,12},{6,14},{8,0},{10,2},{12,20},{14,22},{16,8},{18,10},{20,28},... | collective-permute-start | bytes 1179656 | tf_op jit(solution)/shard_map/ppermute | solution.py:315
  37.7 24.5 %collective-permute-start.19 = (bf16[1,4,64,1536]{3,2,1,0:T(8,128)(2,1)}, bf16[1,4,64,1536]{3,2,1,0:T(8,128)(2,1)S(1)}, u32[]{:S(2)}, u32[]{:S(2)}) collective-permute-start(bf16[1,4,64,1536]{3,2,1,0:T(8,128)(2,1)} %ref.3), channel_id=1, source_target_pairs={{0,1},{1,0},{2,3},{3,2},{4,5},{5,4},{6,7},{7,6},{8,9},{9,8},{10,11... | collective-permute-start | bytes 2359304 | tf_op jit(solution)/shard_map/ppermute | solution.py:315
  37.7 25.1 %collective-permute-start.20 = (bf16[1,4,64,1536]{3,2,1,0:T(8,128)(2,1)}, bf16[1,4,64,1536]{3,2,1,0:T(8,128)(2,1)S(1)}, u32[]{:S(2)}, u32[]{:S(2)}) collective-permute-start(bf16[1,4,64,1536]{3,2,1,0:T(8,128)(2,1)} %ref.3), channel_id=1, source_target_pairs={{0,2},{2,0},{4,6},{6,4},{8,10},{10,8},{12,14},{14,12},{16,18},{18,... | collective-permute-start | bytes 2359304 | tf_op jit(solution)/shard_map/ppermute | solution.py:315
  39.2 14.3 %collective-permute-start.5 = (bf16[1,2,64,1536]{3,2,1,0:T(8,128)(2,1)S(1)}, bf16[1,2,64,1536]{3,2,1,0:T(8,128)(2,1)S(1)}, u32[]{:S(2)}, u32[]{:S(2)}) collective-permute-start(bf16[1,2,64,1536]{3,2,1,0:T(8,128)(2,1)S(1)} %collective-permute-done.4), channel_id=1, source_target_pairs={{0,8},{2,10},{8,16},{10,18},{12,4},{14,6},{16,24},{18,26},{20,12},... | collective-permute-start | bytes 1179656 | tf_op jit(solution)/shard_map/ppermute | solution.py:315
  40.5 20.3 %collective-permute-start.10 = (bf16[1,2,64,1536]{3,2,1,0:T(8,128)(2,1)S(1)}, bf16[1,2,64,1536]{3,2,1,0:T(8,128)(2,1)S(1)}, u32[]{:S(2)}, u32[]{:S(2)}) collective-permute-start(bf16[1,2,64,1536]{3,2,1,0:T(8,128)(2,1)S(1)} %collective-permute-done.9.outer_ref), channel_id=1, source_target_pairs={{0,8},{2,10},{8,16},{10,18},{12,4},{14,6},{16,24},{18,26},{20,12},... | collective-permute-start | bytes 1179656 | tf_op jit(solution)/shard_map/ppermute | solution.py:315
  41.8 32.1 %collective-permute-start.16 = (bf16[1,4,64,1536]{3,2,1,0:T(8,128)(2,1)}, bf16[1,4,64,1536]{3,2,1,0:T(8,128)(2,1)S(1)}, u32[]{:S(2)}, u32[]{:S(2)}) collective-permute-start(bf16[1,4,64,1536]{3,2,1,0:T(8,128)(2,1)} %ref.3), channel_id=1, source_target_pairs={{4,12},{6,14},{8,0},{10,2},{12,20},{14,22},{16,8},{18,10},{20,28},... | collective-permute-start | bytes 2359304 | tf_op jit(solution)/shard_map/ppermute | solution.py:315
  53.5 10.8 %collective-permute-start.17 = (bf16[1,2,64,1536]{3,2,1,0:T(8,128)(2,1)S(1)}, bf16[1,2,64,1536]{3,2,1,0:T(8,128)(2,1)S(1)}, u32[]{:S(2)}, u32[]{:S(2)}) collective-permute-start(bf16[1,2,64,1536]{3,2,1,0:T(8,128)(2,1)S(1)} %collective-permute-done.6.outer_ref), channel_id=1, source_target_pairs={{0,4},{2,6},{4,0},{6,2},{8,12},{10,14},{12,8},{14,10},{16,20},{18,... | collective-permute-start | bytes 1179656 | tf_op jit(solution)/shard_map/ppermute | solution.py:315
  60.8 11.9 %collective-permute-start.13 = (bf16[1,2,64,1536]{3,2,1,0:T(8,128)(2,1)S(1)}, bf16[1,2,64,1536]{3,2,1,0:T(8,128)(2,1)S(1)}, u32[]{:S(2)}, u32[]{:S(2)}) collective-permute-start(bf16[1,2,64,1536]{3,2,1,0:T(8,128)(2,1)S(1)} %collective-permute-done.12.outer_ref), channel_id=1, source_target_pairs={{0,8},{2,10},{8,16},{10,18},{12,4},{14,6},{16,24},{18,26},{20,12},... | collective-permute-start | bytes 1179656 | tf_op jit(solution)/shard_map/ppermute | solution.py:315
  62.2 13.1 %collective-permute-start.7 = (bf16[1,2,64,1536]{3,2,1,0:T(8,128)(2,1)S(1)}, bf16[1,2,64,1536]{3,2,1,0:T(8,128)(2,1)S(1)}, u32[]{:S(2)}, u32[]{:S(2)}) collective-permute-start(bf16[1,2,64,1536]{3,2,1,0:T(8,128)(2,1)S(1)} %pick.3), channel_id=1, source_target_pairs={{0,2},{2,0},{4,6},{6,4},{8,10},{10,8},{12,14},{14,12},{16,18},{18,... | collective-permute-start | bytes 1179656 | tf_op jit(solution)/shard_map/ppermute | solution.py:315
  62.8 19.9 %collective-permute-start.11 = (bf16[1,2,64,1536]{3,2,1,0:T(8,128)(2,1)S(1)}, bf16[1,2,64,1536]{3,2,1,0:T(8,128)(2,1)S(1)}, u32[]{:S(2)}, u32[]{:S(2)}) collective-permute-start(bf16[1,2,64,1536]{3,2,1,0:T(8,128)(2,1)S(1)} %pick.4), channel_id=1, source_target_pairs={{0,2},{2,0},{4,6},{6,4},{8,10},{10,8},{12,14},{14,12},{16,18},{18,... | collective-permute-start | bytes 1179656 | tf_op jit(solution)/shard_map/ppermute | solution.py:315
  64.3 28.0 %collective-permute-start.3 = (bf16[1,4,64,1536]{3,2,1,0:T(8,128)(2,1)S(1)}, bf16[1,4,64,1536]{3,2,1,0:T(8,128)(2,1)S(1)}, u32[]{:S(2)}, u32[]{:S(2)}) collective-permute-start(bf16[1,4,64,1536]{3,2,1,0:T(8,128)(2,1)S(1)} %collective-permute-done.2), channel_id=1, source_target_pairs={{0,4},{6,2},{8,12},{14,10},{16,20},{22,18},{24,28},{30,26},{1,5},{... | collective-permute-start | bytes 2359304 | tf_op jit(solution)/shard_map/ppermute | solution.py:315
  72.7 22.3 %collective-permute-start = (bf16[1,4,64,1536]{3,2,1,0:T(8,128)(2,1)S(1)}, bf16[1,4,64,1536]{3,2,1,0:T(8,128)(2,1)S(1)}, u32[]{:S(2)}, u32[]{:S(2)}) collective-permute-start(bf16[1,4,64,1536]{3,2,1,0:T(8,128)(2,1)S(1)} %copy-done.2), channel_id=1, source_target_pairs={{0,8},{2,10},{8,16},{10,18},{12,4},{14,6},{16,24},{18,26},{20,12},... | collective-permute-start | bytes 2359304 | tf_op jit(solution)/shard_map/ppermute | solution.py:315
  74.0 35.0 %collective-permute-start.1 = (bf16[1,4,64,1536]{3,2,1,0:T(8,128)(2,1)}, bf16[1,4,64,1536]{3,2,1,0:T(8,128)(2,1)S(1)}, u32[]{:S(2)}, u32[]{:S(2)}) collective-permute-start(bf16[1,4,64,1536]{3,2,1,0:T(8,128)(2,1)} %ref.3), channel_id=1, source_target_pairs={{0,8},{2,10},{8,16},{10,18},{12,4},{14,6},{16,24},{18,26},{20,12},... | collective-permute-start | bytes 2359304 | tf_op jit(solution)/shard_map/ppermute | solution.py:315
  75.3 16.2 %collective-permute-start.14 = (bf16[1,2,64,1536]{3,2,1,0:T(8,128)(2,1)S(1)}, bf16[1,2,64,1536]{3,2,1,0:T(8,128)(2,1)S(1)}, u32[]{:S(2)}, u32[]{:S(2)}) collective-permute-start(bf16[1,2,64,1536]{3,2,1,0:T(8,128)(2,1)S(1)} %pick.5), channel_id=1, source_target_pairs={{0,2},{2,0},{4,6},{6,4},{8,10},{10,8},{12,14},{14,12},{16,18},{18,... | collective-permute-start | bytes 1179656 | tf_op jit(solution)/shard_map/ppermute | solution.py:315
  82.7 9.7 %collective-permute-start.8 = (bf16[1,2,64,1536]{3,2,1,0:T(8,128)(2,1)S(1)}, bf16[1,2,64,1536]{3,2,1,0:T(8,128)(2,1)S(1)}, u32[]{:S(2)}, u32[]{:S(2)}) collective-permute-start(bf16[1,2,64,1536]{3,2,1,0:T(8,128)(2,1)S(1)} %collective-permute-done.7), channel_id=1, source_target_pairs={{2,6},{4,0},{10,14},{12,8},{18,22},{20,16},{26,30},{28,24},{3,7},{... | collective-permute-start | bytes 1179656 | tf_op jit(solution)/shard_map/ppermute | solution.py:315

commit v6 on v5

--- a/solution.py
+++ b/solution.py
@@ -13,6 +13,7 @@
 GROUP = 2 ** (OFFSETS - 1)
 SUBLANES = 8
 UNROLL = 2
+LAST_UNROLL = 6
 VMEM_LIMIT = 16 * 2**20
 NEG = -1e30
 SCALE2 = math.log2(math.e) / math.sqrt(HEAD_DIM)
@@ -65,9 +66,11 @@
     return parts[0] if len(parts) == 1 else jnp.concatenate(parts, axis=axis)
 
 
-def stage_call(q, entries, state, lists, density, final):
+def stage_call(q, entries, state, lists, density, ahead=()):
     tokens, features = q.shape
     heads = features // HEAD_DIM
+    mixed_count = len(entries)
+    entries = list(entries) + [(kind, k, ()) for kind, k in ahead]
     kinds = [entry[0] for entry in entries]
     starts = [0]
     for _, k, v in entries:
@@ -134,7 +137,7 @@
         def stacked(h, part):
             cols = columns(h)
             pieces = []
-            for i, kind in enumerate(kinds):
+            for i, kind in enumerate(kinds if part == 0 else kinds[:mixed_count]):
                 rows = rows_of.get(kind, slice(None))
                 refs_i = kv[starts[2 * i + part] : starts[2 * i + part + 1]]
                 if kind == "GE" and part == 0:
@@ -161,14 +164,17 @@
                 tops.append(jnp.max(top, axis=0, keepdims=True))
             return join(tops, 1)
 
-        def weigh(src, dst, top):
+        def weigh(h, src, dst, top):
             for half in range(halves):
                 cols = slice(half * edge, (half + 1) * edge)
                 shift = top[:, cols] * SCALE2
                 for row, rows, allow in bands_of:
                     off = shift if allow[half] is None else jnp.where(allow[half], shift, -NEG)
                     w = jnp.exp2(src[row : row + rows, cols] * SCALE2 - off)
-                    dst[row : row + rows, cols] = w.astype(jnp.bfloat16)
+                    if row < keys:
+                        dst[row : row + rows, cols] = w.astype(jnp.bfloat16)
+                    else:
+                        rest[3][h, row - keys : row - keys + rows, cols] = w.astype(jnp.bfloat16)
 
         def mix(h, src, top):
             v = jnp.transpose(stacked(h, 1))
@@ -179,13 +185,9 @@
                 decay = jnp.exp2((old_refs[0][h][0:1] - top) * SCALE2)
                 total = total + old_refs[1][h] * decay
                 acc = acc + old_refs[2][h] * decay
-            if final:
-                scaled = acc * (1.0 / total[0:1])
-                rest[0][:, columns(h)] = jnp.transpose(scaled.astype(jnp.bfloat16))
-            else:
-                rest[0][h] = jnp.broadcast_to(top, (SUBLANES, tokens))
-                rest[1][h] = total
-                rest[2][h] = acc
+            rest[0][h] = jnp.broadcast_to(top, (SUBLANES, tokens))
+            rest[1][h] = total
+            rest[2][h] = acc
 
         s_refs, w_refs = scratch[:2], scratch[2:]
 
@@ -195,7 +197,7 @@
                     mix(h + n, w_refs[n], ready[n])
             if next_ready is not None:
                 for n in range(2):
-                    weigh(s_refs[n], w_refs[n], next_ready[n])
+                    weigh(h + 2 + n, s_refs[n], w_refs[n], next_ready[n])
             if ahead:
                 return tuple(scores(h + 4 + n, s_refs[n]) for n in range(2))
             return None
@@ -215,35 +217,69 @@
     smem = pl.BlockSpec(memory_space=pltpu.SMEM)
     vmem = pl.BlockSpec(memory_space=pltpu.VMEM)
     operands = [lists, density, q]
-    keys = 0
+    keys = more = 0
     for kind, k, v in entries:
         operands += [*k, *v]
-        keys += edge if kind in ("before", "after", "other") else tokens
+        count = edge if kind in ("before", "after", "other") else tokens
+        keys, more = (keys + count, more) if len(v) > 0 else (keys, more + count)
     if state is not None:
         operands += list(state)
     operands = operands[:2] + [
         pltpu.with_memory_space_constraint(value, pltpu.VMEM) for value in operands[2:]
     ]
     specs = [smem, smem] + [vmem] * (len(operands) - 2)
-    if final:
-        outs, out_specs = jax.ShapeDtypeStruct((tokens, features), jnp.bfloat16), vmem
-    else:
-        small = pltpu.VMEM((heads, SUBLANES, tokens), jnp.float32)
-        large = pltpu.VMEM((heads, HEAD_DIM, tokens), jnp.float32)
-        outs, out_specs = (small, small, large), (vmem, vmem, vmem)
+    small = pltpu.VMEM((heads, SUBLANES, tokens), jnp.float32)
+    large = pltpu.VMEM((heads, HEAD_DIM, tokens), jnp.float32)
+    outs = [small, small, large]
+    if more > 0:
+        outs.append(pltpu.VMEM((heads, more, tokens), jnp.bfloat16))
     return pl.pallas_call(
         kernel,
         in_specs=specs,
-        out_specs=out_specs,
+        out_specs=[vmem] * len(outs),
         out_shape=outs,
-        scratch_shapes=[pltpu.VMEM((keys, tokens), jnp.float32)] * 2
+        scratch_shapes=[pltpu.VMEM((keys + more, tokens), jnp.float32)] * 2
         + [pltpu.VMEM((keys, tokens), jnp.bfloat16)] * 2,
         compiler_params=pltpu.CompilerParams(vmem_limit_bytes=VMEM_LIMIT),
         cost_estimate=pl.CostEstimate(
-            flops=4 * tokens * keys * features,
+            flops=4 * tokens * (keys + more) * features,
             transcendentals=tokens * keys * heads,
             bytes_accessed=2 * features * (2 * keys + 4 * tokens),
         ),
+    )(*operands)
+
+
+def last_call(value_rows, weights, weights_top, state):
+    tokens, features = value_rows.shape
+    heads = features // HEAD_DIM
+
+    def kernel(v_ref, w_ref, w_top_ref, top_ref, total_ref, acc_ref, out_ref):
+        def one_head(h, carry):
+            cols = pl.ds(pl.multiple_of(h * HEAD_DIM, HEAD_DIM), HEAD_DIM)
+            v = jnp.transpose(v_ref[:, cols])
+            ones = jnp.ones((2 * SUBLANES, v.shape[1]), jnp.bfloat16)
+            mixed = contract(join([v, ones], 0), w_ref[h], ((1,), (0,)))
+            decay = jnp.exp2((w_top_ref[h][0:1] - top_ref[h][0:1]) * SCALE2)
+            total = total_ref[h][0:1] + mixed[HEAD_DIM : HEAD_DIM + 1] * decay
+            inverse = 1.0 / total
+            acc = acc_ref[h] * inverse + mixed[:HEAD_DIM] * (decay * inverse)
+            out_ref[:, cols] = jnp.transpose(acc.astype(jnp.bfloat16))
+            return carry
+
+        lax.fori_loop(0, heads, one_head, 0, unroll=LAST_UNROLL)
+
+    vmem = pl.BlockSpec(memory_space=pltpu.VMEM)
+    operands = [
+        pltpu.with_memory_space_constraint(value, pltpu.VMEM)
+        for value in (value_rows, weights, weights_top, *state)
+    ]
+    return pl.pallas_call(
+        kernel,
+        in_specs=[vmem] * len(operands),
+        out_specs=vmem,
+        out_shape=jax.ShapeDtypeStruct((tokens, features), jnp.bfloat16),
+        compiler_params=pltpu.CompilerParams(vmem_limit_bytes=VMEM_LIMIT),
+        name="last",
     )(*operands)
 
 
@@ -367,9 +403,8 @@
         None,
         lists,
         density,
-        False,
     )
-    state = stage_call(
+    *state, weights = stage_call(
         q,
         [
             ("O", (flat(o_k0), flat(o_k1)), (flat(o_v),)),
@@ -378,19 +413,17 @@
         state,
         lists,
         density,
-        False,
+        [("B", (flat(b_k),))],
     )
+    weights_top = state[0]
     state = stage_call(
         q,
         [("GE", (flat(g_k), flat(e_k0), flat(r_k)), (flat(r_v0), flat(r_v1)))],
         state,
         lists,
         density,
-        False,
     )
-    result = stage_call(
-        q, [("B", (flat(b_k),), (flat(b_v),))], state, lists, density, True
-    )
+    result = last_call(flat(b_v), weights, weights_top, state)
     return result.reshape(1, rows_dev, width, features)
 
 

time: 113 us -> 121 us (1.071)
  the two profiles are of different devices: /device:TPU:24 before, /device:TPU:0 now
where the time goes in v6:
time: 121 us
  waiting for transfers between devices  64.1 us (53%)
  starting transfers between devices  41.3 us (34%)
  Pallas kernels  13.8 us (11%)
    ppermute x22, waiting for transfers between devices, send(): return lax.ppermute(value, axis, pairs)  64.1 us
    ppermute x22, starting transfers between devices, send(): return lax.ppermute(value, axis, pairs)  41.3 us
    pallas_call x3, Pallas kernels, stage_call(): pl.pallas_call(kernel, in_specs=specs, out_specs=[vmem] * len(outs), out_...  10.4 us
  transfers between devices with their start and end apart: 22, of which 9 were waited for; matrix products, arithmetic and copies ran while one was open for 0% of the time, Pallas kernels for 10%

profile of v6, /device:TPU:0, one launch (start us, length us, event | category | flops | bytes accessed | tf_op | source)
XLA Modules:
  0.0 120.6 jit_solution(7828986783823628322)
XLA Ops:
  0.0 1.1 copy-done.1
  1.5 3.1 %collective-permute-start.5 = (bf16[1,2,64,1536]{3,2,1,0:T(8,128)(2,1)S(1)}, bf16[1,2,64,1536]{3,2,1,0:T(8,128)(2,1)S(1)}, u32[]{:S(2)}, u32[]{:S(2)}) collective-permute-start(bf16[1,2,64,1536]{3,2,1,0:T(8,128)(2,1)S(1)} %get-tuple-element.20), channel_id=1, source_target_pairs={{0,4},{2,6},{4,0},{6,2},{8,12},{10,14},{12,8},{14,10},{16,20},{18,... | collective-permute-start | bytes 1179656 | tf_op jit(solution)/shard_map/ppermute | solution.py:351
  4.6 1.1 shard_map.56
  5.8 2.0 %collective-permute-start.9 = (bf16[1,2,64,1536]{3,2,1,0:T(8,128)(2,1)S(1)}, bf16[1,2,64,1536]{3,2,1,0:T(8,128)(2,1)S(1)}, u32[]{:S(2)}, u32[]{:S(2)}) collective-permute-start(bf16[1,2,64,1536]{3,2,1,0:T(8,128)(2,1)S(1)} %get-tuple-element.22), channel_id=1, source_target_pairs={{0,4},{2,6},{4,0},{6,2},{8,12},{10,14},{12,8},{14,10},{16,20},{18,... | collective-permute-start | bytes 1179656 | tf_op jit(solution)/shard_map/ppermute | solution.py:351
  7.9 1.4 %collective-permute-start.1 = (bf16[1,2,64,1536]{3,2,1,0:T(8,128)(2,1)S(1)}, bf16[1,2,64,1536]{3,2,1,0:T(8,128)(2,1)S(1)}, u32[]{:S(2)}, u32[]{:S(2)}) collective-permute-start(bf16[1,2,64,1536]{3,2,1,0:T(8,128)(2,1)S(1)} %get-tuple-element.19), channel_id=1, source_target_pairs={{4,12},{6,14},{8,0},{10,2},{12,20},{14,22},{16,8},{18,10},{20,28},... | collective-permute-start | bytes 1179656 | tf_op jit(solution)/shard_map/ppermute | solution.py:351
  9.3 5.2 %collective-permute-done.5 = bf16[1,2,64,1536]{3,2,1,0:T(8,128)(2,1)S(1)} collective-permute-done((bf16[1,2,64,1536]{3,2,1,0:T(8,128)(2,1)S(1)}, bf16[1,2,64,1536]{3,2,1,0:T(8,128)(2,1)S(1)}, u32[]{:S(2)}, u32[]{:S(2)}) %collective-permute-start.5) | collective-permute-done | bytes 393248 | tf_op jit(solution)/shard_map/ppermute | solution.py:351
  14.6 2.0 %collective-permute-start.14 = (bf16[1,4,64,1536]{3,2,1,0:T(8,128)(2,1)S(1)}, bf16[1,4,64,1536]{3,2,1,0:T(8,128)(2,1)S(1)}, u32[]{:S(2)}, u32[]{:S(2)}) collective-permute-start(bf16[1,4,64,1536]{3,2,1,0:T(8,128)(2,1)S(1)} %copy-done.2), channel_id=1, source_target_pairs={{0,2},{2,0},{4,6},{6,4},{8,10},{10,8},{12,14},{14,12},{16,18},{18,... | collective-permute-start | bytes 2359304 | tf_op jit(solution)/shard_map/ppermute | solution.py:351
  16.6 6.4 %collective-permute-done.7.outer_ref = bf16[1,2,64,1536]{3,2,1,0:T(8,128)(2,1)S(1)} collective-permute-done((bf16[1,2,64,1536]{3,2,1,0:T(8,128)(2,1)S(1)}, bf16[1,2,64,1536]{3,2,1,0:T(8,128)(2,1)S(1)}, u32[]{:S(2)}, u32[]{:S(2)}) %collective-permute-start.7) | collective-permute-done | bytes 393248 | tf_op jit(solution)/shard_map/ppermute | solution.py:351
  23.0 8.4 %collective-permute-done.9.outer_ref = bf16[1,2,64,1536]{3,2,1,0:T(8,128)(2,1)S(1)} collective-permute-done((bf16[1,2,64,1536]{3,2,1,0:T(8,128)(2,1)S(1)}, bf16[1,2,64,1536]{3,2,1,0:T(8,128)(2,1)S(1)}, u32[]{:S(2)}, u32[]{:S(2)}) %collective-permute-start.9) | collective-permute-done | bytes 393248 | tf_op jit(solution)/shard_map/ppermute | solution.py:351
  31.4 7.6 %collective-permute-done.16 = bf16[1,2,64,1536]{3,2,1,0:T(8,128)(2,1)S(1)} collective-permute-done((bf16[1,2,64,1536]{3,2,1,0:T(8,128)(2,1)S(1)}, bf16[1,2,64,1536]{3,2,1,0:T(8,128)(2,1)S(1)}, u32[]{:S(2)}, u32[]{:S(2)}) %collective-permute-start.16) | collective-permute-done | bytes 393248 | tf_op jit(solution)/shard_map/ppermute | solution.py:351
  39.0 1.7 %collective-permute-start.15 = (bf16[1,4,64,1536]{3,2,1,0:T(8,128)(2,1)}, bf16[1,4,64,1536]{3,2,1,0:T(8,128)(2,1)S(1)}, u32[]{:S(2)}, u32[]{:S(2)}) collective-permute-start(bf16[1,4,64,1536]{3,2,1,0:T(8,128)(2,1)} %ref.3), channel_id=1, source_target_pairs={{0,2},{2,0},{4,6},{6,4},{8,10},{10,8},{12,14},{14,12},{16,18},{18,... | collective-permute-start | bytes 2359304 | tf_op jit(solution)/shard_map/ppermute | solution.py:351
  40.7 1.3 %collective-permute-start.2 = (bf16[1,2,64,1536]{3,2,1,0:T(8,128)(2,1)S(1)}, bf16[1,2,64,1536]{3,2,1,0:T(8,128)(2,1)S(1)}, u32[]{:S(2)}, u32[]{:S(2)}) collective-permute-start(bf16[1,2,64,1536]{3,2,1,0:T(8,128)(2,1)S(1)} %get-tuple-element.20), channel_id=1, source_target_pairs={{4,12},{6,14},{8,0},{10,2},{12,20},{14,22},{16,8},{18,10},{20,28},... | collective-permute-start | bytes 1179656 | tf_op jit(solution)/shard_map/ppermute | solution.py:351
  42.0 10.3 %collective-permute-done.2 = bf16[1,2,64,1536]{3,2,1,0:T(8,128)(2,1)S(1)} collective-permute-done((bf16[1,2,64,1536]{3,2,1,0:T(8,128)(2,1)S(1)}, bf16[1,2,64,1536]{3,2,1,0:T(8,128)(2,1)S(1)}, u32[]{:S(2)}, u32[]{:S(2)}) %collective-permute-start.2) | collective-permute-done | bytes 393248 | tf_op jit(solution)/shard_map/ppermute | solution.py:351
  52.3 3.5 %collective-permute-start.6 = (bf16[1,2,64,1536]{3,2,1,0:T(8,128)(2,1)S(1)}, bf16[1,2,64,1536]{3,2,1,0:T(8,128)(2,1)S(1)}, u32[]{:S(2)}, u32[]{:S(2)}) collective-permute-start(bf16[1,2,64,1536]{3,2,1,0:T(8,128)(2,1)S(1)} %collective-permute-done.5), channel_id=1, source_target_pairs={{0,8},{2,10},{8,16},{10,18},{12,4},{14,6},{16,24},{18,26},{20,12},... | collective-permute-start | bytes 1179656 | tf_op jit(solution)/shard_map/ppermute | solution.py:351
  55.8 3.5 %collective-permute-start.11 = (bf16[1,4,64,1536]{3,2,1,0:T(8,128)(2,1)S(1)}, bf16[1,4,64,1536]{3,2,1,0:T(8,128)(2,1)S(1)}, u32[]{:S(2)}, u32[]{:S(2)}) collective-permute-start(bf16[1,4,64,1536]{3,2,1,0:T(8,128)(2,1)S(1)} %copy-done.2), channel_id=1, source_target_pairs={{0,8},{2,10},{8,16},{10,18},{12,4},{14,6},{16,24},{18,26},{20,12},... | collective-permute-start | bytes 2359304 | tf_op jit(solution)/shard_map/ppermute | solution.py:351
  59.3 1.3 %collective-permute-start.3 = (bf16[1,4,64,1536]{3,2,1,0:T(8,128)(2,1)}, bf16[1,4,64,1536]{3,2,1,0:T(8,128)(2,1)S(1)}, u32[]{:S(2)}, u32[]{:S(2)}) collective-permute-start(bf16[1,4,64,1536]{3,2,1,0:T(8,128)(2,1)} %ref.3), channel_id=1, source_target_pairs={{4,12},{6,14},{8,0},{10,2},{12,20},{14,22},{16,8},{18,10},{20,28},... | collective-permute-start | bytes 2359304 | tf_op jit(solution)/shard_map/ppermute | solution.py:351
  60.7 0.7 collective-permute-start.4
  61.3 4.0 %collective-permute-start.8 = (bf16[1,2,64,1536]{3,2,1,0:T(8,128)(2,1)S(1)}, bf16[1,2,64,1536]{3,2,1,0:T(8,128)(2,1)S(1)}, u32[]{:S(2)}, u32[]{:S(2)}) collective-permute-start(bf16[1,2,64,1536]{3,2,1,0:T(8,128)(2,1)S(1)} %collective-permute-done.7.outer_ref), channel_id=1, source_target_pairs={{0,8},{2,10},{8,16},{10,18},{12,4},{14,6},{16,24},{18,26},{20,12},... | collective-permute-start | bytes 1179656 | tf_op jit(solution)/shard_map/ppermute | solution.py:351
  65.3 4.3 %collective-permute-start.10 = (bf16[1,2,64,1536]{3,2,1,0:T(8,128)(2,1)S(1)}, bf16[1,2,64,1536]{3,2,1,0:T(8,128)(2,1)S(1)}, u32[]{:S(2)}, u32[]{:S(2)}) collective-permute-start(bf16[1,2,64,1536]{3,2,1,0:T(8,128)(2,1)S(1)} %collective-permute-done.9.outer_ref), channel_id=1, source_target_pairs={{0,8},{2,10},{8,16},{10,18},{12,4},{14,6},{16,24},{18,26},{20,12},... | collective-permute-start | bytes 1179656 | tf_op jit(solution)/shard_map/ppermute | solution.py:351
  69.7 0.6 collective-permute-start.18
  70.3 20.2 %collective-permute-done.8.inner_ref = bf16[1,2,64,1536]{3,2,1,0:T(8,128)(2,1)S(1)} collective-permute-done((bf16[1,2,64,1536]{3,2,1,0:T(8,128)(2,1)S(1)}, bf16[1,2,64,1536]{3,2,1,0:T(8,128)(2,1)S(1)}, u32[]{:S(2)}, u32[]{:S(2)}) %collective-permute-start.8) | collective-permute-done | bytes 393248 | tf_op jit(solution)/shard_map/ppermute | solution.py:351
  90.5 3.9 %collective-permute-start.17 = (bf16[1,4,64,1536]{3,2,1,0:T(8,128)(2,1)S(1)}, bf16[1,4,64,1536]{3,2,1,0:T(8,128)(2,1)S(1)}, u32[]{:S(2)}, u32[]{:S(2)}) collective-permute-start(bf16[1,4,64,1536]{3,2,1,0:T(8,128)(2,1)S(1)} %collective-permute-done.14), channel_id=1, source_target_pairs={{0,4},{6,2},{8,12},{14,10},{16,20},{22,18},{24,28},{30,26},{1,5},{... | collective-permute-start | bytes 2359304 | tf_op jit(solution)/shard_map/ppermute | solution.py:351
  94.5 1.4 %collective-permute-done.10.inner_ref = bf16[1,2,64,1536]{3,2,1,0:T(8,128)(2,1)S(1)} collective-permute-done((bf16[1,2,64,1536]{3,2,1,0:T(8,128)(2,1)S(1)}, bf16[1,2,64,1536]{3,2,1,0:T(8,128)(2,1)S(1)}, u32[]{:S(2)}, u32[]{:S(2)}) %collective-permute-start.10) | collective-permute-done | bytes 393248 | tf_op jit(solution)/shard_map/ppermute | solution.py:351
  95.9 4.4 %collective-permute-start = (bf16[1,4,64,1536]{3,2,1,0:T(8,128)(2,1)}, bf16[1,4,64,1536]{3,2,1,0:T(8,128)(2,1)S(1)}, u32[]{:S(2)}, u32[]{:S(2)}) collective-permute-start(bf16[1,4,64,1536]{3,2,1,0:T(8,128)(2,1)} %ref.3), channel_id=1, source_target_pairs={{0,8},{2,10},{8,16},{10,18},{12,4},{14,6},{16,24},{18,26},{20,12},... | collective-permute-start | bytes 2359304 | tf_op jit(solution)/shard_map/ppermute | solution.py:351
  100.4 0.6 collective-permute-start.20
  101.0 1.5 %collective-permute-start.21 = (bf16[1,2,64,1536]{3,2,1,0:T(8,128)(2,1)S(1)}, bf16[1,2,64,1536]{3,2,1,0:T(8,128)(2,1)S(1)}, u32[]{:S(2)}, u32[]{:S(2)}) collective-permute-start(bf16[1,2,64,1536]{3,2,1,0:T(8,128)(2,1)S(1)} %pick.5), channel_id=1, source_target_pairs={{0,2},{2,0},{4,6},{6,4},{8,10},{10,8},{12,14},{14,12},{16,18},{18,... | collective-permute-start | bytes 1179656 | tf_op jit(solution)/shard_map/ppermute | solution.py:351
  102.5 1.3 %collective-permute-start.19 = (bf16[1,2,64,1536]{3,2,1,0:T(8,128)(2,1)S(1)}, bf16[1,2,64,1536]{3,2,1,0:T(8,128)(2,1)S(1)}, u32[]{:S(2)}, u32[]{:S(2)}) collective-permute-start(bf16[1,2,64,1536]{3,2,1,0:T(8,128)(2,1)S(1)} %collective-permute-done.18), channel_id=1, source_target_pairs={{2,6},{4,0},{10,14},{12,8},{18,22},{20,16},{26,30},{28,24},{3,7},{... | collective-permute-start | bytes 1179656 | tf_op jit(solution)/shard_map/ppermute | solution.py:351
  103.8 4.4 %shard_map.57 = (f32[12,8,256]{2,1,0:T(8,128)S(1)}, f32[12,8,256]{2,1,0:T(8,128)S(1)}, f32[12,128,256]{2,1,0:T(8,128)S(1)}) custom-call(s32[1,2,2,6]{3,2,1,0:T(2,128)S(1)} %bitcast.58, s32[1,3]{1,0:T(1,128)S(1)} %copy-done.4, bf16[256,1536]{1,0:T(8,128)(2,1)S(1)} %bitcast.29, bf16[128,1536]{1,0:T(8,128)(2,1)S(1)} %bitcast.52, ...), custom_call_target="tpu_custom_call" | custom-call | flops 1409286144 | bytes 8650752 | tf_op jit(solution)/shard_map/pallas_call | solution.py:236
  108.2 3.8 %shard_map.58 = (f32[12,8,256]{2,1,0:T(8,128)S(1)}, f32[12,8,256]{2,1,0:T(8,128)S(1)}, f32[12,128,256]{2,1,0:T(8,128)S(1)}, bf16[12,256,256]{2,1,0:T(8,128)(2,1)S(1)}) custom-call(s32[1,2,2,6]{3,2,1,0:T(2,128)S(1)} %bitcast.59, s32[1,3]{1,0:T(1,128)S(1)} %copy-done.4, bf16[256,1536]{1,0:T(8,128)(2,1)S(1)} %bitcast.30, bf16[128,1536]{1,0:T(8,128)(2,1)S(1)} %bitcast.32, ...), custom_call_target="tpu_custom_call" | custom-call | flops 1207959552 | bytes 6291456 | tf_op jit(solution)/shard_map/pallas_call | solution.py:236
  112.4 4.2 %collective-permute-done.21 = bf16[1,2,64,1536]{3,2,1,0:T(8,128)(2,1)S(1)} collective-permute-done((bf16[1,2,64,1536]{3,2,1,0:T(8,128)(2,1)S(1)}, bf16[1,2,64,1536]{3,2,1,0:T(8,128)(2,1)S(1)}, u32[]{:S(2)}, u32[]{:S(2)}) %collective-permute-start.21) | collective-permute-done | bytes 393248 | tf_op jit(solution)/shard_map/ppermute | solution.py:351
  116.6 2.2 %shard_map.59 = (f32[12,8,256]{2,1,0:T(8,128)S(1)}, f32[12,8,256]{2,1,0:T(8,128)S(1)}, f32[12,128,256]{2,1,0:T(8,128)S(1)}) custom-call(s32[1,2,2,6]{3,2,1,0:T(2,128)S(1)} %bitcast.60, s32[1,3]{1,0:T(1,128)S(1)} %copy-done.4, bf16[256,1536]{1,0:T(8,128)(2,1)S(1)} %bitcast.31, bf16[256,1536]{1,0:T(8,128)(2,1)S(1)} %bitcast.41, ...), custom_call_target="tpu_custom_call" | custom-call | flops 402653184 | bytes 4718592 | tf_op jit(solution)/shard_map/pallas_call | solution.py:236
  118.8 1.7 %last.1 = bf16[256,1536]{1,0:T(8,128)(2,1)} custom-call(bf16[256,1536]{1,0:T(8,128)(2,1)S(1)} %bitcast.40, bf16[12,256,256]{2,1,0:T(8,128)(2,1)S(1)} %get-tuple-element.26.w_ref, f32[12,8,256]{2,1,0:T(8,128)S(1)} %get-tuple-element.27.refs_6_.w_top_ref, f32[12,8,256]{2,1,0:T(8,128)S(1)} %get-tuple-element.30.top_ref, ...), custom_call_target="tpu_custom_call" | custom-call | tf_op jit(solution)/shard_map/last/pallas_call | solution.py:276
  (31 shorter events, 1.1 us)
Async XLA Ops:
  0.0 1.1 copy-start.1
  1.1 13.4 %copy-start.2 = (bf16[1,4,64,1536]{3,2,1,0:T(8,128)(2,1)S(1)}, bf16[1,4,64,1536]{3,2,1,0:T(8,128)(2,1)}, u32[]{:S(2)}) copy-start(bf16[1,4,64,1536]{3,2,1,0:T(8,128)(2,1)} %ref.2) | copy-start | bytes 2359300
  1.5 13.0 %collective-permute-start.5 = (bf16[1,2,64,1536]{3,2,1,0:T(8,128)(2,1)S(1)}, bf16[1,2,64,1536]{3,2,1,0:T(8,128)(2,1)S(1)}, u32[]{:S(2)}, u32[]{:S(2)}) collective-permute-start(bf16[1,2,64,1536]{3,2,1,0:T(8,128)(2,1)S(1)} %get-tuple-element.20), channel_id=1, source_target_pairs={{0,4},{2,6},{4,0},{6,2},{8,12},{10,14},{12,8},{14,10},{16,20},{18,... | collective-permute-start | bytes 1179656 | tf_op jit(solution)/shard_map/ppermute | solution.py:351
  5.7 17.3 %collective-permute-start.7 = (bf16[1,2,64,1536]{3,2,1,0:T(8,128)(2,1)S(1)}, bf16[1,2,64,1536]{3,2,1,0:T(8,128)(2,1)S(1)}, u32[]{:S(2)}, u32[]{:S(2)}) collective-permute-start(bf16[1,2,64,1536]{3,2,1,0:T(8,128)(2,1)S(1)} %get-tuple-element.21), channel_id=1, source_target_pairs={{0,4},{2,6},{4,0},{6,2},{8,12},{10,14},{12,8},{14,10},{16,20},{18,... | collective-permute-start | bytes 1179656 | tf_op jit(solution)/shard_map/ppermute | solution.py:351
  5.8 25.6 %collective-permute-start.9 = (bf16[1,2,64,1536]{3,2,1,0:T(8,128)(2,1)S(1)}, bf16[1,2,64,1536]{3,2,1,0:T(8,128)(2,1)S(1)}, u32[]{:S(2)}, u32[]{:S(2)}) collective-permute-start(bf16[1,2,64,1536]{3,2,1,0:T(8,128)(2,1)S(1)} %get-tuple-element.22), channel_id=1, source_target_pairs={{0,4},{2,6},{4,0},{6,2},{8,12},{10,14},{12,8},{14,10},{16,20},{18,... | collective-permute-start | bytes 1179656 | tf_op jit(solution)/shard_map/ppermute | solution.py:351
  7.8 96.0 %copy-start = (bf16[1,4,64,1536]{3,2,1,0:T(8,128)(2,1)S(1)}, bf16[1,4,64,1536]{3,2,1,0:T(8,128)(2,1)}, u32[]{:S(2)}) copy-start(bf16[1,4,64,1536]{3,2,1,0:T(8,128)(2,1)} %param.5) | copy-start | bytes 2359300
  7.8 96.0 %copy-start.3 = (s32[1,2,6,2]{2,3,1,0:T(2,128)S(1)}, s32[1,2,6,2]{2,3,1,0:T(2,128)}, u32[]{:S(2)}) copy-start(s32[1,2,6,2]{2,3,1,0:T(2,128)} %param.8) | copy-start | bytes 292
  7.8 96.0 %copy-start.4 = (s32[1,3]{1,0:T(1,128)S(1)}, s32[1,3]{1,0:T(1,128)}, u32[]{:S(2)}) copy-start(s32[1,3]{1,0:T(1,128)} %density_ref.5) | copy-start | bytes 40
  7.8 31.2 %collective-permute-start.16 = (bf16[1,2,64,1536]{3,2,1,0:T(8,128)(2,1)S(1)}, bf16[1,2,64,1536]{3,2,1,0:T(8,128)(2,1)S(1)}, u32[]{:S(2)}, u32[]{:S(2)}) collective-permute-start(bf16[1,2,64,1536]{3,2,1,0:T(8,128)(2,1)S(1)} %get-tuple-element.19), channel_id=1, source_target_pairs={{0,4},{2,6},{4,0},{6,2},{8,12},{10,14},{12,8},{14,10},{16,20},{18,... | collective-permute-start | bytes 1179656 | tf_op jit(solution)/shard_map/ppermute | solution.py:351
  7.9 32.8 %collective-permute-start.1 = (bf16[1,2,64,1536]{3,2,1,0:T(8,128)(2,1)S(1)}, bf16[1,2,64,1536]{3,2,1,0:T(8,128)(2,1)S(1)}, u32[]{:S(2)}, u32[]{:S(2)}) collective-permute-start(bf16[1,2,64,1536]{3,2,1,0:T(8,128)(2,1)S(1)} %get-tuple-element.19), channel_id=1, source_target_pairs={{4,12},{6,14},{8,0},{10,2},{12,20},{14,22},{16,8},{18,10},{20,28},... | collective-permute-start | bytes 1179656 | tf_op jit(solution)/shard_map/ppermute | solution.py:351
  14.6 41.2 %collective-permute-start.14 = (bf16[1,4,64,1536]{3,2,1,0:T(8,128)(2,1)S(1)}, bf16[1,4,64,1536]{3,2,1,0:T(8,128)(2,1)S(1)}, u32[]{:S(2)}, u32[]{:S(2)}) collective-permute-start(bf16[1,4,64,1536]{3,2,1,0:T(8,128)(2,1)S(1)} %copy-done.2), channel_id=1, source_target_pairs={{0,2},{2,0},{4,6},{6,4},{8,10},{10,8},{12,14},{14,12},{16,18},{18,... | collective-permute-start | bytes 2359304 | tf_op jit(solution)/shard_map/ppermute | solution.py:351
  23.0 36.4 %collective-permute-start.12 = (bf16[1,4,64,1536]{3,2,1,0:T(8,128)(2,1)S(1)}, bf16[1,4,64,1536]{3,2,1,0:T(8,128)(2,1)S(1)}, u32[]{:S(2)}, u32[]{:S(2)}) collective-permute-start(bf16[1,4,64,1536]{3,2,1,0:T(8,128)(2,1)S(1)} %copy-done.2), channel_id=1, source_target_pairs={{0,1},{1,0},{2,3},{3,2},{4,5},{5,4},{6,7},{7,6},{8,9},{9,8},{10,11... | collective-permute-start | bytes 2359304 | tf_op jit(solution)/shard_map/ppermute | solution.py:351
  31.4 29.2 %collective-permute-start.13 = (bf16[1,4,64,1536]{3,2,1,0:T(8,128)(2,1)}, bf16[1,4,64,1536]{3,2,1,0:T(8,128)(2,1)S(1)}, u32[]{:S(2)}, u32[]{:S(2)}) collective-permute-start(bf16[1,4,64,1536]{3,2,1,0:T(8,128)(2,1)} %ref.3), channel_id=1, source_target_pairs={{0,1},{1,0},{2,3},{3,2},{4,5},{5,4},{6,7},{7,6},{8,9},{9,8},{10,11... | collective-permute-start | bytes 2359304 | tf_op jit(solution)/shard_map/ppermute | solution.py:351
  39.0 22.3 %collective-permute-start.15 = (bf16[1,4,64,1536]{3,2,1,0:T(8,128)(2,1)}, bf16[1,4,64,1536]{3,2,1,0:T(8,128)(2,1)S(1)}, u32[]{:S(2)}, u32[]{:S(2)}) collective-permute-start(bf16[1,4,64,1536]{3,2,1,0:T(8,128)(2,1)} %ref.3), channel_id=1, source_target_pairs={{0,2},{2,0},{4,6},{6,4},{8,10},{10,8},{12,14},{14,12},{16,18},{18,... | collective-permute-start | bytes 2359304 | tf_op jit(solution)/shard_map/ppermute | solution.py:351
  40.7 11.6 %collective-permute-start.2 = (bf16[1,2,64,1536]{3,2,1,0:T(8,128)(2,1)S(1)}, bf16[1,2,64,1536]{3,2,1,0:T(8,128)(2,1)S(1)}, u32[]{:S(2)}, u32[]{:S(2)}) collective-permute-start(bf16[1,2,64,1536]{3,2,1,0:T(8,128)(2,1)S(1)} %get-tuple-element.20), channel_id=1, source_target_pairs={{4,12},{6,14},{8,0},{10,2},{12,20},{14,22},{16,8},{18,10},{20,28},... | collective-permute-start | bytes 1179656 | tf_op jit(solution)/shard_map/ppermute | solution.py:351
  52.3 13.0 %collective-permute-start.6 = (bf16[1,2,64,1536]{3,2,1,0:T(8,128)(2,1)S(1)}, bf16[1,2,64,1536]{3,2,1,0:T(8,128)(2,1)S(1)}, u32[]{:S(2)}, u32[]{:S(2)}) collective-permute-start(bf16[1,2,64,1536]{3,2,1,0:T(8,128)(2,1)S(1)} %collective-permute-done.5), channel_id=1, source_target_pairs={{0,8},{2,10},{8,16},{10,18},{12,4},{14,6},{16,24},{18,26},{20,12},... | collective-permute-start | bytes 1179656 | tf_op jit(solution)/shard_map/ppermute | solution.py:351
  55.8 44.6 %collective-permute-start.11 = (bf16[1,4,64,1536]{3,2,1,0:T(8,128)(2,1)S(1)}, bf16[1,4,64,1536]{3,2,1,0:T(8,128)(2,1)S(1)}, u32[]{:S(2)}, u32[]{:S(2)}) collective-permute-start(bf16[1,4,64,1536]{3,2,1,0:T(8,128)(2,1)S(1)} %copy-done.2), channel_id=1, source_target_pairs={{0,8},{2,10},{8,16},{10,18},{12,4},{14,6},{16,24},{18,26},{20,12},... | collective-permute-start | bytes 2359304 | tf_op jit(solution)/shard_map/ppermute | solution.py:351
  59.3 41.7 %collective-permute-start.3 = (bf16[1,4,64,1536]{3,2,1,0:T(8,128)(2,1)}, bf16[1,4,64,1536]{3,2,1,0:T(8,128)(2,1)S(1)}, u32[]{:S(2)}, u32[]{:S(2)}) collective-permute-start(bf16[1,4,64,1536]{3,2,1,0:T(8,128)(2,1)} %ref.3), channel_id=1, source_target_pairs={{4,12},{6,14},{8,0},{10,2},{12,20},{14,22},{16,8},{18,10},{20,28},... | collective-permute-start | bytes 2359304 | tf_op jit(solution)/shard_map/ppermute | solution.py:351
  60.7 9.1 %collective-permute-start.4 = (bf16[1,2,64,1536]{3,2,1,0:T(8,128)(2,1)S(1)}, bf16[1,2,64,1536]{3,2,1,0:T(8,128)(2,1)S(1)}, u32[]{:S(2)}, u32[]{:S(2)}) collective-permute-start(bf16[1,2,64,1536]{3,2,1,0:T(8,128)(2,1)S(1)} %collective-permute-done.1.outer_ref), channel_id=1, source_target_pairs={{0,4},{2,6},{4,0},{6,2},{8,12},{10,14},{12,8},{14,10},{16,20},{18,... | collective-permute-start | bytes 1179656 | tf_op jit(solution)/shard_map/ppermute | solution.py:351
  61.3 29.2 %collective-permute-start.8 = (bf16[1,2,64,1536]{3,2,1,0:T(8,128)(2,1)S(1)}, bf16[1,2,64,1536]{3,2,1,0:T(8,128)(2,1)S(1)}, u32[]{:S(2)}, u32[]{:S(2)}) collective-permute-start(bf16[1,2,64,1536]{3,2,1,0:T(8,128)(2,1)S(1)} %collective-permute-done.7.outer_ref), channel_id=1, source_target_pairs={{0,8},{2,10},{8,16},{10,18},{12,4},{14,6},{16,24},{18,26},{20,12},... | collective-permute-start | bytes 1179656 | tf_op jit(solution)/shard_map/ppermute | solution.py:351
  65.3 30.5 %collective-permute-start.10 = (bf16[1,2,64,1536]{3,2,1,0:T(8,128)(2,1)S(1)}, bf16[1,2,64,1536]{3,2,1,0:T(8,128)(2,1)S(1)}, u32[]{:S(2)}, u32[]{:S(2)}) collective-permute-start(bf16[1,2,64,1536]{3,2,1,0:T(8,128)(2,1)S(1)} %collective-permute-done.9.outer_ref), channel_id=1, source_target_pairs={{0,8},{2,10},{8,16},{10,18},{12,4},{14,6},{16,24},{18,26},{20,12},... | collective-permute-start | bytes 1179656 | tf_op jit(solution)/shard_map/ppermute | solution.py:351
  69.7 32.8 %collective-permute-start.18 = (bf16[1,2,64,1536]{3,2,1,0:T(8,128)(2,1)S(1)}, bf16[1,2,64,1536]{3,2,1,0:T(8,128)(2,1)S(1)}, u32[]{:S(2)}, u32[]{:S(2)}) collective-permute-start(bf16[1,2,64,1536]{3,2,1,0:T(8,128)(2,1)S(1)} %pick.3), channel_id=1, source_target_pairs={{0,2},{2,0},{4,6},{6,4},{8,10},{10,8},{12,14},{14,12},{16,18},{18,... | collective-permute-start | bytes 1179656 | tf_op jit(solution)/shard_map/ppermute | solution.py:351
  90.5 26.1 %collective-permute-start.17 = (bf16[1,4,64,1536]{3,2,1,0:T(8,128)(2,1)S(1)}, bf16[1,4,64,1536]{3,2,1,0:T(8,128)(2,1)S(1)}, u32[]{:S(2)}, u32[]{:S(2)}) collective-permute-start(bf16[1,4,64,1536]{3,2,1,0:T(8,128)(2,1)S(1)} %collective-permute-done.14), channel_id=1, source_target_pairs={{0,4},{6,2},{8,12},{14,10},{16,20},{22,18},{24,28},{30,26},{1,5},{... | collective-permute-start | bytes 2359304 | tf_op jit(solution)/shard_map/ppermute | solution.py:351
  95.9 23.0 %collective-permute-start = (bf16[1,4,64,1536]{3,2,1,0:T(8,128)(2,1)}, bf16[1,4,64,1536]{3,2,1,0:T(8,128)(2,1)S(1)}, u32[]{:S(2)}, u32[]{:S(2)}) collective-permute-start(bf16[1,4,64,1536]{3,2,1,0:T(8,128)(2,1)} %ref.3), channel_id=1, source_target_pairs={{0,8},{2,10},{8,16},{10,18},{12,4},{14,6},{16,24},{18,26},{20,12},... | collective-permute-start | bytes 2359304 | tf_op jit(solution)/shard_map/ppermute | solution.py:351
  100.4 12.0 %collective-permute-start.20 = (bf16[1,2,64,1536]{3,2,1,0:T(8,128)(2,1)S(1)}, bf16[1,2,64,1536]{3,2,1,0:T(8,128)(2,1)S(1)}, u32[]{:S(2)}, u32[]{:S(2)}) collective-permute-start(bf16[1,2,64,1536]{3,2,1,0:T(8,128)(2,1)S(1)} %pick.4), channel_id=1, source_target_pairs={{0,2},{2,0},{4,6},{6,4},{8,10},{10,8},{12,14},{14,12},{16,18},{18,... | collective-permute-start | bytes 1179656 | tf_op jit(solution)/shard_map/ppermute | solution.py:351
  101.0 15.6 %collective-permute-start.21 = (bf16[1,2,64,1536]{3,2,1,0:T(8,128)(2,1)S(1)}, bf16[1,2,64,1536]{3,2,1,0:T(8,128)(2,1)S(1)}, u32[]{:S(2)}, u32[]{:S(2)}) collective-permute-start(bf16[1,2,64,1536]{3,2,1,0:T(8,128)(2,1)S(1)} %pick.5), channel_id=1, source_target_pairs={{0,2},{2,0},{4,6},{6,4},{8,10},{10,8},{12,14},{14,12},{16,18},{18,... | collective-permute-start | bytes 1179656 | tf_op jit(solution)/shard_map/ppermute | solution.py:351
  102.5 14.1 %collective-permute-start.19 = (bf16[1,2,64,1536]{3,2,1,0:T(8,128)(2,1)S(1)}, bf16[1,2,64,1536]{3,2,1,0:T(8,128)(2,1)S(1)}, u32[]{:S(2)}, u32[]{:S(2)}) collective-permute-start(bf16[1,2,64,1536]{3,2,1,0:T(8,128)(2,1)S(1)} %collective-permute-done.18), channel_id=1, source_target_pairs={{2,6},{4,0},{10,14},{12,8},{18,22},{20,16},{26,30},{28,24},{3,7},{... | collective-permute-start | bytes 1179656 | tf_op jit(solution)/shard_map/ppermute | solution.py:351

commit v7 on v6

--- a/solution.py
+++ b/solution.py
@@ -13,7 +13,7 @@
 GROUP = 2 ** (OFFSETS - 1)
 SUBLANES = 8
 UNROLL = 2
-LAST_UNROLL = 6
+LAST_UNROLL = 12
 VMEM_LIMIT = 16 * 2**20
 NEG = -1e30
 SCALE2 = math.log2(math.e) / math.sqrt(HEAD_DIM)
@@ -130,9 +130,6 @@
             for kb in range(len(allow[0])):
                 row = bands_of[-1][0] + bands_of[-1][1] if bands_of else 0
                 bands_of.append((row, rows, [allow[half][kb] for half in range(halves)]))
-
-        def columns(h):
-            return pl.ds(pl.multiple_of(h * HEAD_DIM, HEAD_DIM), HEAD_DIM)
 
         def stacked(h, part):
             cols = columns(h)
@@ -249,13 +246,21 @@
     )(*operands)
 
 
+def columns(h):
+    return pl.ds(pl.multiple_of(h * HEAD_DIM, HEAD_DIM), HEAD_DIM)
+
+
 def last_call(value_rows, weights, weights_top, state):
     tokens, features = value_rows.shape
     heads = features // HEAD_DIM
 
-    def kernel(v_ref, w_ref, w_top_ref, top_ref, total_ref, acc_ref, out_ref):
+    def kernel(v_ref, w_ref, w_top_ref, top_ref, total_ref, acc_ref, out_ref, done_ref, sems):
+        def leave(h):
+            cols = columns(h)
+            return pltpu.make_async_copy(done_ref.at[:, cols], out_ref.at[:, cols], sems.at[h])
+
         def one_head(h, carry):
-            cols = pl.ds(pl.multiple_of(h * HEAD_DIM, HEAD_DIM), HEAD_DIM)
+            cols = columns(h)
             v = jnp.transpose(v_ref[:, cols])
             ones = jnp.ones((2 * SUBLANES, v.shape[1]), jnp.bfloat16)
             mixed = contract(join([v, ones], 0), w_ref[h], ((1,), (0,)))
@@ -263,10 +268,13 @@
             total = total_ref[h][0:1] + mixed[HEAD_DIM : HEAD_DIM + 1] * decay
             inverse = 1.0 / total
             acc = acc_ref[h] * inverse + mixed[:HEAD_DIM] * (decay * inverse)
-            out_ref[:, cols] = jnp.transpose(acc.astype(jnp.bfloat16))
+            done_ref[:, cols] = jnp.transpose(acc.astype(jnp.bfloat16))
+            leave(h).start()
             return carry
 
         lax.fori_loop(0, heads, one_head, 0, unroll=LAST_UNROLL)
+        for h in range(heads):
+            leave(h).wait()
 
     vmem = pl.BlockSpec(memory_space=pltpu.VMEM)
     operands = [
@@ -276,8 +284,12 @@
     return pl.pallas_call(
         kernel,
         in_specs=[vmem] * len(operands),
-        out_specs=vmem,
+        out_specs=pl.BlockSpec(memory_space=pl.ANY),
         out_shape=jax.ShapeDtypeStruct((tokens, features), jnp.bfloat16),
+        scratch_shapes=[
+            pltpu.VMEM((tokens, features), jnp.bfloat16),
+            pltpu.SemaphoreType.DMA((heads,)),
+        ],
         compiler_params=pltpu.CompilerParams(vmem_limit_bytes=VMEM_LIMIT),
         name="last",
     )(*operands)

time: 121 us -> 121 us (level)
  no operation moved by 1% of the time
where the time goes in v7:
time: 121 us; the launch traced here: 120 us
  waiting for transfers between devices  64.1 us (53%)
  starting transfers between devices  41.3 us (34%)
  Pallas kernels  13.4 us (11%)
    ppermute x22, waiting for transfers between devices, send(): return lax.ppermute(value, axis, pairs)  64.1 us
    ppermute x22, starting transfers between devices, send(): return lax.ppermute(value, axis, pairs)  41.3 us
    pallas_call x3, Pallas kernels, stage_call(): pl.pallas_call(kernel, in_specs=specs, out_specs=[vmem] * len(outs), out_...  10.4 us
  transfers between devices with their start and end apart: 22, of which 9 were waited for; matrix products, arithmetic and copies ran while one was open for 0% of the time, Pallas kernels for 10%

profile of v7, /device:TPU:0, one launch (start us, length us, event | category | flops | bytes accessed | tf_op | source)
XLA Modules:
  0.0 120.2 jit_solution(13911960249231665042)
XLA Ops:
  0.0 1.1 copy-done.1
  1.5 3.1 %collective-permute-start.5 = (bf16[1,2,64,1536]{3,2,1,0:T(8,128)(2,1)S(1)}, bf16[1,2,64,1536]{3,2,1,0:T(8,128)(2,1)S(1)}, u32[]{:S(2)}, u32[]{:S(2)}) collective-permute-start(bf16[1,2,64,1536]{3,2,1,0:T(8,128)(2,1)S(1)} %get-tuple-element.20), channel_id=1, source_target_pairs={{0,4},{2,6},{4,0},{6,2},{8,12},{10,14},{12,8},{14,10},{16,20},{18,... | collective-permute-start | bytes 1179656 | tf_op jit(solution)/shard_map/ppermute | solution.py:363
  4.6 1.1 shard_map.56
  5.8 2.0 %collective-permute-start.9 = (bf16[1,2,64,1536]{3,2,1,0:T(8,128)(2,1)S(1)}, bf16[1,2,64,1536]{3,2,1,0:T(8,128)(2,1)S(1)}, u32[]{:S(2)}, u32[]{:S(2)}) collective-permute-start(bf16[1,2,64,1536]{3,2,1,0:T(8,128)(2,1)S(1)} %get-tuple-element.22), channel_id=1, source_target_pairs={{0,4},{2,6},{4,0},{6,2},{8,12},{10,14},{12,8},{14,10},{16,20},{18,... | collective-permute-start | bytes 1179656 | tf_op jit(solution)/shard_map/ppermute | solution.py:363
  7.9 1.4 %collective-permute-start.1 = (bf16[1,2,64,1536]{3,2,1,0:T(8,128)(2,1)S(1)}, bf16[1,2,64,1536]{3,2,1,0:T(8,128)(2,1)S(1)}, u32[]{:S(2)}, u32[]{:S(2)}) collective-permute-start(bf16[1,2,64,1536]{3,2,1,0:T(8,128)(2,1)S(1)} %get-tuple-element.19), channel_id=1, source_target_pairs={{4,12},{6,14},{8,0},{10,2},{12,20},{14,22},{16,8},{18,10},{20,28},... | collective-permute-start | bytes 1179656 | tf_op jit(solution)/shard_map/ppermute | solution.py:363
  9.3 5.2 %collective-permute-done.5 = bf16[1,2,64,1536]{3,2,1,0:T(8,128)(2,1)S(1)} collective-permute-done((bf16[1,2,64,1536]{3,2,1,0:T(8,128)(2,1)S(1)}, bf16[1,2,64,1536]{3,2,1,0:T(8,128)(2,1)S(1)}, u32[]{:S(2)}, u32[]{:S(2)}) %collective-permute-start.5) | collective-permute-done | bytes 393248 | tf_op jit(solution)/shard_map/ppermute | solution.py:363
  14.6 2.0 %collective-permute-start.14 = (bf16[1,4,64,1536]{3,2,1,0:T(8,128)(2,1)S(1)}, bf16[1,4,64,1536]{3,2,1,0:T(8,128)(2,1)S(1)}, u32[]{:S(2)}, u32[]{:S(2)}) collective-permute-start(bf16[1,4,64,1536]{3,2,1,0:T(8,128)(2,1)S(1)} %copy-done.2), channel_id=1, source_target_pairs={{0,2},{2,0},{4,6},{6,4},{8,10},{10,8},{12,14},{14,12},{16,18},{18,... | collective-permute-start | bytes 2359304 | tf_op jit(solution)/shard_map/ppermute | solution.py:363
  16.6 6.4 %collective-permute-done.7.outer_ref = bf16[1,2,64,1536]{3,2,1,0:T(8,128)(2,1)S(1)} collective-permute-done((bf16[1,2,64,1536]{3,2,1,0:T(8,128)(2,1)S(1)}, bf16[1,2,64,1536]{3,2,1,0:T(8,128)(2,1)S(1)}, u32[]{:S(2)}, u32[]{:S(2)}) %collective-permute-start.7) | collective-permute-done | bytes 393248 | tf_op jit(solution)/shard_map/ppermute | solution.py:363
  23.0 8.4 %collective-permute-done.9.outer_ref = bf16[1,2,64,1536]{3,2,1,0:T(8,128)(2,1)S(1)} collective-permute-done((bf16[1,2,64,1536]{3,2,1,0:T(8,128)(2,1)S(1)}, bf16[1,2,64,1536]{3,2,1,0:T(8,128)(2,1)S(1)}, u32[]{:S(2)}, u32[]{:S(2)}) %collective-permute-start.9) | collective-permute-done | bytes 393248 | tf_op jit(solution)/shard_map/ppermute | solution.py:363
  31.4 7.6 %collective-permute-done.16 = bf16[1,2,64,1536]{3,2,1,0:T(8,128)(2,1)S(1)} collective-permute-done((bf16[1,2,64,1536]{3,2,1,0:T(8,128)(2,1)S(1)}, bf16[1,2,64,1536]{3,2,1,0:T(8,128)(2,1)S(1)}, u32[]{:S(2)}, u32[]{:S(2)}) %collective-permute-start.16) | collective-permute-done | bytes 393248 | tf_op jit(solution)/shard_map/ppermute | solution.py:363
  39.0 1.7 %collective-permute-start.15 = (bf16[1,4,64,1536]{3,2,1,0:T(8,128)(2,1)}, bf16[1,4,64,1536]{3,2,1,0:T(8,128)(2,1)S(1)}, u32[]{:S(2)}, u32[]{:S(2)}) collective-permute-start(bf16[1,4,64,1536]{3,2,1,0:T(8,128)(2,1)} %ref.3), channel_id=1, source_target_pairs={{0,2},{2,0},{4,6},{6,4},{8,10},{10,8},{12,14},{14,12},{16,18},{18,... | collective-permute-start | bytes 2359304 | tf_op jit(solution)/shard_map/ppermute | solution.py:363
  40.7 1.3 %collective-permute-start.2 = (bf16[1,2,64,1536]{3,2,1,0:T(8,128)(2,1)S(1)}, bf16[1,2,64,1536]{3,2,1,0:T(8,128)(2,1)S(1)}, u32[]{:S(2)}, u32[]{:S(2)}) collective-permute-start(bf16[1,2,64,1536]{3,2,1,0:T(8,128)(2,1)S(1)} %get-tuple-element.20), channel_id=1, source_target_pairs={{4,12},{6,14},{8,0},{10,2},{12,20},{14,22},{16,8},{18,10},{20,28},... | collective-permute-start | bytes 1179656 | tf_op jit(solution)/shard_map/ppermute | solution.py:363
  42.0 10.3 %collective-permute-done.2 = bf16[1,2,64,1536]{3,2,1,0:T(8,128)(2,1)S(1)} collective-permute-done((bf16[1,2,64,1536]{3,2,1,0:T(8,128)(2,1)S(1)}, bf16[1,2,64,1536]{3,2,1,0:T(8,128)(2,1)S(1)}, u32[]{:S(2)}, u32[]{:S(2)}) %collective-permute-start.2) | collective-permute-done | bytes 393248 | tf_op jit(solution)/shard_map/ppermute | solution.py:363
  52.3 3.5 %collective-permute-start.6 = (bf16[1,2,64,1536]{3,2,1,0:T(8,128)(2,1)S(1)}, bf16[1,2,64,1536]{3,2,1,0:T(8,128)(2,1)S(1)}, u32[]{:S(2)}, u32[]{:S(2)}) collective-permute-start(bf16[1,2,64,1536]{3,2,1,0:T(8,128)(2,1)S(1)} %collective-permute-done.5), channel_id=1, source_target_pairs={{0,8},{2,10},{8,16},{10,18},{12,4},{14,6},{16,24},{18,26},{20,12},... | collective-permute-start | bytes 1179656 | tf_op jit(solution)/shard_map/ppermute | solution.py:363
  55.8 3.5 %collective-permute-start.11 = (bf16[1,4,64,1536]{3,2,1,0:T(8,128)(2,1)S(1)}, bf16[1,4,64,1536]{3,2,1,0:T(8,128)(2,1)S(1)}, u32[]{:S(2)}, u32[]{:S(2)}) collective-permute-start(bf16[1,4,64,1536]{3,2,1,0:T(8,128)(2,1)S(1)} %copy-done.2), channel_id=1, source_target_pairs={{0,8},{2,10},{8,16},{10,18},{12,4},{14,6},{16,24},{18,26},{20,12},... | collective-permute-start | bytes 2359304 | tf_op jit(solution)/shard_map/ppermute | solution.py:363
  59.3 1.3 %collective-permute-start.3 = (bf16[1,4,64,1536]{3,2,1,0:T(8,128)(2,1)}, bf16[1,4,64,1536]{3,2,1,0:T(8,128)(2,1)S(1)}, u32[]{:S(2)}, u32[]{:S(2)}) collective-permute-start(bf16[1,4,64,1536]{3,2,1,0:T(8,128)(2,1)} %ref.3), channel_id=1, source_target_pairs={{4,12},{6,14},{8,0},{10,2},{12,20},{14,22},{16,8},{18,10},{20,28},... | collective-permute-start | bytes 2359304 | tf_op jit(solution)/shard_map/ppermute | solution.py:363
  60.7 0.7 collective-permute-start.4
  61.3 4.0 %collective-permute-start.8 = (bf16[1,2,64,1536]{3,2,1,0:T(8,128)(2,1)S(1)}, bf16[1,2,64,1536]{3,2,1,0:T(8,128)(2,1)S(1)}, u32[]{:S(2)}, u32[]{:S(2)}) collective-permute-start(bf16[1,2,64,1536]{3,2,1,0:T(8,128)(2,1)S(1)} %collective-permute-done.7.outer_ref), channel_id=1, source_target_pairs={{0,8},{2,10},{8,16},{10,18},{12,4},{14,6},{16,24},{18,26},{20,12},... | collective-permute-start | bytes 1179656 | tf_op jit(solution)/shard_map/ppermute | solution.py:363
  65.3 4.3 %collective-permute-start.10 = (bf16[1,2,64,1536]{3,2,1,0:T(8,128)(2,1)S(1)}, bf16[1,2,64,1536]{3,2,1,0:T(8,128)(2,1)S(1)}, u32[]{:S(2)}, u32[]{:S(2)}) collective-permute-start(bf16[1,2,64,1536]{3,2,1,0:T(8,128)(2,1)S(1)} %collective-permute-done.9.outer_ref), channel_id=1, source_target_pairs={{0,8},{2,10},{8,16},{10,18},{12,4},{14,6},{16,24},{18,26},{20,12},... | collective-permute-start | bytes 1179656 | tf_op jit(solution)/shard_map/ppermute | solution.py:363
  69.7 0.6 collective-permute-start.18
  70.3 20.2 %collective-permute-done.8.inner_ref = bf16[1,2,64,1536]{3,2,1,0:T(8,128)(2,1)S(1)} collective-permute-done((bf16[1,2,64,1536]{3,2,1,0:T(8,128)(2,1)S(1)}, bf16[1,2,64,1536]{3,2,1,0:T(8,128)(2,1)S(1)}, u32[]{:S(2)}, u32[]{:S(2)}) %collective-permute-start.8) | collective-permute-done | bytes 393248 | tf_op jit(solution)/shard_map/ppermute | solution.py:363
  90.5 3.9 %collective-permute-start.17 = (bf16[1,4,64,1536]{3,2,1,0:T(8,128)(2,1)S(1)}, bf16[1,4,64,1536]{3,2,1,0:T(8,128)(2,1)S(1)}, u32[]{:S(2)}, u32[]{:S(2)}) collective-permute-start(bf16[1,4,64,1536]{3,2,1,0:T(8,128)(2,1)S(1)} %collective-permute-done.14), channel_id=1, source_target_pairs={{0,4},{6,2},{8,12},{14,10},{16,20},{22,18},{24,28},{30,26},{1,5},{... | collective-permute-start | bytes 2359304 | tf_op jit(solution)/shard_map/ppermute | solution.py:363
  94.5 1.4 %collective-permute-done.10.inner_ref = bf16[1,2,64,1536]{3,2,1,0:T(8,128)(2,1)S(1)} collective-permute-done((bf16[1,2,64,1536]{3,2,1,0:T(8,128)(2,1)S(1)}, bf16[1,2,64,1536]{3,2,1,0:T(8,128)(2,1)S(1)}, u32[]{:S(2)}, u32[]{:S(2)}) %collective-permute-start.10) | collective-permute-done | bytes 393248 | tf_op jit(solution)/shard_map/ppermute | solution.py:363
  95.9 4.4 %collective-permute-start = (bf16[1,4,64,1536]{3,2,1,0:T(8,128)(2,1)}, bf16[1,4,64,1536]{3,2,1,0:T(8,128)(2,1)S(1)}, u32[]{:S(2)}, u32[]{:S(2)}) collective-permute-start(bf16[1,4,64,1536]{3,2,1,0:T(8,128)(2,1)} %ref.3), channel_id=1, source_target_pairs={{0,8},{2,10},{8,16},{10,18},{12,4},{14,6},{16,24},{18,26},{20,12},... | collective-permute-start | bytes 2359304 | tf_op jit(solution)/shard_map/ppermute | solution.py:363
  100.4 0.6 collective-permute-start.20
  101.0 1.5 %collective-permute-start.21 = (bf16[1,2,64,1536]{3,2,1,0:T(8,128)(2,1)S(1)}, bf16[1,2,64,1536]{3,2,1,0:T(8,128)(2,1)S(1)}, u32[]{:S(2)}, u32[]{:S(2)}) collective-permute-start(bf16[1,2,64,1536]{3,2,1,0:T(8,128)(2,1)S(1)} %pick.5), channel_id=1, source_target_pairs={{0,2},{2,0},{4,6},{6,4},{8,10},{10,8},{12,14},{14,12},{16,18},{18,... | collective-permute-start | bytes 1179656 | tf_op jit(solution)/shard_map/ppermute | solution.py:363
  102.5 1.3 %collective-permute-start.19 = (bf16[1,2,64,1536]{3,2,1,0:T(8,128)(2,1)S(1)}, bf16[1,2,64,1536]{3,2,1,0:T(8,128)(2,1)S(1)}, u32[]{:S(2)}, u32[]{:S(2)}) collective-permute-start(bf16[1,2,64,1536]{3,2,1,0:T(8,128)(2,1)S(1)} %collective-permute-done.18), channel_id=1, source_target_pairs={{2,6},{4,0},{10,14},{12,8},{18,22},{20,16},{26,30},{28,24},{3,7},{... | collective-permute-start | bytes 1179656 | tf_op jit(solution)/shard_map/ppermute | solution.py:363
  103.8 4.4 %shard_map.57 = (f32[12,8,256]{2,1,0:T(8,128)S(1)}, f32[12,8,256]{2,1,0:T(8,128)S(1)}, f32[12,128,256]{2,1,0:T(8,128)S(1)}) custom-call(s32[1,2,2,6]{3,2,1,0:T(2,128)S(1)} %bitcast.58, s32[1,3]{1,0:T(1,128)S(1)} %copy-done.4, bf16[256,1536]{1,0:T(8,128)(2,1)S(1)} %bitcast.29, bf16[128,1536]{1,0:T(8,128)(2,1)S(1)} %bitcast.52, ...), custom_call_target="tpu_custom_call" | custom-call | flops 1409286144 | bytes 8650752 | tf_op jit(solution)/shard_map/pallas_call | solution.py:233
  108.2 3.8 %shard_map.58 = (f32[12,8,256]{2,1,0:T(8,128)S(1)}, f32[12,8,256]{2,1,0:T(8,128)S(1)}, f32[12,128,256]{2,1,0:T(8,128)S(1)}, bf16[12,256,256]{2,1,0:T(8,128)(2,1)S(1)}) custom-call(s32[1,2,2,6]{3,2,1,0:T(2,128)S(1)} %bitcast.59, s32[1,3]{1,0:T(1,128)S(1)} %copy-done.4, bf16[256,1536]{1,0:T(8,128)(2,1)S(1)} %bitcast.30, bf16[128,1536]{1,0:T(8,128)(2,1)S(1)} %bitcast.32, ...), custom_call_target="tpu_custom_call" | custom-call | flops 1207959552 | bytes 6291456 | tf_op jit(solution)/shard_map/pallas_call | solution.py:233
  112.4 4.2 %collective-permute-done.21 = bf16[1,2,64,1536]{3,2,1,0:T(8,128)(2,1)S(1)} collective-permute-done((bf16[1,2,64,1536]{3,2,1,0:T(8,128)(2,1)S(1)}, bf16[1,2,64,1536]{3,2,1,0:T(8,128)(2,1)S(1)}, u32[]{:S(2)}, u32[]{:S(2)}) %collective-permute-start.21) | collective-permute-done | bytes 393248 | tf_op jit(solution)/shard_map/ppermute | solution.py:363
  116.6 2.2 %shard_map.59 = (f32[12,8,256]{2,1,0:T(8,128)S(1)}, f32[12,8,256]{2,1,0:T(8,128)S(1)}, f32[12,128,256]{2,1,0:T(8,128)S(1)}) custom-call(s32[1,2,2,6]{3,2,1,0:T(2,128)S(1)} %bitcast.60, s32[1,3]{1,0:T(1,128)S(1)} %copy-done.4, bf16[256,1536]{1,0:T(8,128)(2,1)S(1)} %bitcast.31, bf16[256,1536]{1,0:T(8,128)(2,1)S(1)} %bitcast.41, ...), custom_call_target="tpu_custom_call" | custom-call | flops 402653184 | bytes 4718592 | tf_op jit(solution)/shard_map/pallas_call | solution.py:233
  118.8 1.4 %last.1 = bf16[256,1536]{1,0:T(8,128)(2,1)} custom-call(bf16[256,1536]{1,0:T(8,128)(2,1)S(1)} %bitcast.40, bf16[12,256,256]{2,1,0:T(8,128)(2,1)S(1)} %get-tuple-element.26.w_ref, f32[12,8,256]{2,1,0:T(8,128)S(1)} %get-tuple-element.27.refs_6_.w_top_ref, f32[12,8,256]{2,1,0:T(8,128)S(1)} %get-tuple-element.30.top_ref, ...), custom_call_target="tpu_custom_call" | custom-call | tf_op jit(solution)/shard_map/last/pallas_call | solution.py:284
  (31 shorter events, 1.1 us)
Async XLA Ops:
  0.0 1.1 copy-start.1
  1.1 13.4 %copy-start.2 = (bf16[1,4,64,1536]{3,2,1,0:T(8,128)(2,1)S(1)}, bf16[1,4,64,1536]{3,2,1,0:T(8,128)(2,1)}, u32[]{:S(2)}) copy-start(bf16[1,4,64,1536]{3,2,1,0:T(8,128)(2,1)} %ref.2) | copy-start | bytes 2359300
  1.5 13.0 %collective-permute-start.5 = (bf16[1,2,64,1536]{3,2,1,0:T(8,128)(2,1)S(1)}, bf16[1,2,64,1536]{3,2,1,0:T(8,128)(2,1)S(1)}, u32[]{:S(2)}, u32[]{:S(2)}) collective-permute-start(bf16[1,2,64,1536]{3,2,1,0:T(8,128)(2,1)S(1)} %get-tuple-element.20), channel_id=1, source_target_pairs={{0,4},{2,6},{4,0},{6,2},{8,12},{10,14},{12,8},{14,10},{16,20},{18,... | collective-permute-start | bytes 1179656 | tf_op jit(solution)/shard_map/ppermute | solution.py:363
  5.7 17.3 %collective-permute-start.7 = (bf16[1,2,64,1536]{3,2,1,0:T(8,128)(2,1)S(1)}, bf16[1,2,64,1536]{3,2,1,0:T(8,128)(2,1)S(1)}, u32[]{:S(2)}, u32[]{:S(2)}) collective-permute-start(bf16[1,2,64,1536]{3,2,1,0:T(8,128)(2,1)S(1)} %get-tuple-element.21), channel_id=1, source_target_pairs={{0,4},{2,6},{4,0},{6,2},{8,12},{10,14},{12,8},{14,10},{16,20},{18,... | collective-permute-start | bytes 1179656 | tf_op jit(solution)/shard_map/ppermute | solution.py:363
  5.8 25.6 %collective-permute-start.9 = (bf16[1,2,64,1536]{3,2,1,0:T(8,128)(2,1)S(1)}, bf16[1,2,64,1536]{3,2,1,0:T(8,128)(2,1)S(1)}, u32[]{:S(2)}, u32[]{:S(2)}) collective-permute-start(bf16[1,2,64,1536]{3,2,1,0:T(8,128)(2,1)S(1)} %get-tuple-element.22), channel_id=1, source_target_pairs={{0,4},{2,6},{4,0},{6,2},{8,12},{10,14},{12,8},{14,10},{16,20},{18,... | collective-permute-start | bytes 1179656 | tf_op jit(solution)/shard_map/ppermute | solution.py:363
  7.8 96.0 %copy-start = (bf16[1,4,64,1536]{3,2,1,0:T(8,128)(2,1)S(1)}, bf16[1,4,64,1536]{3,2,1,0:T(8,128)(2,1)}, u32[]{:S(2)}) copy-start(bf16[1,4,64,1536]{3,2,1,0:T(8,128)(2,1)} %param.5) | copy-start | bytes 2359300
  7.8 96.0 %copy-start.3 = (s32[1,2,6,2]{2,3,1,0:T(2,128)S(1)}, s32[1,2,6,2]{2,3,1,0:T(2,128)}, u32[]{:S(2)}) copy-start(s32[1,2,6,2]{2,3,1,0:T(2,128)} %param.8) | copy-start | bytes 292
  7.8 96.0 %copy-start.4 = (s32[1,3]{1,0:T(1,128)S(1)}, s32[1,3]{1,0:T(1,128)}, u32[]{:S(2)}) copy-start(s32[1,3]{1,0:T(1,128)} %density_ref.5) | copy-start | bytes 40
  7.8 31.2 %collective-permute-start.16 = (bf16[1,2,64,1536]{3,2,1,0:T(8,128)(2,1)S(1)}, bf16[1,2,64,1536]{3,2,1,0:T(8,128)(2,1)S(1)}, u32[]{:S(2)}, u32[]{:S(2)}) collective-permute-start(bf16[1,2,64,1536]{3,2,1,0:T(8,128)(2,1)S(1)} %get-tuple-element.19), channel_id=1, source_target_pairs={{0,4},{2,6},{4,0},{6,2},{8,12},{10,14},{12,8},{14,10},{16,20},{18,... | collective-permute-start | bytes 1179656 | tf_op jit(solution)/shard_map/ppermute | solution.py:363
  7.9 32.8 %collective-permute-start.1 = (bf16[1,2,64,1536]{3,2,1,0:T(8,128)(2,1)S(1)}, bf16[1,2,64,1536]{3,2,1,0:T(8,128)(2,1)S(1)}, u32[]{:S(2)}, u32[]{:S(2)}) collective-permute-start(bf16[1,2,64,1536]{3,2,1,0:T(8,128)(2,1)S(1)} %get-tuple-element.19), channel_id=1, source_target_pairs={{4,12},{6,14},{8,0},{10,2},{12,20},{14,22},{16,8},{18,10},{20,28},... | collective-permute-start | bytes 1179656 | tf_op jit(solution)/shard_map/ppermute | solution.py:363
  14.6 41.2 %collective-permute-start.14 = (bf16[1,4,64,1536]{3,2,1,0:T(8,128)(2,1)S(1)}, bf16[1,4,64,1536]{3,2,1,0:T(8,128)(2,1)S(1)}, u32[]{:S(2)}, u32[]{:S(2)}) collective-permute-start(bf16[1,4,64,1536]{3,2,1,0:T(8,128)(2,1)S(1)} %copy-done.2), channel_id=1, source_target_pairs={{0,2},{2,0},{4,6},{6,4},{8,10},{10,8},{12,14},{14,12},{16,18},{18,... | collective-permute-start | bytes 2359304 | tf_op jit(solution)/shard_map/ppermute | solution.py:363
  23.0 36.4 %collective-permute-start.12 = (bf16[1,4,64,1536]{3,2,1,0:T(8,128)(2,1)S(1)}, bf16[1,4,64,1536]{3,2,1,0:T(8,128)(2,1)S(1)}, u32[]{:S(2)}, u32[]{:S(2)}) collective-permute-start(bf16[1,4,64,1536]{3,2,1,0:T(8,128)(2,1)S(1)} %copy-done.2), channel_id=1, source_target_pairs={{0,1},{1,0},{2,3},{3,2},{4,5},{5,4},{6,7},{7,6},{8,9},{9,8},{10,11... | collective-permute-start | bytes 2359304 | tf_op jit(solution)/shard_map/ppermute | solution.py:363
  31.4 29.2 %collective-permute-start.13 = (bf16[1,4,64,1536]{3,2,1,0:T(8,128)(2,1)}, bf16[1,4,64,1536]{3,2,1,0:T(8,128)(2,1)S(1)}, u32[]{:S(2)}, u32[]{:S(2)}) collective-permute-start(bf16[1,4,64,1536]{3,2,1,0:T(8,128)(2,1)} %ref.3), channel_id=1, source_target_pairs={{0,1},{1,0},{2,3},{3,2},{4,5},{5,4},{6,7},{7,6},{8,9},{9,8},{10,11... | collective-permute-start | bytes 2359304 | tf_op jit(solution)/shard_map/ppermute | solution.py:363
  39.0 22.3 %collective-permute-start.15 = (bf16[1,4,64,1536]{3,2,1,0:T(8,128)(2,1)}, bf16[1,4,64,1536]{3,2,1,0:T(8,128)(2,1)S(1)}, u32[]{:S(2)}, u32[]{:S(2)}) collective-permute-start(bf16[1,4,64,1536]{3,2,1,0:T(8,128)(2,1)} %ref.3), channel_id=1, source_target_pairs={{0,2},{2,0},{4,6},{6,4},{8,10},{10,8},{12,14},{14,12},{16,18},{18,... | collective-permute-start | bytes 2359304 | tf_op jit(solution)/shard_map/ppermute | solution.py:363
  40.7 11.6 %collective-permute-start.2 = (bf16[1,2,64,1536]{3,2,1,0:T(8,128)(2,1)S(1)}, bf16[1,2,64,1536]{3,2,1,0:T(8,128)(2,1)S(1)}, u32[]{:S(2)}, u32[]{:S(2)}) collective-permute-start(bf16[1,2,64,1536]{3,2,1,0:T(8,128)(2,1)S(1)} %get-tuple-element.20), channel_id=1, source_target_pairs={{4,12},{6,14},{8,0},{10,2},{12,20},{14,22},{16,8},{18,10},{20,28},... | collective-permute-start | bytes 1179656 | tf_op jit(solution)/shard_map/ppermute | solution.py:363
  52.3 13.0 %collective-permute-start.6 = (bf16[1,2,64,1536]{3,2,1,0:T(8,128)(2,1)S(1)}, bf16[1,2,64,1536]{3,2,1,0:T(8,128)(2,1)S(1)}, u32[]{:S(2)}, u32[]{:S(2)}) collective-permute-start(bf16[1,2,64,1536]{3,2,1,0:T(8,128)(2,1)S(1)} %collective-permute-done.5), channel_id=1, source_target_pairs={{0,8},{2,10},{8,16},{10,18},{12,4},{14,6},{16,24},{18,26},{20,12},... | collective-permute-start | bytes 1179656 | tf_op jit(solution)/shard_map/ppermute | solution.py:363
  55.8 44.6 %collective-permute-start.11 = (bf16[1,4,64,1536]{3,2,1,0:T(8,128)(2,1)S(1)}, bf16[1,4,64,1536]{3,2,1,0:T(8,128)(2,1)S(1)}, u32[]{:S(2)}, u32[]{:S(2)}) collective-permute-start(bf16[1,4,64,1536]{3,2,1,0:T(8,128)(2,1)S(1)} %copy-done.2), channel_id=1, source_target_pairs={{0,8},{2,10},{8,16},{10,18},{12,4},{14,6},{16,24},{18,26},{20,12},... | collective-permute-start | bytes 2359304 | tf_op jit(solution)/shard_map/ppermute | solution.py:363
  59.3 41.7 %collective-permute-start.3 = (bf16[1,4,64,1536]{3,2,1,0:T(8,128)(2,1)}, bf16[1,4,64,1536]{3,2,1,0:T(8,128)(2,1)S(1)}, u32[]{:S(2)}, u32[]{:S(2)}) collective-permute-start(bf16[1,4,64,1536]{3,2,1,0:T(8,128)(2,1)} %ref.3), channel_id=1, source_target_pairs={{4,12},{6,14},{8,0},{10,2},{12,20},{14,22},{16,8},{18,10},{20,28},... | collective-permute-start | bytes 2359304 | tf_op jit(solution)/shard_map/ppermute | solution.py:363
  60.7 9.1 %collective-permute-start.4 = (bf16[1,2,64,1536]{3,2,1,0:T(8,128)(2,1)S(1)}, bf16[1,2,64,1536]{3,2,1,0:T(8,128)(2,1)S(1)}, u32[]{:S(2)}, u32[]{:S(2)}) collective-permute-start(bf16[1,2,64,1536]{3,2,1,0:T(8,128)(2,1)S(1)} %collective-permute-done.1.outer_ref), channel_id=1, source_target_pairs={{0,4},{2,6},{4,0},{6,2},{8,12},{10,14},{12,8},{14,10},{16,20},{18,... | collective-permute-start | bytes 1179656 | tf_op jit(solution)/shard_map/ppermute | solution.py:363
  61.3 29.2 %collective-permute-start.8 = (bf16[1,2,64,1536]{3,2,1,0:T(8,128)(2,1)S(1)}, bf16[1,2,64,1536]{3,2,1,0:T(8,128)(2,1)S(1)}, u32[]{:S(2)}, u32[]{:S(2)}) collective-permute-start(bf16[1,2,64,1536]{3,2,1,0:T(8,128)(2,1)S(1)} %collective-permute-done.7.outer_ref), channel_id=1, source_target_pairs={{0,8},{2,10},{8,16},{10,18},{12,4},{14,6},{16,24},{18,26},{20,12},... | collective-permute-start | bytes 1179656 | tf_op jit(solution)/shard_map/ppermute | solution.py:363
  65.3 30.5 %collective-permute-start.10 = (bf16[1,2,64,1536]{3,2,1,0:T(8,128)(2,1)S(1)}, bf16[1,2,64,1536]{3,2,1,0:T(8,128)(2,1)S(1)}, u32[]{:S(2)}, u32[]{:S(2)}) collective-permute-start(bf16[1,2,64,1536]{3,2,1,0:T(8,128)(2,1)S(1)} %collective-permute-done.9.outer_ref), channel_id=1, source_target_pairs={{0,8},{2,10},{8,16},{10,18},{12,4},{14,6},{16,24},{18,26},{20,12},... | collective-permute-start | bytes 1179656 | tf_op jit(solution)/shard_map/ppermute | solution.py:363
  69.7 32.8 %collective-permute-start.18 = (bf16[1,2,64,1536]{3,2,1,0:T(8,128)(2,1)S(1)}, bf16[1,2,64,1536]{3,2,1,0:T(8,128)(2,1)S(1)}, u32[]{:S(2)}, u32[]{:S(2)}) collective-permute-start(bf16[1,2,64,1536]{3,2,1,0:T(8,128)(2,1)S(1)} %pick.3), channel_id=1, source_target_pairs={{0,2},{2,0},{4,6},{6,4},{8,10},{10,8},{12,14},{14,12},{16,18},{18,... | collective-permute-start | bytes 1179656 | tf_op jit(solution)/shard_map/ppermute | solution.py:363
  90.5 26.1 %collective-permute-start.17 = (bf16[1,4,64,1536]{3,2,1,0:T(8,128)(2,1)S(1)}, bf16[1,4,64,1536]{3,2,1,0:T(8,128)(2,1)S(1)}, u32[]{:S(2)}, u32[]{:S(2)}) collective-permute-start(bf16[1,4,64,1536]{3,2,1,0:T(8,128)(2,1)S(1)} %collective-permute-done.14), channel_id=1, source_target_pairs={{0,4},{6,2},{8,12},{14,10},{16,20},{22,18},{24,28},{30,26},{1,5},{... | collective-permute-start | bytes 2359304 | tf_op jit(solution)/shard_map/ppermute | solution.py:363
  95.9 23.0 %collective-permute-start = (bf16[1,4,64,1536]{3,2,1,0:T(8,128)(2,1)}, bf16[1,4,64,1536]{3,2,1,0:T(8,128)(2,1)S(1)}, u32[]{:S(2)}, u32[]{:S(2)}) collective-permute-start(bf16[1,4,64,1536]{3,2,1,0:T(8,128)(2,1)} %ref.3), channel_id=1, source_target_pairs={{0,8},{2,10},{8,16},{10,18},{12,4},{14,6},{16,24},{18,26},{20,12},... | collective-permute-start | bytes 2359304 | tf_op jit(solution)/shard_map/ppermute | solution.py:363
  100.4 12.0 %collective-permute-start.20 = (bf16[1,2,64,1536]{3,2,1,0:T(8,128)(2,1)S(1)}, bf16[1,2,64,1536]{3,2,1,0:T(8,128)(2,1)S(1)}, u32[]{:S(2)}, u32[]{:S(2)}) collective-permute-start(bf16[1,2,64,1536]{3,2,1,0:T(8,128)(2,1)S(1)} %pick.4), channel_id=1, source_target_pairs={{0,2},{2,0},{4,6},{6,4},{8,10},{10,8},{12,14},{14,12},{16,18},{18,... | collective-permute-start | bytes 1179656 | tf_op jit(solution)/shard_map/ppermute | solution.py:363
  101.0 15.6 %collective-permute-start.21 = (bf16[1,2,64,1536]{3,2,1,0:T(8,128)(2,1)S(1)}, bf16[1,2,64,1536]{3,2,1,0:T(8,128)(2,1)S(1)}, u32[]{:S(2)}, u32[]{:S(2)}) collective-permute-start(bf16[1,2,64,1536]{3,2,1,0:T(8,128)(2,1)S(1)} %pick.5), channel_id=1, source_target_pairs={{0,2},{2,0},{4,6},{6,4},{8,10},{10,8},{12,14},{14,12},{16,18},{18,... | collective-permute-start | bytes 1179656 | tf_op jit(solution)/shard_map/ppermute | solution.py:363
  102.5 14.1 %collective-permute-start.19 = (bf16[1,2,64,1536]{3,2,1,0:T(8,128)(2,1)S(1)}, bf16[1,2,64,1536]{3,2,1,0:T(8,128)(2,1)S(1)}, u32[]{:S(2)}, u32[]{:S(2)}) collective-permute-start(bf16[1,2,64,1536]{3,2,1,0:T(8,128)(2,1)S(1)} %collective-permute-done.18), channel_id=1, source_target_pairs={{2,6},{4,0},{10,14},{12,8},{18,22},{20,16},{26,30},{28,24},{3,7},{... | collective-permute-start | bytes 1179656 | tf_op jit(solution)/shard_map/ppermute | solution.py:363

commit v8 on v7

--- a/solution.py
+++ b/solution.py
@@ -139,6 +139,7 @@
                 refs_i = kv[starts[2 * i + part] : starts[2 * i + part + 1]]
                 if kind == "GE" and part == 0:
                     whole, low, high = [ref[:, cols] for ref in refs_i]
+                    high = high[: tokens - low.shape[0]]
                     high = jnp.where(inner, jnp.zeros_like(high), high)
                     piece = whole + join([low, high], 0)
                 else:
@@ -171,9 +172,12 @@
                     if row < keys:
                         dst[row : row + rows, cols] = w.astype(jnp.bfloat16)
                     else:
-                        rest[3][h, row - keys : row - keys + rows, cols] = w.astype(jnp.bfloat16)
+                        rest[-1][h, row - keys : row - keys + rows, cols] = w.astype(jnp.bfloat16)
 
         def mix(h, src, top):
+            rest[0][h] = jnp.broadcast_to(top, (SUBLANES, tokens))
+            if mixed_count == 0:
+                return
             v = jnp.transpose(stacked(h, 1))
             ones = jnp.ones((2 * SUBLANES, v.shape[1]), jnp.bfloat16)
             mixed = contract(join([v, ones], 0), src[...], ((1,), (0,)))
@@ -182,7 +186,6 @@
                 decay = jnp.exp2((old_refs[0][h][0:1] - top) * SCALE2)
                 total = total + old_refs[1][h] * decay
                 acc = acc + old_refs[2][h] * decay
-            rest[0][h] = jnp.broadcast_to(top, (SUBLANES, tokens))
             rest[1][h] = total
             rest[2][h] = acc
 
@@ -227,7 +230,7 @@
     specs = [smem, smem] + [vmem] * (len(operands) - 2)
     small = pltpu.VMEM((heads, SUBLANES, tokens), jnp.float32)
     large = pltpu.VMEM((heads, HEAD_DIM, tokens), jnp.float32)
-    outs = [small, small, large]
+    outs = [small, small, large] if keys > 0 else [small]
     if more > 0:
         outs.append(pltpu.VMEM((heads, more, tokens), jnp.bfloat16))
     return pl.pallas_call(
@@ -236,7 +239,7 @@
         out_specs=[vmem] * len(outs),
         out_shape=outs,
         scratch_shapes=[pltpu.VMEM((keys + more, tokens), jnp.float32)] * 2
-        + [pltpu.VMEM((keys, tokens), jnp.bfloat16)] * 2,
+        + [pltpu.VMEM((max(keys, tokens), tokens), jnp.bfloat16)] * 2,
         compiler_params=pltpu.CompilerParams(vmem_limit_bytes=VMEM_LIMIT),
         cost_estimate=pl.CostEstimate(
             flops=4 * tokens * (keys + more) * features,
@@ -248,6 +251,45 @@
 
 def columns(h):
     return pl.ds(pl.multiple_of(h * HEAD_DIM, HEAD_DIM), HEAD_DIM)
+
+
+def blend_call(value_parts, weights, top, state):
+    _, old_total, old_acc = state
+    heads = old_acc.shape[0]
+    count = len(value_parts)
+
+    def kernel(*refs):
+        v_refs = refs[:count]
+        w_ref, top_ref, old_top_ref, old_total_ref, old_acc_ref, total_ref, acc_ref = refs[count:]
+
+        def one_head(h, carry):
+            cols = columns(h)
+            v = jnp.transpose(join([ref[:, cols] for ref in v_refs], 0))
+            ones = jnp.ones((2 * SUBLANES, v.shape[1]), jnp.bfloat16)
+            mixed = contract(join([v, ones], 0), w_ref[h], ((1,), (0,)))
+            decay = jnp.exp2((old_top_ref[h][0:1] - top_ref[h][0:1]) * SCALE2)
+            total_ref[h] = old_total_ref[h] * decay + mixed[HEAD_DIM : HEAD_DIM + SUBLANES]
+            acc_ref[h] = old_acc_ref[h] * decay + mixed[:HEAD_DIM]
+            return carry
+
+        lax.fori_loop(0, heads, one_head, 0, unroll=LAST_UNROLL)
+
+    vmem = pl.BlockSpec(memory_space=pltpu.VMEM)
+    operands = [
+        pltpu.with_memory_space_constraint(value, pltpu.VMEM)
+        for value in (*value_parts, weights, top, *state)
+    ]
+    return pl.pallas_call(
+        kernel,
+        in_specs=[vmem] * len(operands),
+        out_specs=[vmem] * 2,
+        out_shape=[
+            pltpu.VMEM(old_total.shape, jnp.float32),
+            pltpu.VMEM(old_acc.shape, jnp.float32),
+        ],
+        compiler_params=pltpu.CompilerParams(vmem_limit_bytes=VMEM_LIMIT),
+        name="blend",
+    )(*operands)
 
 
 def last_call(value_rows, weights, weights_top, state):
@@ -301,12 +343,16 @@
 
 
 def pick_call(inner_value, outer_value):
+    rows = inner_value.shape[0]
+
     def kernel(inner_ref, outer_ref, out_ref):
         inner = is_inner(lax.axis_index("tm"))
 
         @pl.when(inner)
         def _():
-            out_ref[...] = inner_ref[...]
+            out_ref[:rows] = inner_ref[...]
+            if rows < out_ref.shape[0]:
+                out_ref[rows:] = jnp.zeros_like(out_ref[rows:])
 
         @pl.when(jnp.logical_not(inner))
         def _():
@@ -321,20 +367,20 @@
         kernel,
         in_specs=[vmem, vmem],
         out_specs=vmem,
-        out_shape=pltpu.VMEM(inner_value.shape, inner_value.dtype),
+        out_shape=pltpu.VMEM(outer_value.shape, outer_value.dtype),
         compiler_params=pltpu.CompilerParams(vmem_limit_bytes=VMEM_LIMIT // 2),
         name="pick",
     )(*operands)
 
 
-def split_call(value):
-    half = value.shape[1] // 2
-    part = pltpu.VMEM((1, half) + value.shape[2:], value.dtype)
+def split_call(value, cut):
+    rows, features = value.shape
+    parts = [pltpu.VMEM((size, features), value.dtype) for size in (cut, rows - cut)]
 
     def kernel(ref, low, high, sems):
         copies = [
-            pltpu.make_async_copy(ref.at[:, :half], low, sems.at[0]),
-            pltpu.make_async_copy(ref.at[:, half:], high, sems.at[1]),
+            pltpu.make_async_copy(ref.at[:cut], low, sems.at[0]),
+            pltpu.make_async_copy(ref.at[cut:], high, sems.at[1]),
         ]
         for copy in copies:
             copy.start()
@@ -345,7 +391,7 @@
         kernel,
         in_specs=[pl.BlockSpec(memory_space=pl.ANY)],
         out_specs=[pl.BlockSpec(memory_space=pltpu.VMEM)] * 2,
-        out_shape=[part] * 2,
+        out_shape=parts,
         scratch_shapes=[pltpu.SemaphoreType.DMA((2,))],
         compiler_params=pltpu.CompilerParams(vmem_limit_bytes=VMEM_LIMIT),
     )(value)
@@ -353,6 +399,7 @@
 
 def body(queries, keys, values, key_lists, density):
     _, rows_dev, width, features = queries.shape
+    tokens = rows_dev * width
     frames = lax.axis_size("tm")
     bands = lax.axis_size("space")
     route = routes(frames)
@@ -368,8 +415,8 @@
     b_k = send(keys, route["b"])
     x_k = send(keys, route["x"])
     x_v = send(values, route["x"])
-    keys0, keys1 = split_call(keys)
-    values0, values1 = split_call(values)
+    keys0, keys1 = split_call(flat(keys), tokens * 17 // 32)
+    values0, values1 = split_call(flat(values), tokens // 2)
     y_k1 = send(keys1, route["y"])
     y_v0 = send(values0, route["y"])
     y_v1 = send(values1, route["y"])
@@ -428,13 +475,11 @@
         [("B", (flat(b_k),))],
     )
     weights_top = state[0]
-    state = stage_call(
-        q,
-        [("GE", (flat(g_k), flat(e_k0), flat(r_k)), (flat(r_v0), flat(r_v1)))],
-        state,
-        lists,
-        density,
+    top, ready = stage_call(
+        q, [], state, lists, density, [("GE", (flat(g_k), flat(e_k0), flat(r_k)))]
     )
+    total, acc = blend_call((flat(r_v0), flat(r_v1)), ready, top, state)
+    state = (top, total, acc)
     result = last_call(flat(b_v), weights, weights_top, state)
     return result.reshape(1, rows_dev, width, features)
 

time: 121 us -> 107 us (0.88)
  the two profiles are of different devices: /device:TPU:0 before, /device:TPU:4 now
where the time goes in v8:
time: 107 us
  waiting for transfers between devices  56.9 us (53%)
  starting transfers between devices  35.2 us (33%)
  Pallas kernels  13.4 us (13%)
  local copies, waits for them, and re-layouts  1.16 us (1%)
    ppermute x22, waiting for transfers between devices, send(): return lax.ppermute(value, axis, pairs)  56.9 us
    ppermute x22, starting transfers between devices, send(): return lax.ppermute(value, axis, pairs)  35.2 us
    pallas_call x3, Pallas kernels, stage_call(): pl.pallas_call(kernel, in_specs=specs, out_specs=[vmem] * len(outs), out_...  9.93 us
  transfers between devices with their start and end apart: 22, of which 10 were waited for; matrix products, arithmetic and copies ran while one was open for 0% of the time, Pallas kernels for 11%

profile of v8, /device:TPU:4, one launch (start us, length us, event | category | flops | bytes accessed | tf_op | source)
XLA Modules:
  0.0 107.0 jit_solution(11047554265336880895)
XLA Ops:
  0.0 1.1 %copy-done.1 = bf16[1,4,64,1536]{3,2,1,0:T(8,128)(2,1)S(1)} copy-done((bf16[1,4,64,1536]{3,2,1,0:T(8,128)(2,1)S(1)}, bf16[1,4,64,1536]{3,2,1,0:T(8,128)(2,1)}, u32[]{:S(2)}) %copy-start.1) | copy-done | bytes 786456
  1.6 1.1 %shard_map.56 = (bf16[128,1536]{1,0:T(8,128)(2,1)S(1)}, bf16[128,1536]{1,0:T(8,128)(2,1)S(1)}) custom-call(bf16[256,1536]{1,0:T(8,128)(2,1)} %bitcast.5.ref), custom_call_target="tpu_custom_call" | custom-call | tf_op jit(solution)/shard_map/pallas_call | solution.py:390
  2.8 2.1 %collective-permute-start.7 = (bf16[128,1536]{1,0:T(8,128)(2,1)S(1)}, bf16[128,1536]{1,0:T(8,128)(2,1)S(1)}, u32[]{:S(2)}, u32[]{:S(2)}) collective-permute-start(bf16[128,1536]{1,0:T(8,128)(2,1)S(1)} %get-tuple-element.22.refs_3_), channel_id=1, source_target_pairs={{0,4},{2,6},{4,0},{6,2},{8,12},{10,14},{12,8},{14,10},{16,20},{18,... | collective-permute-start | bytes 1179656 | tf_op jit(solution)/shard_map/ppermute | solution.py:410
  4.8 3.5 %collective-permute-start.2 = (bf16[120,1536]{1,0:T(8,128)(2,1)S(1)}, bf16[120,1536]{1,0:T(8,128)(2,1)S(1)}, u32[]{:S(2)}, u32[]{:S(2)}) collective-permute-start(bf16[120,1536]{1,0:T(8,128)(2,1)S(1)} %get-tuple-element.21.refs_2_), channel_id=1, source_target_pairs={{4,12},{6,14},{8,0},{10,2},{12,20},{14,22},{16,8},{18,10},{20,28},... | collective-permute-start | bytes 1105928 | tf_op jit(solution)/shard_map/ppermute | solution.py:410
  8.4 2.0 %collective-permute-start.16 = (bf16[136,1536]{1,0:T(8,128)(2,1)S(1)}, bf16[136,1536]{1,0:T(8,128)(2,1)S(1)}, u32[]{:S(2)}, u32[]{:S(2)}) collective-permute-start(bf16[136,1536]{1,0:T(8,128)(2,1)S(1)} %get-tuple-element.20.refs_1_), channel_id=1, source_target_pairs={{0,4},{2,6},{4,0},{6,2},{8,12},{10,14},{12,8},{14,10},{16,20},{18,... | collective-permute-start | bytes 1253384 | tf_op jit(solution)/shard_map/ppermute | solution.py:410
  10.4 2.6 %collective-permute-done.5.refs_10_ = bf16[120,1536]{1,0:T(8,128)(2,1)S(1)} collective-permute-done((bf16[120,1536]{1,0:T(8,128)(2,1)S(1)}, bf16[120,1536]{1,0:T(8,128)(2,1)S(1)}, u32[]{:S(2)}, u32[]{:S(2)}) %collective-permute-start.5) | collective-permute-done | bytes 368672 | tf_op jit(solution)/shard_map/ppermute | solution.py:410
  13.1 3.5 %collective-permute-start.1 = (bf16[136,1536]{1,0:T(8,128)(2,1)S(1)}, bf16[136,1536]{1,0:T(8,128)(2,1)S(1)}, u32[]{:S(2)}, u32[]{:S(2)}) collective-permute-start(bf16[136,1536]{1,0:T(8,128)(2,1)S(1)} %get-tuple-element.20.refs_1_), channel_id=1, source_target_pairs={{4,12},{6,14},{8,0},{10,2},{12,20},{14,22},{16,8},{18,10},{20,28},... | collective-permute-start | bytes 1253384 | tf_op jit(solution)/shard_map/ppermute | solution.py:410
  16.7 1.5 %collective-permute-start.14 = (bf16[1,4,64,1536]{3,2,1,0:T(8,128)(2,1)S(1)}, bf16[1,4,64,1536]{3,2,1,0:T(8,128)(2,1)S(1)}, u32[]{:S(2)}, u32[]{:S(2)}) collective-permute-start(bf16[1,4,64,1536]{3,2,1,0:T(8,128)(2,1)S(1)} %copy-done.2), channel_id=1, source_target_pairs={{0,2},{2,0},{4,6},{6,4},{8,10},{10,8},{12,14},{14,12},{16,18},{18,... | collective-permute-start | bytes 2359304 | tf_op jit(solution)/shard_map/ppermute | solution.py:410
  18.2 3.3 %collective-permute-done.7.refs_11_.outer_ref = bf16[128,1536]{1,0:T(8,128)(2,1)S(1)} collective-permute-done((bf16[128,1536]{1,0:T(8,128)(2,1)S(1)}, bf16[128,1536]{1,0:T(8,128)(2,1)S(1)}, u32[]{:S(2)}, u32[]{:S(2)}) %collective-permute-start.7) | collective-permute-done | bytes 393248 | tf_op jit(solution)/shard_map/ppermute | solution.py:410
  21.5 1.5 %collective-permute-start.15 = (bf16[1,4,64,1536]{3,2,1,0:T(8,128)(2,1)}, bf16[1,4,64,1536]{3,2,1,0:T(8,128)(2,1)S(1)}, u32[]{:S(2)}, u32[]{:S(2)}) collective-permute-start(bf16[1,4,64,1536]{3,2,1,0:T(8,128)(2,1)} %param.7), channel_id=1, source_target_pairs={{0,2},{2,0},{4,6},{6,4},{8,10},{10,8},{12,14},{14,12},{16,18},{18,... | collective-permute-start | bytes 2359304 | tf_op jit(solution)/shard_map/ppermute | solution.py:410
  23.0 6.9 %collective-permute-done.9.refs_12_.outer_ref = bf16[128,1536]{1,0:T(8,128)(2,1)S(1)} collective-permute-done((bf16[128,1536]{1,0:T(8,128)(2,1)S(1)}, bf16[128,1536]{1,0:T(8,128)(2,1)S(1)}, u32[]{:S(2)}, u32[]{:S(2)}) %collective-permute-start.9) | collective-permute-done | bytes 393248 | tf_op jit(solution)/shard_map/ppermute | solution.py:410
  29.9 7.8 %collective-permute-done.16.refs_9_ = bf16[136,1536]{1,0:T(8,128)(2,1)S(1)} collective-permute-done((bf16[136,1536]{1,0:T(8,128)(2,1)S(1)}, bf16[136,1536]{1,0:T(8,128)(2,1)S(1)}, u32[]{:S(2)}, u32[]{:S(2)}) %collective-permute-start.16) | collective-permute-done | bytes 417824 | tf_op jit(solution)/shard_map/ppermute | solution.py:410
  37.7 1.3 %collective-permute-start.6 = (bf16[120,1536]{1,0:T(8,128)(2,1)S(1)}, bf16[120,1536]{1,0:T(8,128)(2,1)S(1)}, u32[]{:S(2)}, u32[]{:S(2)}) collective-permute-start(bf16[120,1536]{1,0:T(8,128)(2,1)S(1)} %collective-permute-done.5.refs_10_), channel_id=1, source_target_pairs={{0,8},{2,10},{8,16},{10,18},{12,4},{14,6},{16,24},{18,26},{20,12},... | collective-permute-start | bytes 1105928 | tf_op jit(solution)/shard_map/ppermute | solution.py:410
  39.1 10.0 %collective-permute-done.6.refs_5_.inner_ref = bf16[120,1536]{1,0:T(8,128)(2,1)S(1)} collective-permute-done((bf16[120,1536]{1,0:T(8,128)(2,1)S(1)}, bf16[120,1536]{1,0:T(8,128)(2,1)S(1)}, u32[]{:S(2)}, u32[]{:S(2)}) %collective-permute-start.6) | collective-permute-done | bytes 368672 | tf_op jit(solution)/shard_map/ppermute | solution.py:410
  49.1 3.5 %collective-permute-start.3 = (bf16[1,4,64,1536]{3,2,1,0:T(8,128)(2,1)}, bf16[1,4,64,1536]{3,2,1,0:T(8,128)(2,1)S(1)}, u32[]{:S(2)}, u32[]{:S(2)}) collective-permute-start(bf16[1,4,64,1536]{3,2,1,0:T(8,128)(2,1)} %param.7), channel_id=1, source_target_pairs={{4,12},{6,14},{8,0},{10,2},{12,20},{14,22},{16,8},{18,10},{20,28},... | collective-permute-start | bytes 2359304 | tf_op jit(solution)/shard_map/ppermute | solution.py:410
  52.6 1.3 %collective-permute-start.10 = (bf16[128,1536]{1,0:T(8,128)(2,1)S(1)}, bf16[128,1536]{1,0:T(8,128)(2,1)S(1)}, u32[]{:S(2)}, u32[]{:S(2)}) collective-permute-start(bf16[128,1536]{1,0:T(8,128)(2,1)S(1)} %collective-permute-done.9.refs_12_.outer_ref), channel_id=1, source_target_pairs={{0,8},{2,10},{8,16},{10,18},{12,4},{14,6},{16,24},{18,26},{20,12},... | collective-permute-start | bytes 1179656 | tf_op jit(solution)/shard_map/ppermute | solution.py:410
  53.9 1.3 %collective-permute-start.8 = (bf16[128,1536]{1,0:T(8,128)(2,1)S(1)}, bf16[128,1536]{1,0:T(8,128)(2,1)S(1)}, u32[]{:S(2)}, u32[]{:S(2)}) collective-permute-start(bf16[128,1536]{1,0:T(8,128)(2,1)S(1)} %collective-permute-done.7.refs_11_.outer_ref), channel_id=1, source_target_pairs={{0,8},{2,10},{8,16},{10,18},{12,4},{14,6},{16,24},{18,26},{20,12},... | collective-permute-start | bytes 1179656 | tf_op jit(solution)/shard_map/ppermute | solution.py:410
  55.2 1.3 %collective-permute-start.11 = (bf16[1,4,64,1536]{3,2,1,0:T(8,128)(2,1)S(1)}, bf16[1,4,64,1536]{3,2,1,0:T(8,128)(2,1)S(1)}, u32[]{:S(2)}, u32[]{:S(2)}) collective-permute-start(bf16[1,4,64,1536]{3,2,1,0:T(8,128)(2,1)S(1)} %copy-done.2), channel_id=1, source_target_pairs={{0,8},{2,10},{8,16},{10,18},{12,4},{14,6},{16,24},{18,26},{20,12},... | collective-permute-start | bytes 2359304 | tf_op jit(solution)/shard_map/ppermute | solution.py:410
  56.6 1.6 %collective-permute-start.18 = (bf16[136,1536]{1,0:T(8,128)(2,1)S(1)}, bf16[136,1536]{1,0:T(8,128)(2,1)S(1)}, u32[]{:S(2)}, u32[]{:S(2)}) collective-permute-start(bf16[136,1536]{1,0:T(8,128)(2,1)S(1)} %pick.3), channel_id=1, source_target_pairs={{0,2},{2,0},{4,6},{6,4},{8,10},{10,8},{12,14},{14,12},{16,18},{18,... | collective-permute-start | bytes 1253384 | tf_op jit(solution)/shard_map/ppermute | solution.py:410
  58.2 8.3 %collective-permute-done.10.refs_7_.inner_ref = bf16[128,1536]{1,0:T(8,128)(2,1)S(1)} collective-permute-done((bf16[128,1536]{1,0:T(8,128)(2,1)S(1)}, bf16[128,1536]{1,0:T(8,128)(2,1)S(1)}, u32[]{:S(2)}, u32[]{:S(2)}) %collective-permute-start.10) | collective-permute-done | bytes 393248 | tf_op jit(solution)/shard_map/ppermute | solution.py:410
  66.5 1.3 %collective-permute-start.17 = (bf16[1,4,64,1536]{3,2,1,0:T(8,128)(2,1)S(1)}, bf16[1,4,64,1536]{3,2,1,0:T(8,128)(2,1)S(1)}, u32[]{:S(2)}, u32[]{:S(2)}) collective-permute-start(bf16[1,4,64,1536]{3,2,1,0:T(8,128)(2,1)S(1)} %collective-permute-done.14), channel_id=1, source_target_pairs={{0,4},{6,2},{8,12},{14,10},{16,20},{22,18},{24,28},{30,26},{1,5},{... | collective-permute-start | bytes 2359304 | tf_op jit(solution)/shard_map/ppermute | solution.py:410
  67.8 7.1 %collective-permute-done.8.refs_6_.inner_ref = bf16[128,1536]{1,0:T(8,128)(2,1)S(1)} collective-permute-done((bf16[128,1536]{1,0:T(8,128)(2,1)S(1)}, bf16[128,1536]{1,0:T(8,128)(2,1)S(1)}, u32[]{:S(2)}, u32[]{:S(2)}) %collective-permute-start.8) | collective-permute-done | bytes 393248 | tf_op jit(solution)/shard_map/ppermute | solution.py:410
  74.9 1.3 %collective-permute-start = (bf16[1,4,64,1536]{3,2,1,0:T(8,128)(2,1)}, bf16[1,4,64,1536]{3,2,1,0:T(8,128)(2,1)S(1)}, u32[]{:S(2)}, u32[]{:S(2)}) collective-permute-start(bf16[1,4,64,1536]{3,2,1,0:T(8,128)(2,1)} %param.7), channel_id=1, source_target_pairs={{0,8},{2,10},{8,16},{10,18},{12,4},{14,6},{16,24},{18,26},{20,12},... | collective-permute-start | bytes 2359304 | tf_op jit(solution)/shard_map/ppermute | solution.py:410
  76.2 6.1 %collective-permute-start.19 = (bf16[136,1536]{1,0:T(8,128)(2,1)S(1)}, bf16[136,1536]{1,0:T(8,128)(2,1)S(1)}, u32[]{:S(2)}, u32[]{:S(2)}) collective-permute-start(bf16[136,1536]{1,0:T(8,128)(2,1)S(1)} %collective-permute-done.18.refs_3_), channel_id=1, source_target_pairs={{2,6},{4,0},{10,14},{12,8},{18,22},{20,16},{26,30},{28,24},{3,7},{... | collective-permute-start | bytes 1253384 | tf_op jit(solution)/shard_map/ppermute | solution.py:410
  82.5 9.3 %collective-permute-done.11 = bf16[1,4,64,1536]{3,2,1,0:T(8,128)(2,1)S(1)} collective-permute-done((bf16[1,4,64,1536]{3,2,1,0:T(8,128)(2,1)S(1)}, bf16[1,4,64,1536]{3,2,1,0:T(8,128)(2,1)S(1)}, u32[]{:S(2)}, u32[]{:S(2)}) %collective-permute-start.11) | collective-permute-done | bytes 786464 | tf_op jit(solution)/shard_map/ppermute | solution.py:410
  91.8 1.5 %collective-permute-start.20 = (bf16[128,1536]{1,0:T(8,128)(2,1)S(1)}, bf16[128,1536]{1,0:T(8,128)(2,1)S(1)}, u32[]{:S(2)}, u32[]{:S(2)}) collective-permute-start(bf16[128,1536]{1,0:T(8,128)(2,1)S(1)} %pick.4), channel_id=1, source_target_pairs={{0,2},{2,0},{4,6},{6,4},{8,10},{10,8},{12,14},{14,12},{16,18},{18,... | collective-permute-start | bytes 1179656 | tf_op jit(solution)/shard_map/ppermute | solution.py:410
  93.3 0.5 collective-permute-start.21
  93.8 4.4 %shard_map.57 = (f32[12,8,256]{2,1,0:T(8,128)S(1)}, f32[12,8,256]{2,1,0:T(8,128)S(1)}, f32[12,128,256]{2,1,0:T(8,128)S(1)}) custom-call(s32[1,2,2,6]{3,2,1,0:T(2,128)S(1)} %bitcast.25, s32[1,3]{1,0:T(1,128)S(1)} %copy-done.4, bf16[256,1536]{1,0:T(8,128)(2,1)S(1)} %bitcast.13, bf16[136,1536]{1,0:T(8,128)(2,1)S(1)} %get-tuple-element.20.refs_1_, ...), custom_call_target="tpu_custom_call" | custom-call | flops 1409286144 | bytes 8650752 | tf_op jit(solution)/shard_map/pallas_call | solution.py:236
  98.2 3.8 %shard_map.58 = (f32[12,8,256]{2,1,0:T(8,128)S(1)}, f32[12,8,256]{2,1,0:T(8,128)S(1)}, f32[12,128,256]{2,1,0:T(8,128)S(1)}, bf16[12,256,256]{2,1,0:T(8,128)(2,1)S(1)}) custom-call(s32[1,2,2,6]{3,2,1,0:T(2,128)S(1)} %bitcast.26, s32[1,3]{1,0:T(1,128)S(1)} %copy-done.4, bf16[256,1536]{1,0:T(8,128)(2,1)S(1)} %bitcast.14, ...), custom_call_target="tpu_custom_call" | custom-call | flops 1207959552 | bytes 6291456 | tf_op jit(solution)/shard_map/pallas_call | solution.py:236
  102.1 1.7 %shard_map.59 = (f32[12,8,256]{2,1,0:T(8,128)S(1)}, bf16[12,256,256]{2,1,0:T(8,128)(2,1)S(1)}) custom-call(s32[1,2,2,6]{3,2,1,0:T(2,128)S(1)} %bitcast.27, s32[1,3]{1,0:T(1,128)S(1)} %copy-done.4, bf16[256,1536]{1,0:T(8,128)(2,1)S(1)} %bitcast.15, bf16[256,1536]{1,0:T(8,128)(2,1)S(1)} %bitcast.24, bf16[136,1536]{1,0:T(8,128)(2,1)S(1)} %collective-permute-done.19.refs_2_, ...), custom_call_target="tpu_custom_call" | custom-call | flops 402653184 | bytes 3145728 | tf_op jit(solution)/shard_map/pallas_call | solution.py:236
  103.8 1.3 %collective-permute-done.21.refs_1_ = bf16[128,1536]{1,0:T(8,128)(2,1)S(1)} collective-permute-done((bf16[128,1536]{1,0:T(8,128)(2,1)S(1)}, bf16[128,1536]{1,0:T(8,128)(2,1)S(1)}, u32[]{:S(2)}, u32[]{:S(2)}) %collective-permute-start.21) | collective-permute-done | bytes 393248 | tf_op jit(solution)/shard_map/ppermute | solution.py:410
  105.6 1.4 %last.1 = bf16[256,1536]{1,0:T(8,128)(2,1)} custom-call(bf16[256,1536]{1,0:T(8,128)(2,1)S(1)} %bitcast.17, bf16[12,256,256]{2,1,0:T(8,128)(2,1)S(1)} %get-tuple-element.27.w_ref, f32[12,8,256]{2,1,0:T(8,128)S(1)} %get-tuple-element.28.refs_4_.w_top_ref, f32[12,8,256]{2,1,0:T(8,128)S(1)} %get-tuple-element.31.refs_3_.top_ref, ...), custom_call_target="tpu_custom_call" | custom-call | tf_op jit(solution)/shard_map/last/pallas_call | solution.py:326
  (32 shorter events, 1.4 us)
Async XLA Ops:
  0.0 1.1 %copy-start.1 = (bf16[1,4,64,1536]{3,2,1,0:T(8,128)(2,1)S(1)}, bf16[1,4,64,1536]{3,2,1,0:T(8,128)(2,1)}, u32[]{:S(2)}) copy-start(bf16[1,4,64,1536]{3,2,1,0:T(8,128)(2,1)} %param.6) | copy-start | bytes 2359300
  1.1 15.5 %copy-start.2 = (bf16[1,4,64,1536]{3,2,1,0:T(8,128)(2,1)S(1)}, bf16[1,4,64,1536]{3,2,1,0:T(8,128)(2,1)}, u32[]{:S(2)}) copy-start(bf16[1,4,64,1536]{3,2,1,0:T(8,128)(2,1)} %param.6) | copy-start | bytes 2359300
  1.5 11.5 %collective-permute-start.5 = (bf16[120,1536]{1,0:T(8,128)(2,1)S(1)}, bf16[120,1536]{1,0:T(8,128)(2,1)S(1)}, u32[]{:S(2)}, u32[]{:S(2)}) collective-permute-start(bf16[120,1536]{1,0:T(8,128)(2,1)S(1)} %get-tuple-element.21.refs_2_), channel_id=1, source_target_pairs={{0,4},{2,6},{4,0},{6,2},{8,12},{10,14},{12,8},{14,10},{16,20},{18,... | collective-permute-start | bytes 1105928 | tf_op jit(solution)/shard_map/ppermute | solution.py:410
  2.8 18.7 %collective-permute-start.7 = (bf16[128,1536]{1,0:T(8,128)(2,1)S(1)}, bf16[128,1536]{1,0:T(8,128)(2,1)S(1)}, u32[]{:S(2)}, u32[]{:S(2)}) collective-permute-start(bf16[128,1536]{1,0:T(8,128)(2,1)S(1)} %get-tuple-element.22.refs_3_), channel_id=1, source_target_pairs={{0,4},{2,6},{4,0},{6,2},{8,12},{10,14},{12,8},{14,10},{16,20},{18,... | collective-permute-start | bytes 1179656 | tf_op jit(solution)/shard_map/ppermute | solution.py:410
  4.8 11.8 %collective-permute-start.2 = (bf16[120,1536]{1,0:T(8,128)(2,1)S(1)}, bf16[120,1536]{1,0:T(8,128)(2,1)S(1)}, u32[]{:S(2)}, u32[]{:S(2)}) collective-permute-start(bf16[120,1536]{1,0:T(8,128)(2,1)S(1)} %get-tuple-element.21.refs_2_), channel_id=1, source_target_pairs={{4,12},{6,14},{8,0},{10,2},{12,20},{14,22},{16,8},{18,10},{20,28},... | collective-permute-start | bytes 1105928 | tf_op jit(solution)/shard_map/ppermute | solution.py:410
  8.3 21.6 %collective-permute-start.9 = (bf16[128,1536]{1,0:T(8,128)(2,1)S(1)}, bf16[128,1536]{1,0:T(8,128)(2,1)S(1)}, u32[]{:S(2)}, u32[]{:S(2)}) collective-permute-start(bf16[128,1536]{1,0:T(8,128)(2,1)S(1)} %get-tuple-element.23.refs_4_), channel_id=1, source_target_pairs={{0,4},{2,6},{4,0},{6,2},{8,12},{10,14},{12,8},{14,10},{16,20},{18,... | collective-permute-start | bytes 1179656 | tf_op jit(solution)/shard_map/ppermute | solution.py:410
  8.4 85.4 %copy-start = (bf16[1,4,64,1536]{3,2,1,0:T(8,128)(2,1)S(1)}, bf16[1,4,64,1536]{3,2,1,0:T(8,128)(2,1)}, u32[]{:S(2)}) copy-start(bf16[1,4,64,1536]{3,2,1,0:T(8,128)(2,1)} %param.5) | copy-start | bytes 2359300
  8.4 85.4 %copy-start.3 = (s32[1,2,6,2]{2,3,1,0:T(2,128)S(1)}, s32[1,2,6,2]{2,3,1,0:T(2,128)}, u32[]{:S(2)}) copy-start(s32[1,2,6,2]{2,3,1,0:T(2,128)} %param.8) | copy-start | bytes 292
  8.4 85.4 %copy-start.4 = (s32[1,3]{1,0:T(1,128)S(1)}, s32[1,3]{1,0:T(1,128)}, u32[]{:S(2)}) copy-start(s32[1,3]{1,0:T(1,128)} %density_ref.5) | copy-start | bytes 40
  8.4 29.3 %collective-permute-start.16 = (bf16[136,1536]{1,0:T(8,128)(2,1)S(1)}, bf16[136,1536]{1,0:T(8,128)(2,1)S(1)}, u32[]{:S(2)}, u32[]{:S(2)}) collective-permute-start(bf16[136,1536]{1,0:T(8,128)(2,1)S(1)} %get-tuple-element.20.refs_1_), channel_id=1, source_target_pairs={{0,4},{2,6},{4,0},{6,2},{8,12},{10,14},{12,8},{14,10},{16,20},{18,... | collective-permute-start | bytes 1253384 | tf_op jit(solution)/shard_map/ppermute | solution.py:410
  13.1 26.0 %collective-permute-start.1 = (bf16[136,1536]{1,0:T(8,128)(2,1)S(1)}, bf16[136,1536]{1,0:T(8,128)(2,1)S(1)}, u32[]{:S(2)}, u32[]{:S(2)}) collective-permute-start(bf16[136,1536]{1,0:T(8,128)(2,1)S(1)} %get-tuple-element.20.refs_1_), channel_id=1, source_target_pairs={{4,12},{6,14},{8,0},{10,2},{12,20},{14,22},{16,8},{18,10},{20,28},... | collective-permute-start | bytes 1253384 | tf_op jit(solution)/shard_map/ppermute | solution.py:410
  16.7 36.0 %collective-permute-start.14 = (bf16[1,4,64,1536]{3,2,1,0:T(8,128)(2,1)S(1)}, bf16[1,4,64,1536]{3,2,1,0:T(8,128)(2,1)S(1)}, u32[]{:S(2)}, u32[]{:S(2)}) collective-permute-start(bf16[1,4,64,1536]{3,2,1,0:T(8,128)(2,1)S(1)} %copy-done.2), channel_id=1, source_target_pairs={{0,2},{2,0},{4,6},{6,4},{8,10},{10,8},{12,14},{14,12},{16,18},{18,... | collective-permute-start | bytes 2359304 | tf_op jit(solution)/shard_map/ppermute | solution.py:410
  21.5 32.4 %collective-permute-start.15 = (bf16[1,4,64,1536]{3,2,1,0:T(8,128)(2,1)}, bf16[1,4,64,1536]{3,2,1,0:T(8,128)(2,1)S(1)}, u32[]{:S(2)}, u32[]{:S(2)}) collective-permute-start(bf16[1,4,64,1536]{3,2,1,0:T(8,128)(2,1)} %param.7), channel_id=1, source_target_pairs={{0,2},{2,0},{4,6},{6,4},{8,10},{10,8},{12,14},{14,12},{16,18},{18,... | collective-permute-start | bytes 2359304 | tf_op jit(solution)/shard_map/ppermute | solution.py:410
  29.9 25.3 %collective-permute-start.12 = (bf16[1,4,64,1536]{3,2,1,0:T(8,128)(2,1)S(1)}, bf16[1,4,64,1536]{3,2,1,0:T(8,128)(2,1)S(1)}, u32[]{:S(2)}, u32[]{:S(2)}) collective-permute-start(bf16[1,4,64,1536]{3,2,1,0:T(8,128)(2,1)S(1)} %copy-done.2), channel_id=1, source_target_pairs={{0,1},{1,0},{2,3},{3,2},{4,5},{5,4},{6,7},{7,6},{8,9},{9,8},{10,11... | collective-permute-start | bytes 2359304 | tf_op jit(solution)/shard_map/ppermute | solution.py:410
  37.7 11.4 %collective-permute-start.6 = (bf16[120,1536]{1,0:T(8,128)(2,1)S(1)}, bf16[120,1536]{1,0:T(8,128)(2,1)S(1)}, u32[]{:S(2)}, u32[]{:S(2)}) collective-permute-start(bf16[120,1536]{1,0:T(8,128)(2,1)S(1)} %collective-permute-done.5.refs_10_), channel_id=1, source_target_pairs={{0,8},{2,10},{8,16},{10,18},{12,4},{14,6},{16,24},{18,26},{20,12},... | collective-permute-start | bytes 1105928 | tf_op jit(solution)/shard_map/ppermute | solution.py:410
  39.0 17.6 %collective-permute-start.13 = (bf16[1,4,64,1536]{3,2,1,0:T(8,128)(2,1)}, bf16[1,4,64,1536]{3,2,1,0:T(8,128)(2,1)S(1)}, u32[]{:S(2)}, u32[]{:S(2)}) collective-permute-start(bf16[1,4,64,1536]{3,2,1,0:T(8,128)(2,1)} %param.7), channel_id=1, source_target_pairs={{0,1},{1,0},{2,3},{3,2},{4,5},{5,4},{6,7},{7,6},{8,9},{9,8},{10,11... | collective-permute-start | bytes 2359304 | tf_op jit(solution)/shard_map/ppermute | solution.py:410
  49.1 25.9 %collective-permute-start.3 = (bf16[1,4,64,1536]{3,2,1,0:T(8,128)(2,1)}, bf16[1,4,64,1536]{3,2,1,0:T(8,128)(2,1)S(1)}, u32[]{:S(2)}, u32[]{:S(2)}) collective-permute-start(bf16[1,4,64,1536]{3,2,1,0:T(8,128)(2,1)} %param.7), channel_id=1, source_target_pairs={{4,12},{6,14},{8,0},{10,2},{12,20},{14,22},{16,8},{18,10},{20,28},... | collective-permute-start | bytes 2359304 | tf_op jit(solution)/shard_map/ppermute | solution.py:410
  52.6 13.9 %collective-permute-start.10 = (bf16[128,1536]{1,0:T(8,128)(2,1)S(1)}, bf16[128,1536]{1,0:T(8,128)(2,1)S(1)}, u32[]{:S(2)}, u32[]{:S(2)}) collective-permute-start(bf16[128,1536]{1,0:T(8,128)(2,1)S(1)} %collective-permute-done.9.refs_12_.outer_ref), channel_id=1, source_target_pairs={{0,8},{2,10},{8,16},{10,18},{12,4},{14,6},{16,24},{18,26},{20,12},... | collective-permute-start | bytes 1179656 | tf_op jit(solution)/shard_map/ppermute | solution.py:410
  53.9 21.0 %collective-permute-start.8 = (bf16[128,1536]{1,0:T(8,128)(2,1)S(1)}, bf16[128,1536]{1,0:T(8,128)(2,1)S(1)}, u32[]{:S(2)}, u32[]{:S(2)}) collective-permute-start(bf16[128,1536]{1,0:T(8,128)(2,1)S(1)} %collective-permute-done.7.refs_11_.outer_ref), channel_id=1, source_target_pairs={{0,8},{2,10},{8,16},{10,18},{12,4},{14,6},{16,24},{18,26},{20,12},... | collective-permute-start | bytes 1179656 | tf_op jit(solution)/shard_map/ppermute | solution.py:410
  55.2 36.5 %collective-permute-start.11 = (bf16[1,4,64,1536]{3,2,1,0:T(8,128)(2,1)S(1)}, bf16[1,4,64,1536]{3,2,1,0:T(8,128)(2,1)S(1)}, u32[]{:S(2)}, u32[]{:S(2)}) collective-permute-start(bf16[1,4,64,1536]{3,2,1,0:T(8,128)(2,1)S(1)} %copy-done.2), channel_id=1, source_target_pairs={{0,8},{2,10},{8,16},{10,18},{12,4},{14,6},{16,24},{18,26},{20,12},... | collective-permute-start | bytes 2359304 | tf_op jit(solution)/shard_map/ppermute | solution.py:410
  56.6 19.6 %collective-permute-start.18 = (bf16[136,1536]{1,0:T(8,128)(2,1)S(1)}, bf16[136,1536]{1,0:T(8,128)(2,1)S(1)}, u32[]{:S(2)}, u32[]{:S(2)}) collective-permute-start(bf16[136,1536]{1,0:T(8,128)(2,1)S(1)} %pick.3), channel_id=1, source_target_pairs={{0,2},{2,0},{4,6},{6,4},{8,10},{10,8},{12,14},{14,12},{16,18},{18,... | collective-permute-start | bytes 1253384 | tf_op jit(solution)/shard_map/ppermute | solution.py:410
  66.5 35.5 %collective-permute-start.17 = (bf16[1,4,64,1536]{3,2,1,0:T(8,128)(2,1)S(1)}, bf16[1,4,64,1536]{3,2,1,0:T(8,128)(2,1)S(1)}, u32[]{:S(2)}, u32[]{:S(2)}) collective-permute-start(bf16[1,4,64,1536]{3,2,1,0:T(8,128)(2,1)S(1)} %collective-permute-done.14), channel_id=1, source_target_pairs={{0,4},{6,2},{8,12},{14,10},{16,20},{22,18},{24,28},{30,26},{1,5},{... | collective-permute-start | bytes 2359304 | tf_op jit(solution)/shard_map/ppermute | solution.py:410
  74.9 18.3 %collective-permute-start.4 = (bf16[136,1536]{1,0:T(8,128)(2,1)S(1)}, bf16[136,1536]{1,0:T(8,128)(2,1)S(1)}, u32[]{:S(2)}, u32[]{:S(2)}) collective-permute-start(bf16[136,1536]{1,0:T(8,128)(2,1)S(1)} %collective-permute-done.1.refs_1_.outer_ref), channel_id=1, source_target_pairs={{0,4},{2,6},{4,0},{6,2},{8,12},{10,14},{12,8},{14,10},{16,20},{18,... | collective-permute-start | bytes 1253384 | tf_op jit(solution)/shard_map/ppermute | solution.py:410
  74.9 30.6 %collective-permute-start = (bf16[1,4,64,1536]{3,2,1,0:T(8,128)(2,1)}, bf16[1,4,64,1536]{3,2,1,0:T(8,128)(2,1)S(1)}, u32[]{:S(2)}, u32[]{:S(2)}) collective-permute-start(bf16[1,4,64,1536]{3,2,1,0:T(8,128)(2,1)} %param.7), channel_id=1, source_target_pairs={{0,8},{2,10},{8,16},{10,18},{12,4},{14,6},{16,24},{18,26},{20,12},... | collective-permute-start | bytes 2359304 | tf_op jit(solution)/shard_map/ppermute | solution.py:410
  76.2 25.8 %collective-permute-start.19 = (bf16[136,1536]{1,0:T(8,128)(2,1)S(1)}, bf16[136,1536]{1,0:T(8,128)(2,1)S(1)}, u32[]{:S(2)}, u32[]{:S(2)}) collective-permute-start(bf16[136,1536]{1,0:T(8,128)(2,1)S(1)} %collective-permute-done.18.refs_3_), channel_id=1, source_target_pairs={{2,6},{4,0},{10,14},{12,8},{18,22},{20,16},{26,30},{28,24},{3,7},{... | collective-permute-start | bytes 1253384 | tf_op jit(solution)/shard_map/ppermute | solution.py:410
  91.8 12.0 %collective-permute-start.20 = (bf16[128,1536]{1,0:T(8,128)(2,1)S(1)}, bf16[128,1536]{1,0:T(8,128)(2,1)S(1)}, u32[]{:S(2)}, u32[]{:S(2)}) collective-permute-start(bf16[128,1536]{1,0:T(8,128)(2,1)S(1)} %pick.4), channel_id=1, source_target_pairs={{0,2},{2,0},{4,6},{6,4},{8,10},{10,8},{12,14},{14,12},{16,18},{18,... | collective-permute-start | bytes 1179656 | tf_op jit(solution)/shard_map/ppermute | solution.py:410
  93.3 11.8 %collective-permute-start.21 = (bf16[128,1536]{1,0:T(8,128)(2,1)S(1)}, bf16[128,1536]{1,0:T(8,128)(2,1)S(1)}, u32[]{:S(2)}, u32[]{:S(2)}) collective-permute-start(bf16[128,1536]{1,0:T(8,128)(2,1)S(1)} %pick.5), channel_id=1, source_target_pairs={{0,2},{2,0},{4,6},{6,4},{8,10},{10,8},{12,14},{14,12},{16,18},{18,... | collective-permute-start | bytes 1179656 | tf_op jit(solution)/shard_map/ppermute | solution.py:410
